TPU v7x, 32 devices: a whole 2x2x4 slice. The times are simulated.
32 devices in a mesh: dp: 4 (over y, x), fsdp: 8 (over z, core).
Axes of the slice: x: 2, y: 2, z: 4, core: 2. Of those that a mesh axis runs over, the one named last changes fastest.
Arguments:
- tokens: bfloat16 [32, 512, 768], P(('dp', 'fsdp')), may hold values from -6 to 6
- lengths: int32 [32], P(('dp', 'fsdp')), may hold values from 30 to 512, as said below
- cotangent: bfloat16 [32, 512, 768], P(('dp', 'fsdp')), may hold values from -6 to 6
- query_weight: bfloat16 [768, 768], P('fsdp'), may hold values from -0.21875 to 0.21875
- query_bias: bfloat16 [768], P('fsdp'), may hold values from -3 to 3
- key_weight: bfloat16 [768, 768], P('fsdp'), may hold values from -0.21875 to 0.21875
- value_weight: bfloat16 [768, 768], P('fsdp'), may hold values from -0.21875 to 0.21875
- value_bias: bfloat16 [768], P('fsdp'), may hold values from -3 to 3
- output_weight: bfloat16 [768, 768], P('fsdp'), may hold values from -3.5 to 3.5
- output_bias: bfloat16 [768], P('fsdp'), may hold values from -3 to 3
- first_gain: bfloat16 [768], P('fsdp'), may hold values from 0.25 to 1.75
- first_shift: bfloat16 [768], P('fsdp'), may hold values from -3 to 3
- inner_weight: bfloat16 [768, 3072], P('fsdp'), may hold values from -0.21875 to 0.21875
- inner_bias: bfloat16 [3072], P('fsdp'), may hold values from -3 to 3
- outer_weight: bfloat16 [3072, 768], P('fsdp'), may hold values from -0.109375 to 0.109375
- outer_bias: bfloat16 [768], P('fsdp'), may hold values from -3 to 3
- second_gain: bfloat16 [768], P('fsdp'), may hold values from 0.25 to 1.75
- second_shift: bfloat16 [768], P('fsdp'), may hold values from -3 to 3
Outputs:
- block_output: bfloat16 [32, 512, 768], P(('dp', 'fsdp'))
- input_grad: float32 [32, 512, 768], P(('dp', 'fsdp'))
- query_weight_grad: float32 [768, 768], P('fsdp')
- query_bias_grad: float32 [768], P('fsdp')
- key_weight_grad: float32 [768, 768], P('fsdp')
- value_weight_grad: float32 [768, 768], P('fsdp')
- value_bias_grad: float32 [768], P('fsdp')
- output_weight_grad: float32 [768, 768], P('fsdp')
- output_bias_grad: float32 [768], P('fsdp')
- first_gain_grad: float32 [768], P('fsdp')
- first_shift_grad: float32 [768], P('fsdp')
- inner_weight_grad: float32 [768, 3072], P('fsdp')
- inner_bias_grad: float32 [3072], P('fsdp')
- outer_weight_grad: float32 [3072, 768], P('fsdp')
- outer_bias_grad: float32 [768], P('fsdp')
- second_gain_grad: float32 [768], P('fsdp')
- second_shift_grad: float32 [768], P('fsdp')
Inputs may be any that keep to these rules, and one draw needn't show every extreme that they name: Document i holds its true tokens in slots 0 to lengths[i] - 1, the rest is padding; in every draw some document has exactly 512 and another exactly 30.
All inputs are finite; a program needn't handle non-finite values.
Results may differ from a plain program's by a relative error of at most 0.015.
Values may be sent and summed in bfloat16 or wider, within the bound.
No kernel may reach another device: no remote copies, remote signals or barrier semaphores. Data moves between devices by JAX's collectives and lax.ppermute only.
A program may use at most 192 MiB of HBM per device.

v0:
```python
import math

import jax
import jax.numpy as jnp
from jax import lax
from jax.sharding import PartitionSpec as P

HD = 64


epsilon = 1e-12
masked_score = -1e30
root_half = math.sqrt(0.5)
inv_root_two_pi = 1.0 / math.sqrt(2.0 * math.pi)


def normalize(values):
    center = values - jnp.mean(values, axis=-1, keepdims=True)
    scaled = lax.rsqrt(jnp.mean(center * center, axis=-1, keepdims=True) + epsilon)
    return (center * scaled, scaled)


def norm_back(grad_in, normed, scaled):
    first_mean = jnp.mean(grad_in, axis=-1, keepdims=True)
    second_mean = jnp.mean(grad_in * normed, axis=-1, keepdims=True)
    return scaled * (grad_in - first_mean - normed * second_mean)


def gelu_parts(inner):
    cumulative = 0.5 * (1.0 + lax.erf(inner * root_half))
    density = jnp.exp(-0.5 * inner * inner) * inv_root_two_pi
    return (inner * cumulative, cumulative + inner * density)


def score_block(queries, keysets, length):
    seq_len = queries.shape[0]
    scores = jnp.einsum(
        "qhd,khd->hqk", queries, keysets, preferred_element_type=jnp.float32
    ) * queries.shape[2] ** (-0.5)
    allowed = jnp.arange(seq_len, dtype=jnp.int32) < length
    return jnp.where(allowed[None, None, :], scores, masked_score)


def attend_forward(pieces):
    queries, keysets, values, length = pieces
    scores = score_block(queries, keysets, length)
    highest = jnp.max(scores, axis=-1, keepdims=True)
    logsum = highest + jnp.log(jnp.sum(jnp.exp(scores - highest), axis=-1, keepdims=True))
    probs = jnp.exp(scores - logsum).astype(jnp.bfloat16)
    attended = jnp.einsum("hqk,khd->qhd", probs, values, preferred_element_type=jnp.float32)
    return (attended.astype(jnp.bfloat16), logsum)


def attend_backward(pieces):
    queries, keysets, values, length, logsum, attended_grad = pieces
    scale = queries.shape[2] ** (-0.5)
    scores = score_block(queries, keysets, length)
    probs_full = jnp.exp(scores - logsum)
    probs = probs_full.astype(jnp.bfloat16)
    values_grad = jnp.einsum(
        "hqk,qhd->khd", probs, attended_grad, preferred_element_type=jnp.float32
    )
    prob_grad = jnp.einsum(
        "qhd,khd->hqk", attended_grad, values, preferred_element_type=jnp.float32
    )
    row_term = jnp.sum(prob_grad * probs_full, axis=-1, keepdims=True)
    score_grad = (probs_full * (prob_grad - row_term)).astype(jnp.bfloat16)
    queries_grad = (
        jnp.einsum("hqk,khd->qhd", score_grad, keysets, preferred_element_type=jnp.float32) * scale
    )
    keys_grad = (
        jnp.einsum("hqk,qhd->khd", score_grad, queries, preferred_element_type=jnp.float32) * scale
    )
    return (
        queries_grad.astype(jnp.bfloat16),
        keys_grad.astype(jnp.bfloat16),
        values_grad.astype(jnp.bfloat16),
    )


def column_sum(values):
    return jnp.sum(values.astype(jnp.float32), axis=0)


def weight_grad(left, right):
    return jnp.einsum("tr,tc->rc", left, right, preferred_element_type=jnp.float32)


def back_product(grad_rows, weights):
    return jnp.einsum("tc,rc->tr", grad_rows, weights, preferred_element_type=jnp.float32)


def on_device(
    tokens,
    lengths,
    cotangent,
    query_weight,
    query_bias,
    key_weight,
    value_weight,
    value_bias,
    output_weight,
    output_bias,
    first_gain,
    first_shift,
    inner_weight,
    inner_bias,
    outer_weight,
    outer_bias,
    second_gain,
    second_shift,
):
    gathered = (
        lax.all_gather(query_weight, "fsdp", axis=0, tiled=True),
        lax.all_gather(query_bias, "fsdp", axis=0, tiled=True),
        lax.all_gather(key_weight, "fsdp", axis=0, tiled=True),
        lax.all_gather(value_weight, "fsdp", axis=0, tiled=True),
        lax.all_gather(value_bias, "fsdp", axis=0, tiled=True),
        lax.all_gather(output_weight, "fsdp", axis=0, tiled=True),
        lax.all_gather(output_bias, "fsdp", axis=0, tiled=True),
        lax.all_gather(first_gain, "fsdp", axis=0, tiled=True),
        lax.all_gather(first_shift, "fsdp", axis=0, tiled=True),
        lax.all_gather(inner_weight, "fsdp", axis=0, tiled=True),
        lax.all_gather(inner_bias, "fsdp", axis=0, tiled=True),
        lax.all_gather(outer_weight, "fsdp", axis=0, tiled=True),
        lax.all_gather(outer_bias, "fsdp", axis=0, tiled=True),
        lax.all_gather(second_gain, "fsdp", axis=0, tiled=True),
        lax.all_gather(second_shift, "fsdp", axis=0, tiled=True),
    )
    (
        full_query,
        full_qbias,
        full_key,
        full_value,
        full_vbias,
        full_output,
        full_obias,
        full_gain_one,
        full_shift_one,
        full_inner,
        full_ibias,
        full_outer,
        full_ubias,
        full_gain_two,
        full_shift_two,
    ) = gathered
    doc_count, seq_len, width = tokens.shape
    row_count = doc_count * seq_len
    heads = width // HD
    flat_in = tokens.reshape(row_count, width)
    queries = (
        jnp.dot(flat_in, full_query, preferred_element_type=jnp.float32)
        + full_qbias.astype(jnp.float32)
    ).astype(jnp.bfloat16)
    keysets = jnp.dot(flat_in, full_key, preferred_element_type=jnp.float32).astype(jnp.bfloat16)
    values = (
        jnp.dot(flat_in, full_value, preferred_element_type=jnp.float32)
        + full_vbias.astype(jnp.float32)
    ).astype(jnp.bfloat16)
    shaped = (doc_count, seq_len, heads, HD)
    query_docs = queries.reshape(shaped)
    key_docs = keysets.reshape(shaped)
    value_docs = values.reshape(shaped)
    attended, logsum = lax.map(attend_forward, (query_docs, key_docs, value_docs, lengths))
    attended = attended.reshape(row_count, width)
    first_sum = (
        flat_in.astype(jnp.float32)
        + jnp.dot(attended, full_output, preferred_element_type=jnp.float32)
        + full_obias.astype(jnp.float32)
    )
    normed_one, rstd_one = normalize(first_sum)
    hidden = normed_one * full_gain_one.astype(jnp.float32) + full_shift_one.astype(jnp.float32)
    hidden_low = hidden.astype(jnp.bfloat16)
    inner = jnp.dot(hidden_low, full_inner, preferred_element_type=jnp.float32) + full_ibias.astype(
        jnp.float32
    )
    activated_full, slope = gelu_parts(inner)
    activated = activated_full.astype(jnp.bfloat16)
    second_sum = (
        hidden
        + jnp.dot(activated, full_outer, preferred_element_type=jnp.float32)
        + full_ubias.astype(jnp.float32)
    )
    normed_two, rstd_two = normalize(second_sum)
    valid = (
        (jnp.arange(seq_len, dtype=jnp.int32)[None, :] < lengths[:, None])
        .astype(jnp.float32)
        .reshape(row_count, 1)
    )
    result = valid * (
        normed_two * full_gain_two.astype(jnp.float32) + full_shift_two.astype(jnp.float32)
    )
    block_output = result.astype(jnp.bfloat16).reshape(doc_count, seq_len, width)
    again = (
        lax.all_gather(query_weight, "fsdp", axis=0, tiled=True),
        lax.all_gather(query_bias, "fsdp", axis=0, tiled=True),
        lax.all_gather(key_weight, "fsdp", axis=0, tiled=True),
        lax.all_gather(value_weight, "fsdp", axis=0, tiled=True),
        lax.all_gather(value_bias, "fsdp", axis=0, tiled=True),
        lax.all_gather(output_weight, "fsdp", axis=0, tiled=True),
        lax.all_gather(output_bias, "fsdp", axis=0, tiled=True),
        lax.all_gather(first_gain, "fsdp", axis=0, tiled=True),
        lax.all_gather(first_shift, "fsdp", axis=0, tiled=True),
        lax.all_gather(inner_weight, "fsdp", axis=0, tiled=True),
        lax.all_gather(inner_bias, "fsdp", axis=0, tiled=True),
        lax.all_gather(outer_weight, "fsdp", axis=0, tiled=True),
        lax.all_gather(outer_bias, "fsdp", axis=0, tiled=True),
        lax.all_gather(second_gain, "fsdp", axis=0, tiled=True),
        lax.all_gather(second_shift, "fsdp", axis=0, tiled=True),
    )
    back_query = again[0]
    back_key = again[2]
    back_value = again[3]
    back_output = again[5]
    back_gain_one = again[7]
    back_inner = again[9]
    back_outer = again[11]
    back_gain_two = again[13]
    out_grad = cotangent.reshape(row_count, width).astype(jnp.float32) * valid
    second_shift_grad = jnp.sum(out_grad, axis=0)
    second_gain_grad = jnp.sum(out_grad * normed_two, axis=0)
    second_sum_grad = norm_back(out_grad * back_gain_two.astype(jnp.float32), normed_two, rstd_two)
    outer_grad_low = second_sum_grad.astype(jnp.bfloat16)
    outer_bias_grad = column_sum(outer_grad_low)
    outer_weight_grad = weight_grad(activated, outer_grad_low)
    inner_grad_low = (back_product(outer_grad_low, back_outer) * slope).astype(jnp.bfloat16)
    inner_bias_grad = column_sum(inner_grad_low)
    inner_weight_grad = weight_grad(hidden_low, inner_grad_low)
    hidden_grad = back_product(inner_grad_low, back_inner) + second_sum_grad
    first_shift_grad = jnp.sum(hidden_grad, axis=0)
    first_gain_grad = jnp.sum(hidden_grad * normed_one, axis=0)
    first_sum_grad = norm_back(
        hidden_grad * back_gain_one.astype(jnp.float32), normed_one, rstd_one
    )
    branch_grad_low = first_sum_grad.astype(jnp.bfloat16)
    output_bias_grad = column_sum(branch_grad_low)
    output_weight_grad = weight_grad(attended, branch_grad_low)
    attended_grad_low = back_product(branch_grad_low, back_output).astype(jnp.bfloat16)
    queries_grad, keys_grad, values_grad = lax.map(
        attend_backward,
        (query_docs, key_docs, value_docs, lengths, logsum, attended_grad_low.reshape(shaped)),
    )
    queries_grad = queries_grad.reshape(row_count, width)
    keys_grad = keys_grad.reshape(row_count, width)
    values_grad = values_grad.reshape(row_count, width)
    query_bias_grad = column_sum(queries_grad)
    value_bias_grad = column_sum(values_grad)
    query_weight_grad = weight_grad(flat_in, queries_grad)
    key_weight_grad = weight_grad(flat_in, keys_grad)
    value_weight_grad = weight_grad(flat_in, values_grad)
    input_grad = (
        first_sum_grad
        + back_product(queries_grad, back_query)
        + back_product(keys_grad, back_key)
        + back_product(values_grad, back_value)
    )
    local_grads = (
        query_weight_grad,
        query_bias_grad,
        key_weight_grad,
        value_weight_grad,
        value_bias_grad,
        output_weight_grad,
        output_bias_grad,
        first_gain_grad,
        first_shift_grad,
        inner_weight_grad,
        inner_bias_grad,
        outer_weight_grad,
        outer_bias_grad,
        second_gain_grad,
        second_shift_grad,
    )
    owned = (
        lax.psum_scatter(local_grads[0], "fsdp", scatter_dimension=0, tiled=True),
        lax.psum_scatter(local_grads[1], "fsdp", scatter_dimension=0, tiled=True),
        lax.psum_scatter(local_grads[2], "fsdp", scatter_dimension=0, tiled=True),
        lax.psum_scatter(local_grads[3], "fsdp", scatter_dimension=0, tiled=True),
        lax.psum_scatter(local_grads[4], "fsdp", scatter_dimension=0, tiled=True),
        lax.psum_scatter(local_grads[5], "fsdp", scatter_dimension=0, tiled=True),
        lax.psum_scatter(local_grads[6], "fsdp", scatter_dimension=0, tiled=True),
        lax.psum_scatter(local_grads[7], "fsdp", scatter_dimension=0, tiled=True),
        lax.psum_scatter(local_grads[8], "fsdp", scatter_dimension=0, tiled=True),
        lax.psum_scatter(local_grads[9], "fsdp", scatter_dimension=0, tiled=True),
        lax.psum_scatter(local_grads[10], "fsdp", scatter_dimension=0, tiled=True),
        lax.psum_scatter(local_grads[11], "fsdp", scatter_dimension=0, tiled=True),
        lax.psum_scatter(local_grads[12], "fsdp", scatter_dimension=0, tiled=True),
        lax.psum_scatter(local_grads[13], "fsdp", scatter_dimension=0, tiled=True),
        lax.psum_scatter(local_grads[14], "fsdp", scatter_dimension=0, tiled=True),
    )
    summed = (
        lax.psum(owned[0].astype(jnp.bfloat16), "dp").astype(jnp.float32),
        lax.psum(owned[1].astype(jnp.bfloat16), "dp").astype(jnp.float32),
        lax.psum(owned[2].astype(jnp.bfloat16), "dp").astype(jnp.float32),
        lax.psum(owned[3].astype(jnp.bfloat16), "dp").astype(jnp.float32),
        lax.psum(owned[4].astype(jnp.bfloat16), "dp").astype(jnp.float32),
        lax.psum(owned[5].astype(jnp.bfloat16), "dp").astype(jnp.float32),
        lax.psum(owned[6].astype(jnp.bfloat16), "dp").astype(jnp.float32),
        lax.psum(owned[7].astype(jnp.bfloat16), "dp").astype(jnp.float32),
        lax.psum(owned[8].astype(jnp.bfloat16), "dp").astype(jnp.float32),
        lax.psum(owned[9].astype(jnp.bfloat16), "dp").astype(jnp.float32),
        lax.psum(owned[10].astype(jnp.bfloat16), "dp").astype(jnp.float32),
        lax.psum(owned[11].astype(jnp.bfloat16), "dp").astype(jnp.float32),
        lax.psum(owned[12].astype(jnp.bfloat16), "dp").astype(jnp.float32),
        lax.psum(owned[13].astype(jnp.bfloat16), "dp").astype(jnp.float32),
        lax.psum(owned[14].astype(jnp.bfloat16), "dp").astype(jnp.float32),
    )
    return (
        block_output,
        input_grad.reshape(doc_count, seq_len, width),
        summed[0],
        summed[1],
        summed[2],
        summed[3],
        summed[4],
        summed[5],
        summed[6],
        summed[7],
        summed[8],
        summed[9],
        summed[10],
        summed[11],
        summed[12],
        summed[13],
        summed[14],
    )


def solution(mesh):
    in_specs = (
        P(("dp", "fsdp"), None, None),
        P(("dp", "fsdp")),
        P(("dp", "fsdp"), None, None),
        P("fsdp", None),
        P("fsdp"),
        P("fsdp", None),
        P("fsdp", None),
        P("fsdp"),
        P("fsdp", None),
        P("fsdp"),
        P("fsdp"),
        P("fsdp"),
        P("fsdp", None),
        P("fsdp"),
        P("fsdp", None),
        P("fsdp"),
        P("fsdp"),
        P("fsdp"),
    )
    out_specs = (
        P(("dp", "fsdp"), None, None),
        P(("dp", "fsdp"), None, None),
        P("fsdp", None),
        P("fsdp"),
        P("fsdp", None),
        P("fsdp", None),
        P("fsdp"),
        P("fsdp", None),
        P("fsdp"),
        P("fsdp"),
        P("fsdp"),
        P("fsdp", None),
        P("fsdp"),
        P("fsdp", None),
        P("fsdp"),
        P("fsdp"),
        P("fsdp"),
    )
    return jax.shard_map(
        on_device, mesh=mesh, in_specs=in_specs, out_specs=out_specs, check_vma=False
    )
```

profile of v0, /device:TPU:0, one launch (start us, length us, event | category | flops | bytes accessed | tf_op | source)
XLA Modules:
  0.0 681.5 jit_solution(11375898888319952286)
XLA Ops:
  14.5 30.3 %all-reduce.18 = (bf16[768]{0:T(1024)(128)(2,1)S(1)}, bf16[768]{0:T(1024)(128)(2,1)S(1)}, bf16[768]{0:T(1024)(128)(2,1)S(1)}, bf16[768]{0:T(1024)(128)(2,1)S(1)}...) all-reduce(bf16[768]{0:T(1024)(128)(2,1)S(1)} %dynamic-update-slice, ...), channel_id=1, replica_groups=mesh['dp'=4,'fsdp'=8] {'fsdp'}, use_global_device_ids=true, to_apply=%add | all-reduce | flops 6144 | bytes 24576
  45.5 12.9 %all-gather = bf16[8,1,384]{2,1,0:T(2,128)(2,1)S(1)} all-gather(bf16[1,1,384]{2,1,0:T(2,128)(2,1)S(1)} %reshape.181), channel_id=1, replica_groups=mesh['dp'=4,'fsdp'=8] {'fsdp'}, dimensions={0}, use_global_device_ids=true | all-gather | bytes 6912 | tf_op jit(solution)/shard_map/all_gather | solution.py:124
  63.5 20.0 %all-gather.8.cloned.1.call-done = bf16[768,768]{1,0:T(8,128)(2,1)} async-done(((bf16[96,768]{1,0:T(8,128)(2,1)}), bf16[768,768]{1,0:T(8,128)(2,1)}) %all-gather.8.cloned.1.call-update) | async-done | bytes 1179664 | tf_op jit(solution)/shard_map/all_gather | solution.py:117
  95.4 9.9 %fusion.1 = bf16[12,512,512]{1,2,0:T(8,128)(2,1)} fusion(f32[12,512,512]{1,2,0:T(8,128)} %copy-done, f32[12,512]{1,0:T(8,128)S(1)} %log_add_fusion, pred[512]{0:T(512)(128)(4,1)S(1)} %iota_compare_fusion), kind=kLoop, calls=%fused_computation.7 | loop fusion | flops 12582912 | bytes 18899456 | tf_op jit(solution)/shard_map/while/body/eval_jaxpr/convert_element_type | solution.py:49
  105.3 4.1 convolution_convert_fusion.3
  113.4 47.0 %all-gather.16.cloned.1.call-done = bf16[768,3072]{1,0:T(8,128)(2,1)} async-done(((bf16[96,3072]{1,0:T(8,128)(2,1)}), bf16[768,3072]{1,0:T(8,128)(2,1)}) %all-gather.16.cloned.1.call-update) | async-done | bytes 4718608 | tf_op jit(solution)/shard_map/all_gather | solution.py:123
  160.4 8.5 %multiply_convert_fusion.1 = (bf16[512,3072]{1,0:T(8,128)(2,1)}, f32[512,3072]{1,0:T(8,128)}) fusion(f32[3072]{0:T(1024)S(1)} %bitcast.111, bf16[768,3072]{1,0:T(8,128)(2,1)} %all-gather.16.cloned.1.call-done, f32[512,768]{1,0:T(8,128)} %copy-done.15, f32[768]{0:T(1024)S(1)} %convert_element_type.234, f32[768]{0:T(1024)S(1)} %convert_element_type.233, ...), kind=kOutput, calls=%fused_computation.15 | convolution fusion | flops 2427322368 | bytes 15751168 | tf_op jit(solution)/shard_map/dot_general | solution.py:174
  168.9 43.5 %all-gather.18.cloned.1.call-done = bf16[3072,768]{1,0:T(8,128)(2,1)} async-done(((bf16[384,768]{1,0:T(8,128)(2,1)}), bf16[3072,768]{1,0:T(8,128)(2,1)}) %all-gather.18.cloned.1.call-update) | async-done | bytes 4718608 | tf_op jit(solution)/shard_map/all_gather | solution.py:125
  212.5 6.2 fusion.40
  222.3 5.2 convert_reduce_fusion
  236.1 5.2 convert_reduce_fusion.3
  247.4 7.6 %multiply_reduce_fusion = (f32[12,512]{1,0:T(8,128)S(1)}, f32[12,512,512]{1,2,0:T(8,128)S(1)}) fusion(f32[12,512,512]{1,2,0:T(8,128)} %copy-done, f32[12,512]{1,0:T(8,128)S(1)} %log_add_fusion, pred[512]{0:T(512)(128)(4,1)S(1)} %iota_compare_fusion, bf16[512,12,64]{0,2,1:T(8,128)(2,1)} %bitcast.100, bf16[512,12,64]{0,2,1:T(8,128)(2,1)S(1)} %bitcast.96), kind=kOutput, calls=%fused_computation.1 | convolution fusion | flops 418375680 | bytes 26788352 | tf_op jit(solution)/shard_map/while/body/eval_jaxpr/qhd,khd->hqk/dot_general | solution.py:63
  255.0 7.2 %multiply_convert_fusion = bf16[12,512,512]{1,2,0:T(8,128)(2,1)S(1)} fusion(f32[12,512,512]{1,2,0:T(8,128)S(1)} %get-tuple-element.176, f32[12,512,512]{1,2,0:T(8,128)} %copy-done, f32[12,512]{1,0:T(8,128)S(1)} %get-tuple-element.175, f32[12,512]{1,0:T(8,128)S(1)} %log_add_fusion, pred[512]{0:T(512)(128)(4,1)S(1)} %iota_compare_fusion), kind=kLoop, calls=%fused_computation | loop fusion | flops 18874368 | bytes 31506944 | tf_op jit(solution)/shard_map/while/body/eval_jaxpr/convert_element_type | solution.py:67
  275.6 4.8 multiply_convert_fusion.2
  288.0 7.2 %fusion.33 = f32[768,3072]{1,0:T(8,128)} fusion(bf16[512,3072]{1,0:T(8,128)(2,1)} %copy-done.41, f32[512,768]{1,0:T(8,128)S(1)} %copy-done.18, f32[768]{0:T(1024)S(1)} %convert_element_type.234, f32[768]{0:T(1024)S(1)} %convert_element_type.233, f32[512]{0:T(512)S(1)} %add_rsqrt_fusion.1, f32[512]{0:T(512)S(1)} %broadcast_multiply_fusion.5), kind=kOutput, calls=%fused_computation.91 | convolution fusion | flops 2417885184 | bytes 14166016 | tf_op jit(solution)/shard_map/tr,tc->rc/dot_general | solution.py:86
  296.6 8.2 %fusion.29 = f32[3072,768]{1,0:T(8,128)} fusion(bf16[512,3072]{1,0:T(8,128)(2,1)} %get-tuple-element.170, f32[512,768]{1,0:T(8,128)S(1)} %copy-done.14), kind=kOutput, calls=%fused_computation.87 | convolution fusion | flops 2416312320 | bytes 14155776 | tf_op jit(solution)/shard_map/tr,tc->rc/dot_general | solution.py:86
  306.7 13.6 %reduce-scatter.19.cloned.1.call-done = f32[96,768]{1,0:T(8,128)} async-done(((f32[768,768]{1,0:T(8,128)}), f32[96,768]{1,0:T(8,128)}) %reduce-scatter.19.cloned.1.call-update) | async-done | bytes 294928
  322.1 36.1 %reduce-scatter.13.cloned.1.call-done = f32[96,768]{1,0:T(8,128)} async-done(((f32[768,768]{1,0:T(8,128)}), f32[96,768]{1,0:T(8,128)}) %reduce-scatter.13.cloned.1.call-update) | async-done | bytes 294928 | tf_op jit(solution)/shard_map/reduce_scatter | solution.py:280
  359.8 36.0 %reduce-scatter.21.cloned.1.call-done = f32[96,768]{1,0:T(8,128)} async-done(((f32[768,768]{1,0:T(8,128)}), f32[96,768]{1,0:T(8,128)}) %reduce-scatter.21.cloned.1.call-update) | async-done | bytes 294928
  397.6 99.3 %reduce-scatter.15.cloned.1.call-done = f32[96,3072]{1,0:T(8,128)} async-done(((f32[768,3072]{1,0:T(8,128)}), f32[96,3072]{1,0:T(8,128)}) %reduce-scatter.15.cloned.1.call-update) | async-done | bytes 1179664 | tf_op jit(solution)/shard_map/reduce_scatter | solution.py:284
  499.0 97.9 %reduce-scatter.17.cloned.1.call-done = f32[384,768]{1,0:T(8,128)} async-done(((f32[3072,768]{1,0:T(8,128)}), f32[384,768]{1,0:T(8,128)}) %reduce-scatter.17.cloned.1.call-update) | async-done | bytes 1179664 | tf_op jit(solution)/shard_map/reduce_scatter | solution.py:286
  600.6 26.4 %all-reduce.17 = (bf16[768]{0:T(1024)(128)(2,1)S(1)}, bf16[768]{0:T(1024)(128)(2,1)S(1)}, bf16[768]{0:T(1024)(128)(2,1)S(1)}, bf16[768]{0:T(1024)(128)(2,1)S(1)}...) all-reduce(f32[768]{0:T(1024)S(1)} %reduce_sum.188, ...), channel_id=3, replica_groups=mesh['dp'=4,'fsdp'=8] {'fsdp'}, use_global_device_ids=true, to_apply=%region_14.15.clone | all-reduce | flops 9216 | bytes 55296
  627.7 10.0 %all-reduce.19 = (bf16[96]{0:T(256)(128)(2,1)S(1)}, bf16[96]{0:T(256)(128)(2,1)S(1)}, bf16[96]{0:T(256)(128)(2,1)S(1)}, bf16[96]{0:T(256)(128)(2,1)S(1)}, bf16[9...) all-reduce(bf16[96]{0:T(256)(128)(2,1)S(1)} %dynamic-slice.44, ...), channel_id=1, replica_groups=mesh['dp'=4,'fsdp'=8] {'dp'}, use_global_device_ids=true, to_apply=%region_15.16 | all-reduce | flops 1152 | bytes 4608 | tf_op jit(solution)/shard_map/psum | solution.py:293
  648.2 20.0 %all-reduce.23.cloned.1.call-done = (bf16[96,768]{0,1:T(8,128)(2,1)}, bf16[96,768]{0,1:T(8,128)(2,1)}, bf16[96,768]{0,1:T(8,128)(2,1)}, bf16[96,768]{1,0:T(8,128...) async-done(((bf16[96,768]{0,1:T(8,128)(2,1)}, bf16[96,768]{0,1:T(8,128)(2,1)}, bf16[96,768]{0,1:T(8,128)(2,1)}, bf16[96,768]{1,0:T(8,128)(2,1)}, ...) | async-done | bytes 1769488 | tf_op jit(solution)/shard_map/psum | solution.py:292
  (218 shorter events, 97.2 us)
Async XLA Ops:
  7.2 6.3 copy-start.37
  7.3 6.5 copy-start.38
  7.3 6.7 copy-start.39
  7.3 7.0 %copy-start.40 = (bf16[96]{0:T(256)(128)(2,1)S(1)}, bf16[96]{0:T(256)(128)(2,1)}, u32[]{:S(2)}) copy-start(bf16[96]{0:T(256)(128)(2,1)} %param.35) | copy-start | bytes 580
  7.3 38.2 %copy-start.29 = (bf16[384]{0:T(512)(128)(2,1)S(1)}, bf16[384]{0:T(512)(128)(2,1)}, u32[]{:S(2)}) copy-start(bf16[384]{0:T(512)(128)(2,1)} %param.31) | copy-start | bytes 2308
  7.3 51.2 %copy-start.4 = (bf16[1,512,768]{2,1,0:T(8,128)(2,1)S(1)}, bf16[1,512,768]{2,1,0:T(8,128)(2,1)}, u32[]{:S(2)}) copy-start(bf16[1,512,768]{2,1,0:T(8,128)(2,1)} %param.18) | copy-start | bytes 2359300
  7.3 51.2 %all-gather.10.cloned.1.call-start = ((), (), s32[]{:S(2)}) async-start(), calls=%async_computation.7 | async-start | bytes 1327104 | tf_op jit(solution)/shard_map/all_gather | solution.py:114
  8.0 52.8 %all-gather.12.cloned.1.call-start = ((), (), s32[]{:S(2)}) async-start(), calls=%async_computation.8 | async-start | bytes 1327104 | tf_op jit(solution)/shard_map/all_gather | solution.py:116
  8.8 74.7 %all-gather.8.cloned.1.call-start = ((), (), s32[]{:S(2)}) async-start(), calls=%async_computation.6 | async-start | bytes 1327104 | tf_op jit(solution)/shard_map/all_gather | solution.py:117
  9.5 100.0 %all-gather.14.cloned.1.call-start = ((), (), s32[]{:S(2)}) async-start(), calls=%async_computation.9 | async-start | bytes 1327104 | tf_op jit(solution)/shard_map/all_gather | solution.py:119
  10.1 150.3 %all-gather.16.cloned.1.call-start = ((), (), s32[]{:S(2)}) async-start(), calls=%async_computation.10 | async-start | bytes 5308416 | tf_op jit(solution)/shard_map/all_gather | solution.py:123
  10.7 201.8 %all-gather.18.cloned.1.call-start = ((), (), s32[]{:S(2)}) async-start(), calls=%async_computation.11 | async-start | bytes 5308416 | tf_op jit(solution)/shard_map/all_gather | solution.py:125
  11.3 293.7 %reduce-scatter.23.cloned.1.call-start = ((), (), s32[]{:S(2)}) async-start(), calls=%async_computation.17 | async-start | bytes 2654208
  60.8 26.9 %copy-start.2 = (bf16[512,768]{0,1:T(8,128)(2,1)}, bf16[512,768]{0,1:T(8,128)(2,1)S(1)}, u32[]{:S(2)}) copy-start(bf16[512,768]{0,1:T(8,128)(2,1)S(1)} %copy.62) | copy-start | bytes 2359300
  160.4 52.0 %copy-start.16 = (f32[512,768]{1,0:T(8,128)S(1)}, f32[512,768]{1,0:T(8,128)}, u32[]{:S(2)}) copy-start(f32[512,768]{1,0:T(8,128)} %copy-done.15) | copy-start | bytes 4718596
  212.5 9.9 %copy-start.42 = (f32[512,3072]{1,0:T(8,128)S(1)}, f32[512,3072]{1,0:T(8,128)}, u32[]{:S(2)}) copy-start(f32[512,3072]{1,0:T(8,128)} %get-tuple-element.171) | copy-start | bytes 18874372
  220.7 6.9 %slice-start = ((s8[4718592]{0:T(1024)(128)(4,1)}), s8[4194304]{0:T(1024)(128)(4,1)S(1)}, s32[]{:S(2)}) async-start(s8[4718592]{0:T(1024)(128)(4,1)} %bitcast.113), calls=%async_computation.19 | async-start | bytes 8388608
  247.4 73.0 %reduce-scatter.19.cloned.1.call-start = ((), (), s32[]{:S(2)}) async-start(), calls=%async_computation.15 | async-start | bytes 2654208
  271.1 87.1 %reduce-scatter.13.cloned.1.call-start = ((), (), s32[]{:S(2)}) async-start(), calls=%async_computation.12 | async-start | bytes 2654208 | tf_op jit(solution)/shard_map/reduce_scatter | solution.py:280
  274.5 121.4 %reduce-scatter.21.cloned.1.call-start = ((), (), s32[]{:S(2)}) async-start(), calls=%async_computation.16 | async-start | bytes 2654208
  286.6 210.3 %reduce-scatter.15.cloned.1.call-start = ((), (), s32[]{:S(2)}) async-start(), calls=%async_computation.13 | async-start | bytes 10616832 | tf_op jit(solution)/shard_map/reduce_scatter | solution.py:284
  295.2 301.7 %reduce-scatter.17.cloned.1.call-start = ((), (), s32[]{:S(2)}) async-start(), calls=%async_computation.14 | async-start | bytes 10616832 | tf_op jit(solution)/shard_map/reduce_scatter | solution.py:286
  304.9 363.3 %all-reduce.23.cloned.1.call-start = ((), (), s32[]{:S(2)}) async-start(), calls=%async_computation.18 | async-start | bytes 3833856 | tf_op jit(solution)/shard_map/psum | solution.py:292
  499.0 143.3 %copy-start.12 = (bf16[12,64,512]{2,1,0:T(8,128)(2,1)S(1)}, bf16[12,64,512]{2,1,0:T(8,128)(2,1)}, u32[]{:S(2)}) copy-start(bf16[12,64,512]{2,1,0:T(8,128)(2,1)} %copy-done.11) | copy-start | bytes 2359300
  (34 other events, 100.1 us)
Sparse Core Ops, SparseCore 0:
  9.8 25.5 all-gather.9
  37.0 22.3 all-gather.11
  61.0 22.3 all-gather.7
  84.9 22.4 all-gather.13
  108.9 51.4 all-gather.15
  161.9 50.5 all-gather.17
  247.5 35.3 reduce-scatter.22
  285.2 35.1 reduce-scatter.18
  322.7 35.4 reduce-scatter.12
  360.3 35.4 reduce-scatter.20
  398.1 98.6 reduce-scatter.14
  499.0 97.8 reduce-scatter.16
  601.4 66.7 all-reduce.22
where the time goes:
time: 686 us; the launch traced here: 682 us
  waiting for transfers between devices  417 us (61%)
  matrix products  89.8 us (13%)
  blocking collectives  79.6 us (12%)
  local copies, waits for them, and re-layouts  38.8 us (6%)
  other arithmetic  38.1 us (6%)
  between operations  17.4 us (3%)
    reduce_scatter x1, waiting for transfers between devices, on_device(): lax.psum_scatter(local_grads[9], 'fsdp', scatter_dimension=0, tiled=True)  99.3 us
    reduce_scatter x1, waiting for transfers between devices, on_device(): lax.psum_scatter(local_grads[11], 'fsdp', scatter_dimension=0, tiled=True)  97.9 us
    unnamed x2, blocking collectives  56.7 us
    unnamed x16, waiting for transfers between devices  53.4 us
    all_gather x1, waiting for transfers between devices, on_device(): lax.all_gather(inner_weight, 'fsdp', axis=0, tiled=True)  47 us
    all_gather x1, waiting for transfers between devices, on_device(): lax.all_gather(outer_weight, 'fsdp', axis=0, tiled=True)  43.5 us
    reduce_scatter x1, waiting for transfers between devices, on_device(): lax.psum_scatter(local_grads[5], 'fsdp', scatter_dimension=0, tiled=True)  36.1 us
    unnamed x126, local copies, waits for them, and re-layouts  34.4 us
  transfers between devices with their start and end apart: 13, of which 9 were waited for; matrix products, arithmetic and copies ran while one was open for 16% of the time, Pallas kernels for 0%

commit v1 on v0

v1 whole, which is shorter than its diff:
```python
import functools
import math

import jax
import jax.numpy as jnp
from jax import lax
from jax.experimental import pallas as pl
from jax.experimental.pallas import tpu as pltpu
from jax.sharding import PartitionSpec as P

F32 = jnp.float32
BF16 = jnp.bfloat16
HD = 64
MASKED = -1e30
SCALE = HD ** -0.5
EPSILON = 1e-12
ROOT_HALF = math.sqrt(0.5)
INV_ROOT_TWO_PI = 1.0 / math.sqrt(2.0 * math.pi)

VM = pl.BlockSpec(memory_space=pltpu.VMEM)
SM = pl.BlockSpec(memory_space=pltpu.SMEM)
HB = pl.BlockSpec(memory_space=pl.ANY)


def shape(*dims, dtype=BF16):
    return jax.ShapeDtypeStruct(dims, dtype)


def dot_nn(a, b):
    return lax.dot_general(a, b, (((1,), (0,)), ((), ())), preferred_element_type=F32)


def dot_nt(a, b):
    return lax.dot_general(a, b, (((1,), (1,)), ((), ())), preferred_element_type=F32)


def flip(value):
    return value.astype(F32).T.astype(BF16)


def column_sum(value):
    return jnp.sum(value.astype(F32), axis=0, keepdims=True)


def row_mean(value):
    return jnp.mean(value, axis=-1, keepdims=True)


def aligned(start, size):
    return pl.ds(pl.multiple_of(start, size), size)


class Pieces:
    def __init__(self, arrays, own, sibling, far, far_sibling, stacked):
        self.arrays, self.own, self.sibling = arrays, own, sibling
        self.far, self.far_sibling, self.stacked = far, far_sibling, stacked

    def count(self, blocks):
        return 2 * len(blocks) + 2 * 5 * 3

    def copies(self, refs, me_ref, target, sems, base, blocks):
        i, z, c = me_ref[0], me_ref[1], me_ref[2]
        done = []

        def place(block, z_at, c_at, offset, rows):
            if self.stacked:
                start = (2 * z_at + c_at) * 96 + offset
                return target.at[block, aligned_rows(start, rows), :]
            start = (2 * z_at + c_at) * 384 + block * 96 + offset
            return target.at[aligned_rows(start, rows), :]

        def add(source, where):
            done.append(pltpu.make_async_copy(source, where, sems.at[base + len(done)]))

        for c_at, near, far in ((c, self.own, self.far), (1 - c, self.sibling, self.far_sibling)):
            for block in blocks:
                position, row, lane = near[block]
                add(refs[position].at[pl.ds(row, 96), pl.ds(lane, 768)], place(block, z, c_at, 0, 96))
            for j in range(1, 4):
                for away in range(3):
                    add(refs[far[away]].at[j - 1], place(i ^ away, z ^ j, c_at, 0, 96))
                add(refs[far[3]].at[j - 1], place(i ^ 3, z ^ j, c_at, 0, 48))
                add(refs[far[4]].at[j - 1], place(i ^ 3, z ^ j, c_at, 48, 48))
        return done


def aligned_rows(start, rows):
    return pl.ds(pl.multiple_of(start, 16), rows)


class Whole:
    def __init__(self, arrays, spots, stacked):
        self.arrays, self.spots, self.stacked = arrays, spots, stacked

    def count(self, blocks):
        return len(blocks)

    def copies(self, refs, me_ref, target, sems, base, blocks):
        done = []
        for block in blocks:
            position, row, lane = self.spots[block]
            where = target.at[block] if self.stacked else target.at[pl.ds(block * 768, 768), :]
            source = refs[position].at[pl.ds(row, 768), pl.ds(lane, 768)]
            done.append(pltpu.make_async_copy(source, where, sems.at[base + block]))
        return done


def start_all(copies):
    for copy in copies:
        copy.start()


def wait_all(copies):
    for copy in copies:
        copy.wait()


def pair_masks(dims, axis):
    spot = lax.broadcasted_iota(jnp.int32, dims, axis)
    return spot < HD, spot >= HD


def keep(mask, value):
    return jnp.where(mask, value, jnp.zeros_like(value))


def attend_forward_body(group, me_ref, len_ref, x_ref, vec_ref, *refs):
    sources = refs[: len(group.arrays)]
    q_ref, k_ref, v_ref, att_ref, left_ref, lse_ref, w_ref, sems = refs[len(group.arrays) :]
    seq, width = x_ref.shape
    tile = min(256, seq)
    loads = group.copies(sources, me_ref, w_ref, sems, 0, (0, 1, 2))
    start_all(loads)
    for p in range(width // 128):
        left_ref[0, p * 128 : (p + 1) * 128, :] = flip(x_ref[:, p * 128 : (p + 1) * 128])
    wait_all(loads)

    def project(r, carry):
        rows = aligned(r * tile, tile)
        x = x_ref[rows, :]
        q_ref[rows, :] = (dot_nn(x, w_ref[0]) + vec_ref[0:1, :]).astype(BF16)
        k_ref[rows, :] = dot_nn(x, w_ref[1]).astype(BF16)
        v_ref[rows, :] = (dot_nn(x, w_ref[2]) + vec_ref[1:2, :]).astype(BF16)
        return carry

    lax.fori_loop(0, seq // tile, project, 0)
    length = len_ref[0]

    def pair(p, carry):
        lanes = aligned(p * 128, 128)
        k_pair = k_ref[:, lanes]
        q_t = (q_ref[:, lanes].astype(F32) * SCALE).T.astype(BF16)
        v_t = flip(v_ref[:, lanes])
        masks = pair_masks((128, seq), 0)
        allowed = lax.broadcasted_iota(jnp.int32, (seq, seq), 0) < length
        for e in range(2):
            s = dot_nn(k_pair, keep(masks[e], q_t))
            s = jnp.where(allowed, s, MASKED)
            top = jnp.max(s, axis=0, keepdims=True)
            p_t = jnp.exp(s - top)
            total = jnp.sum(p_t, axis=0, keepdims=True)
            o_t = dot_nn(v_t[e * HD : (e + 1) * HD, :], p_t.astype(BF16)) / total
            left_ref[1, aligned(p * 128 + e * HD, HD), :] = o_t.astype(BF16)
            lse_ref[pl.ds(p * 2 + e, 1), :] = top + jnp.log(total)
        att_ref[:, lanes] = flip(left_ref[1, aligned(p * 128, 128), :])
        return carry

    lax.fori_loop(0, width // 128, pair, 0)


def attend_forward(group, me, length, x, vec):
    seq, width = x.shape
    heads = width // HD
    return pl.pallas_call(
        functools.partial(attend_forward_body, group),
        out_shape=(shape(seq, width),) * 4 + (shape(2, width, seq), shape(-(-heads // 8) * 8, seq, dtype=F32)),
        in_specs=[SM, SM, VM, VM] + [HB] * len(group.arrays),
        out_specs=[VM] * 6,
        scratch_shapes=[pltpu.VMEM((4, width, width), BF16), pltpu.SemaphoreType.DMA((group.count((0, 1, 2)),))],
        cost_estimate=pl.CostEstimate(flops=12_000_000_000, bytes_accessed=20_000_000, transcendentals=3_200_000),
        name="attend_forward",
    )(me, length, x, vec, *group.arrays)


def attend_backward_body(len_ref, q_ref, k_ref, v_ref, do_ref, lse_ref, branch_ref, g_ref, sum_ref):
    seq, width = q_ref.shape
    length = len_ref[0]

    def pair(p, carry):
        lanes = aligned(p * 128, 128)
        q_pair = (q_ref[:, lanes].astype(F32) * SCALE).astype(BF16)
        k_pair = k_ref[:, lanes]
        v_pair = v_ref[:, lanes]
        do_pair = do_ref[:, lanes]
        q_t = flip(q_pair)
        k_t = (k_pair.astype(F32) * SCALE).T.astype(BF16)
        do_t = flip(do_pair)
        sub_masks = pair_masks((128, seq), 0)
        lane_masks = pair_masks((seq, 128), 1)
        allowed = lax.broadcasted_iota(jnp.int32, (seq, seq), 0) < length
        dk = jnp.zeros((seq, 128), F32)
        dv = jnp.zeros((seq, 128), F32)
        dq_t = []
        for e in range(2):
            s = dot_nn(k_pair, keep(sub_masks[e], q_t))
            s = jnp.where(allowed, s, MASKED)
            p_t = jnp.exp(s - lse_ref[pl.ds(p * 2 + e, 1), :])
            dp = dot_nn(v_pair, keep(sub_masks[e], do_t))
            dv = dv + dot_nn(p_t.astype(BF16), keep(lane_masks[e], do_pair))
            t = p_t * dp
            row = jnp.sum(t, axis=0, keepdims=True)
            ds = (t - p_t * row).astype(BF16)
            dk = dk + dot_nn(ds, keep(lane_masks[e], q_pair))
            dq_t.append(dot_nn(k_t[e * HD : (e + 1) * HD, :], ds))
        dq = jnp.concatenate(dq_t, axis=0).T.astype(BF16)
        dv = dv.astype(BF16)
        g_ref[0, :, lanes] = dq
        g_ref[1, :, lanes] = dk.astype(BF16)
        g_ref[2, :, lanes] = dv
        g_ref[3, :, lanes] = branch_ref[:, lanes]
        sum_ref[0:1, lanes] = column_sum(dq)
        sum_ref[1:2, lanes] = column_sum(dv)
        return carry

    lax.fori_loop(0, width // 128, pair, 0)


def attend_backward(length, q, k, v, do, lse, branch):
    seq, width = q.shape
    return pl.pallas_call(
        attend_backward_body,
        out_shape=(shape(4, seq, width), shape(8, width, dtype=F32)),
        in_specs=[SM] + [VM] * 6,
        out_specs=[VM] * 2,
        cost_estimate=pl.CostEstimate(flops=16_000_000_000, bytes_accessed=9_000_000, transcendentals=3_200_000),
        name="attend_backward",
    )(length, q, k, v, do, lse, branch)


def gelu_parts(inner):
    cumulative = 0.5 * (1.0 + lax.erf(inner * ROOT_HALF))
    density = jnp.exp(-0.5 * inner * inner) * INV_ROOT_TWO_PI
    return inner * cumulative, cumulative + inner * density


def middle_forward_body(groups, me_ref, len_ref, x_ref, att_ref, cot_ref, vec_ref, ib_ref, *refs):
    counts = [len(g.arrays) for g in groups]
    sources = [refs[sum(counts[:n]) : sum(counts[: n + 1])] for n in range(3)]
    (out_ref, ssg_ref, low_ref, actT_ref, slope_ref, norm_ref, rstd_ref, hidT_ref, sum_ref, wa, wi, wu, sems) = refs[sum(counts) :]
    seq, width = x_ref.shape
    blocks = wi.shape[0]
    tile = min(256, seq)
    spots = [0, groups[0].count((3,)), groups[0].count((3,)) + groups[1].count(range(blocks))]
    load_a = groups[0].copies(sources[0], me_ref, wa, sems, spots[0], (3,))
    load_i = groups[1].copies(sources[1], me_ref, wi, sems, spots[1], range(blocks))
    load_u = groups[2].copies(sources[2], me_ref, wu, sems, spots[2], range(blocks))
    start_all(load_a + load_i + load_u)
    length = len_ref[0]
    sum_ref[...] = jnp.zeros_like(sum_ref)
    wait_all(load_a + load_i + load_u)

    def rows_step(r, carry):
        rows = aligned(r * tile, tile)
        first = x_ref[rows, :].astype(F32) + dot_nn(att_ref[rows, :], wa[3]) + vec_ref[2:3, :]
        center = first - row_mean(first)
        rstd = lax.rsqrt(row_mean(center * center) + EPSILON)
        normed = center * rstd
        norm_ref[rows, :] = normed
        rstd_ref[rows, :] = rstd
        hidden = normed * vec_ref[3:4, :] + vec_ref[4:5, :]
        low = hidden.astype(BF16)
        hidT_ref[:, rows] = low.astype(F32).T.astype(BF16)

        def block(f, second):
            inner = dot_nn(low, wi[f]) + ib_ref[pl.ds(f, 1), :]
            active, slope = gelu_parts(inner)
            active = active.astype(BF16)
            spot = aligned(f * width, width)
            slope_ref[rows, spot] = slope.astype(BF16)
            actT_ref[spot, rows] = flip(active)
            return second + dot_nn(active, wu[spot, :])

        second = lax.fori_loop(0, blocks, block, hidden + vec_ref[5:6, :])
        center = second - row_mean(second)
        rstd = lax.rsqrt(row_mean(center * center) + EPSILON)
        normed = center * rstd
        spot = r * tile + lax.broadcasted_iota(jnp.int32, (tile, width), 0)
        valid = spot < length
        result = normed * vec_ref[6:7, :] + vec_ref[7:8, :]
        out_ref[rows, :] = jnp.where(valid, result, 0.0).astype(BF16)
        grad = jnp.where(valid, cot_ref[rows, :].astype(F32), 0.0)
        sum_ref[7:8, :] += column_sum(grad)
        sum_ref[6:7, :] += column_sum(grad * normed)
        grad = grad * vec_ref[6:7, :]
        grad = rstd * (grad - row_mean(grad) - normed * row_mean(grad * normed))
        ssg_ref[rows, :] = grad
        low = grad.astype(BF16)
        low_ref[rows, :] = low
        sum_ref[5:6, :] += column_sum(low)
        return carry

    lax.fori_loop(0, seq // tile, rows_step, 0)


def middle_forward(groups, me, length, x, att, cot, vec, ib):
    seq, width = x.shape
    blocks = ib.shape[0]
    count = groups[0].count((3,)) + groups[1].count(range(blocks)) + groups[2].count(range(blocks))
    arrays = [a for g in groups for a in g.arrays]
    return pl.pallas_call(
        functools.partial(middle_forward_body, groups),
        out_shape=(
            shape(seq, width),
            shape(seq, width, dtype=F32),
            shape(seq, width),
            shape(blocks * width, seq),
            shape(seq, blocks * width),
            shape(seq, width, dtype=F32),
            shape(seq, 1, dtype=F32),
            shape(width, seq),
            shape(8, width, dtype=F32),
        ),
        in_specs=[SM, SM] + [VM] * 5 + [HB] * len(arrays),
        out_specs=[VM] * 9,
        scratch_shapes=[
            pltpu.VMEM((4, width, width), BF16),
            pltpu.VMEM((blocks, width, width), BF16),
            pltpu.VMEM((blocks * width, width), BF16),
            pltpu.SemaphoreType.DMA((count,)),
        ],
        cost_estimate=pl.CostEstimate(flops=12_000_000_000, bytes_accessed=30_000_000, transcendentals=3_200_000),
        name="middle_forward",
    )(me, length, x, att, cot, vec, ib, *arrays)


def middle_backward_body(groups, me_ref, low_ref, ssg_ref, slope_ref, norm_ref, rstd_ref, vec_ref, *refs):
    counts = [len(g.arrays) for g in groups]
    sources = [refs[sum(counts[:n]) : sum(counts[: n + 1])] for n in range(3)]
    (igl_ref, fsg_ref, branch_ref, att_ref, ib_ref, sum_ref, wa, wi, wu, sems) = refs[sum(counts) :]
    seq, width = low_ref.shape
    blocks = wi.shape[0]
    tile = min(256, seq)
    spots = [0, groups[0].count((3,)), groups[0].count((3,)) + groups[1].count(range(blocks))]
    load_a = groups[0].copies(sources[0], me_ref, wa, sems, spots[0], (3,))
    load_i = groups[1].copies(sources[1], me_ref, wi, sems, spots[1], range(blocks))
    load_u = groups[2].copies(sources[2], me_ref, wu, sems, spots[2], range(blocks))
    start_all(load_u + load_i + load_a)
    sum_ref[...] = jnp.zeros_like(sum_ref)
    ib_ref[...] = jnp.zeros_like(ib_ref)
    wait_all(load_u + load_i + load_a)

    def rows_step(r, carry):
        rows = aligned(r * tile, tile)
        low = low_ref[rows, :]

        def block(f, grad):
            spot = aligned(f * width, width)
            inner = (dot_nt(low, wu[spot, :]) * slope_ref[rows, spot].astype(F32)).astype(BF16)
            igl_ref[f, rows, :] = inner
            ib_ref[pl.ds(f, 1), :] += column_sum(inner)
            return grad + dot_nt(inner, wi[f])

        grad = lax.fori_loop(0, blocks, block, ssg_ref[rows, :])
        normed = norm_ref[rows, :]
        sum_ref[4:5, :] += column_sum(grad)
        sum_ref[3:4, :] += column_sum(grad * normed)
        grad = grad * vec_ref[3:4, :]
        grad = rstd_ref[rows, :] * (grad - row_mean(grad) - normed * row_mean(grad * normed))
        fsg_ref[rows, :] = grad
        branch = grad.astype(BF16)
        branch_ref[rows, :] = branch
        sum_ref[2:3, :] += column_sum(branch)
        att_ref[rows, :] = dot_nt(branch, wa[3]).astype(BF16)
        return carry

    lax.fori_loop(0, seq // tile, rows_step, 0)


def middle_backward(groups, me, low, ssg, slope, norm, rstd, vec, blocks):
    seq, width = low.shape
    count = groups[0].count((3,)) + groups[1].count(range(blocks)) + groups[2].count(range(blocks))
    arrays = [a for g in groups for a in g.arrays]
    return pl.pallas_call(
        functools.partial(middle_backward_body, groups),
        out_shape=(
            shape(blocks, seq, width),
            shape(seq, width, dtype=F32),
            shape(seq, width),
            shape(seq, width),
            shape(blocks, width, dtype=F32),
            shape(8, width, dtype=F32),
        ),
        in_specs=[SM] + [VM] * 6 + [HB] * len(arrays),
        out_specs=[VM] * 6,
        scratch_shapes=[
            pltpu.VMEM((4, width, width), BF16),
            pltpu.VMEM((blocks, width, width), BF16),
            pltpu.VMEM((blocks * width, width), BF16),
            pltpu.SemaphoreType.DMA((count,)),
        ],
        cost_estimate=pl.CostEstimate(flops=9_000_000_000, bytes_accessed=25_000_000, transcendentals=0),
        name="middle_backward",
    )(me, low, ssg, slope, norm, rstd, vec, *arrays)


def input_grad_body(group, me_ref, g_ref, fsg_ref, *refs):
    sources = refs[: len(group.arrays)]
    out_ref, w_ref, sems = refs[len(group.arrays) :]
    seq, width = fsg_ref.shape
    tile = min(256, seq)
    loads = group.copies(sources, me_ref, w_ref, sems, 0, (0, 1, 2))
    start_all(loads)
    wait_all(loads)

    def rows_step(r, carry):
        rows = aligned(r * tile, tile)
        total = fsg_ref[rows, :]
        for n in range(3):
            total = total + dot_nt(g_ref[n, rows, :], w_ref[n])
        out_ref[rows, :] = total
        return carry

    lax.fori_loop(0, seq // tile, rows_step, 0)


def input_grad(group, me, g, fsg):
    seq, width = fsg.shape
    return pl.pallas_call(
        functools.partial(input_grad_body, group),
        out_shape=shape(seq, width, dtype=F32),
        in_specs=[SM, VM, VM] + [HB] * len(group.arrays),
        out_specs=VM,
        scratch_shapes=[pltpu.VMEM((4, width, width), BF16), pltpu.SemaphoreType.DMA((group.count((0, 1, 2)),))],
        cost_estimate=pl.CostEstimate(flops=4_000_000_000, bytes_accessed=10_000_000, transcendentals=0),
        name="input_grad",
    )(me, g, fsg, *group.arrays)


Z_ORDER = (0, 2, 1, 3)


def weight_grad_body(kind, orders, sibling, summed, me_ref, left_ref, g_ref, *refs):
    if summed:
        add_ref, refs = refs[0], refs[1:]
    outs, left = refs[:-1], refs[-1]
    i, z, c = me_ref[0], me_ref[1], me_ref[2]
    c_at = (1 - c) if sibling else c
    for out_ref, order in zip(outs, orders, strict=True):
        for spot, away in enumerate(order):
            block = i ^ away
            for n, j in enumerate(Z_ORDER):
                z_at = z ^ j
                if kind == "outer":
                    rows = left_ref[aligned_rows((2 * z_at + c_at) * 384 + block * 96, 96), :]
                elif kind == "inner":
                    rows = left_ref[aligned_rows((2 * z_at + c_at) * 96, 96), :]
                else:
                    rows = left_ref[block // 3, aligned_rows((2 * z_at + c_at) * 96, 96), :]
                left[n * 96 : (n + 1) * 96, :] = rows
            right = g_ref[...] if kind == "outer" else g_ref[block]
            total = dot_nn(left[...], right).reshape(4, 96, 768)
            if summed:
                total = total + add_ref[away].astype(F32)
            out_ref[spot] = total.astype(BF16)


def weight_grad(kind, orders, sibling, me, left, g, add=None):
    summed = add is not None
    return pl.pallas_call(
        functools.partial(weight_grad_body, kind, orders, sibling, summed),
        out_shape=tuple(shape(len(order), 4, 96, 768) for order in orders),
        in_specs=[SM, VM, VM] + [VM] * summed,
        out_specs=[VM] * len(orders),
        scratch_shapes=[pltpu.VMEM((384, left.shape[-1]), BF16)],
        cost_estimate=pl.CostEstimate(flops=2_000_000_000, bytes_accessed=6_000_000, transcendentals=0),
        name=f"weight_grad_{kind}",
    )(*((me, left, g) + ((add,) if summed else ())))


def swap(value, axis, size, mask):
    return lax.ppermute(value, axis, [(n, n ^ mask) for n in range(size)])


def gather_group(piece, fsdp, dp):
    far = [swap(piece, "fsdp", fsdp, 2 * j) for j in (1, 2, 3)]
    mine = jnp.stack(far)
    over_x = swap(mine, "dp", dp, 1)
    over_y = swap(mine, "dp", dp, 2)
    half_a = swap(over_x[:, :48], "dp", dp, 2)
    half_b = swap(over_y[:, 48:], "dp", dp, 1)
    near = (mine, over_x, over_y, half_a, half_b)
    return near, tuple(swap(v, "fsdp", fsdp, 1) for v in near)


def add_low(a, b):
    return (a.astype(F32) + b.astype(F32)).astype(BF16)


def scatter_planes(send, held, first, fsdp, dp):
    got = swap(send, "dp", dp, first)
    onward = swap(add_low(held[1], got[1]), "dp", dp, 3 - first)
    return (held[0].astype(F32) + got[0].astype(F32) + onward.astype(F32)).astype(BF16)


def scatter_z(value, fsdp):
    got = swap(value[2:], "fsdp", fsdp, 2)
    onward = swap(add_low(value[1], got[1]), "fsdp", fsdp, 4)
    return (value[0].astype(F32) + got[0].astype(F32) + onward.astype(F32)).astype(BF16)


def spread(value, dp):
    return (value,) + tuple(swap(value, "dp", dp, m) for m in (1, 2, 3))


def pick(pieces, index):
    return jnp.where(index == 0, pieces[0], jnp.where(index == 1, pieces[1], jnp.where(index == 2, pieces[2], pieces[3])))


def in_order(pieces, i):
    return [pick(pieces, n ^ i) for n in range(4)]


def on_device(
    sizes,
    tokens,
    lengths,
    cotangent,
    query_weight,
    query_bias,
    key_weight,
    value_weight,
    value_bias,
    output_weight,
    output_bias,
    first_gain,
    first_shift,
    inner_weight,
    inner_bias,
    outer_weight,
    outer_bias,
    second_gain,
    second_shift,
):
    dp, fsdp = sizes
    docs, seq, width = tokens.shape
    blocks = inner_weight.shape[1] // width
    direct = dp == 4 and fsdp == 8 and docs == 1 and query_weight.shape == (96, 768) and blocks == 4
    i = lax.axis_index("dp")
    f = lax.axis_index("fsdp")
    me = jnp.stack([i, f // 2, f % 2, jnp.zeros_like(i)]).astype(jnp.int32)

    small = (query_bias, value_bias, output_bias, first_gain, first_shift, outer_bias, second_gain, second_shift, inner_bias)
    part = query_bias.shape[0]
    packed = lax.all_gather(jnp.concatenate(small), "fsdp", axis=0, tiled=False).astype(F32)
    vec = packed[:, : 8 * part].reshape(fsdp, 8, part).transpose(1, 0, 2).reshape(8, width)
    ib = packed[:, 8 * part :].reshape(blocks, width)

    if direct:
        mine = (query_weight, key_weight, value_weight, output_weight)
        near_a, far_a = gather_group(pick(mine, i), fsdp, dp)
        near_i, far_i = gather_group(lax.dynamic_slice(inner_weight, (0, i * 768), (96, 768)), fsdp, dp)
        near_u, far_u = gather_group(lax.dynamic_slice(outer_weight, (i * 96, 0), (96, 768)), fsdp, dp)
        theirs = tuple(swap(w, "fsdp", fsdp, 1) for w in mine)
        inner_other = swap(inner_weight, "fsdp", fsdp, 1)
        outer_other = swap(outer_weight, "fsdp", fsdp, 1)
        four = range(4)
        group_a = Pieces(
            mine + theirs + near_a + far_a,
            [(n, 0, 0) for n in four],
            [(4 + n, 0, 0) for n in four],
            tuple(range(8, 13)),
            tuple(range(13, 18)),
            True,
        )
        group_i = Pieces(
            (inner_weight, inner_other) + near_i + far_i,
            [(0, 0, 768 * n) for n in four],
            [(1, 0, 768 * n) for n in four],
            tuple(range(2, 7)),
            tuple(range(7, 12)),
            True,
        )
        group_u = Pieces(
            (outer_weight, outer_other) + near_u + far_u,
            [(0, 96 * n, 0) for n in four],
            [(1, 96 * n, 0) for n in four],
            tuple(range(2, 7)),
            tuple(range(7, 12)),
            False,
        )
    else:
        whole = tuple(
            lax.all_gather(w, "fsdp", axis=0, tiled=True)
            for w in (query_weight, key_weight, value_weight, output_weight, inner_weight, outer_weight)
        )
        group_a = Whole(whole[:4], [(n, 0, 0) for n in range(4)], True)
        group_i = Whole(whole[4:5], [(0, 0, width * n) for n in range(blocks)], True)
        group_u = Whole(whole[5:6], [(0, width * n, 0) for n in range(blocks)], False)

    x = tokens.reshape(seq, width)
    cot = cotangent.reshape(seq, width)
    groups = (group_a, group_i, group_u)
    q, k, v, att, left_a, lse = attend_forward(group_a, me, lengths, x, vec)
    out, ssg, low, act_t, slope, norm, rstd, hid_t, sum_one = middle_forward(groups, me, lengths, x, att, cot, vec, ib)

    if direct:
        (sent_u,) = weight_grad("outer", ((0, 1, 2, 3),), True, me, act_t, low)
        got_u = swap(sent_u, "fsdp", fsdp, 1)
        send_u, held_u = weight_grad("outer", ((1, 3), (0, 2)), False, me, act_t, low, got_u)
        plane_u = scatter_planes(send_u, held_u, 1, fsdp, dp)
    igl, fsg, branch, att_g, ib_sum, sum_two = middle_backward(groups, me, low, ssg, slope, norm, rstd, vec, blocks)
    if direct:
        (sent_i,) = weight_grad("inner", ((0, 1, 2, 3),), True, me, hid_t, igl)
        got_i = swap(sent_i, "fsdp", fsdp, 1)
        send_i, held_i = weight_grad("inner", ((2, 3), (0, 1)), False, me, hid_t, igl, got_i)
        plane_i = scatter_planes(send_i, held_i, 2, fsdp, dp)
    g, sum_three = attend_backward(lengths, q, k, v, att_g, lse, branch)
    in_grad = input_grad(group_a, me, g, fsg)

    vec_sum = jnp.concatenate([sum_three[:2], sum_two[2:5], sum_one[5:8]])
    vec_sum = vec_sum.reshape(8, fsdp, part).transpose(1, 0, 2).reshape(fsdp, 8 * part)
    small_sum = jnp.concatenate([vec_sum, ib_sum.reshape(fsdp, blocks * part)], axis=1)
    small_sum = lax.psum(small_sum, ("dp", "fsdp"))
    small_own = lax.dynamic_index_in_dim(small_sum, f, 0, keepdims=False)
    small_grads = [small_own[n * part : (n + 1) * part] for n in range(8)] + [small_own[8 * part :]]

    if direct:
        (sent_a,) = weight_grad("attend", ((0, 1, 2, 3),), True, me, left_a, g)
        got_a = swap(sent_a, "fsdp", fsdp, 1)
        send_a, held_a = weight_grad("attend", ((1, 3), (0, 2)), False, me, left_a, g, got_a)
        plane_a = scatter_planes(send_a, held_a, 1, fsdp, dp)
        own = [in_order(spread(scatter_z(p, fsdp), dp), i) for p in (plane_a, plane_i, plane_u)]
        q_g, k_g, v_g, o_g = (w.astype(F32) for w in own[0])
        i_g = jnp.concatenate(own[1], axis=1).astype(F32)
        u_g = jnp.concatenate(own[2], axis=0).astype(F32)
    else:
        x_t, att_t = left_a[0], left_a[1]
        locals_ = (
            dot_nn(x_t, g[0]),
            dot_nn(x_t, g[1]),
            dot_nn(x_t, g[2]),
            dot_nn(att_t, g[3]),
            jnp.concatenate([dot_nn(hid_t, igl[n]) for n in range(blocks)], axis=1),
            dot_nn(act_t, low),
        )
        owned = [lax.psum_scatter(w, "fsdp", scatter_dimension=0, tiled=True) for w in locals_]
        q_g, k_g, v_g, o_g, i_g, u_g = (lax.psum(w.astype(BF16), "dp").astype(F32) for w in owned)

    qb, vb, ob, g1, s1, ub, g2, s2, ibg = small_grads
    return (
        out.reshape(docs, seq, width),
        in_grad.reshape(docs, seq, width),
        q_g,
        qb,
        k_g,
        v_g,
        vb,
        o_g,
        ob,
        g1,
        s1,
        i_g,
        ibg,
        u_g,
        ub,
        g2,
        s2,
    )


def solution(mesh):
    rows, row = P("fsdp", None), P("fsdp")
    docs = P(("dp", "fsdp"), None, None)
    in_specs = (docs, P(("dp", "fsdp")), docs, rows, row, rows, rows, row, rows, row, row, row, rows, row, rows, row, row, row)
    out_specs = (docs, docs, rows, row, rows, rows, row, rows, row, row, row, rows, row, rows, row, row, row)
    sizes = (mesh.shape["dp"], mesh.shape["fsdp"])
    return jax.shard_map(
        functools.partial(on_device, sizes), mesh=mesh, in_specs=in_specs, out_specs=out_specs, check_vma=False
    )
```

time: 686 us -> 378 us (0.55)
  waiting for transfers between devices: 417 us -> 89.1 us
  Pallas kernels: 0 us -> 116 us
  matrix products: 89.8 us -> 0 us
  starting transfers between devices: 0.69 us -> 63.6 us
  other arithmetic: 38.1 us -> 8.74 us
  local copies, waits for them, and re-layouts: 38.8 us -> 10.2 us
  between operations: 17.4 us -> 2.12 us
  blocking collectives: 79.6 us -> 87.3 us
    reduce_scatter x3 -> x0, waiting for transfers between devices: 233 us -> none  [the longest x1 99.3 us: on_device(): lax.psum_scatter(local_grads[9], 'fsdp', scatter_dimension=0, tiled=True)]
    pallas_call x0 -> x11, Pallas kernels: none -> 116 us  [the longest x6 31.4 us: weight_grad(): pl.pallas_call(functools.partial(weight_grad_body, kind, orders, sibling,...]
    all_gather x6 -> x0, waiting for transfers between devices: 111 us -> none  [the longest x1 47 us: on_device(): lax.all_gather(inner_weight, 'fsdp', axis=0, tiled=True)]
    dot_general x24 -> x0, matrix products: 89.8 us -> none  [the longest x6 24.3 us: weight_grad(): jnp.einsum('tr,tc->rc', left, right, preferred_element_type=jnp.float32)]
    ppermute x0 -> x66, waiting for transfers between devices: none -> 89.1 us  [swap(): return lax.ppermute(value, axis, [(n, n ^ mask) for n in range(size)])]
    ppermute x0 -> x66, starting transfers between devices: none -> 63.6 us  [swap(): return lax.ppermute(value, axis, [(n, n ^ mask) for n in range(size)])]
    psum x1, blocking collectives: 9.97 us -> 73.3 us  [on_device(): small_sum = lax.psum(small_sum, ('dp', 'fsdp'))]
    unnamed x2 -> x0, blocking collectives: 56.7 us -> none
  transfers between devices with their start and end apart: 13 -> 66, of which waited for: 9 -> 23; matrix products, arithmetic and copies ran while one was open for 16% -> 4% of each run, Pallas kernels for 0% -> 23%
where the time goes in v1:
time: 378 us; the launch traced here: 377 us
  Pallas kernels  116 us (31%)
  waiting for transfers between devices  89.1 us (24%)
  blocking collectives  87.3 us (23%)
  starting transfers between devices  63.6 us (17%)
  local copies, waits for them, and re-layouts  10.2 us (3%)
  other arithmetic  8.74 us (2%)
    ppermute x66, waiting for transfers between devices, swap(): return lax.ppermute(value, axis, [(n, n ^ mask) for n in range(size)])  89.1 us
    psum x1, blocking collectives, on_device(): small_sum = lax.psum(small_sum, ('dp', 'fsdp'))  73.3 us
    ppermute x66, starting transfers between devices, swap(): return lax.ppermute(value, axis, [(n, n ^ mask) for n in range(size)])  63.6 us
    pallas_call x6, Pallas kernels, weight_grad(): pl.pallas_call(functools.partial(weight_grad_body, kind, orders, sibling,...  31.4 us
    pallas_call x1, Pallas kernels, middle_forward(): pl.pallas_call(functools.partial(middle_forward_body, groups), out_shape=...  23.8 us
    pallas_call x1, Pallas kernels, middle_backward(): pl.pallas_call(functools.partial(middle_backward_body, groups), out_shape...  20.8 us
    pallas_call x1, Pallas kernels, attend_backward(): pl.pallas_call(attend_backward_body, out_shape=(shape(4, seq, width), sha...  16.2 us
    pallas_call x1, Pallas kernels, attend_forward(): pl.pallas_call(functools.partial(attend_forward_body, group), out_shape=(...  15.6 us
  transfers between devices with their start and end apart: 66, of which 23 were waited for; matrix products, arithmetic and copies ran while one was open for 4% of the time, Pallas kernels for 23%

profile of v1, /device:TPU:0, one launch (start us, length us, event | category | flops | bytes accessed | tf_op | source)
XLA Modules:
  0.0 377.4 jit_solution(5053445058847036352)
XLA Ops:
  12.6 9.4 %collective-permute-done.5 = bf16[96,768]{1,0:T(8,128)(2,1)S(1)} collective-permute-done((bf16[96,768]{1,0:T(8,128)(2,1)S(1)}, bf16[96,768]{1,0:T(8,128)(2,1)S(1)}, u32[]{:S(2)}, u32[]{:S(2)}) %collective-permute-start.5) | collective-permute-done | bytes 147488 | tf_op jit(solution)/shard_map/ppermute | solution.py:481
  39.9 4.2 %collective-permute-done.31 = bf16[96,768]{1,0:T(8,128)(2,1)S(1)} collective-permute-done((bf16[96,768]{1,0:T(8,128)(2,1)S(1)}, bf16[96,768]{1,0:T(8,128)(2,1)S(1)}, u32[]{:S(2)}, u32[]{:S(2)}) %collective-permute-start.31) | collective-permute-done | bytes 147488 | tf_op jit(solution)/shard_map/ppermute | solution.py:481
  48.4 6.3 %collective-permute-done.8.refs_10_ = bf16[3,96,768]{2,1,0:T(8,128)(2,1)S(1)} collective-permute-done((bf16[3,96,768]{2,1,0:T(8,128)(2,1)S(1)}, bf16[3,96,768]{2,1,0:T(8,128)(2,1)S(1)}, u32[]{:S(2)}, u32[]{:S(2)}) %collective-permute-start.8) | collective-permute-done | bytes 442400 | tf_op jit(solution)/shard_map/ppermute | solution.py:481
  59.4 3.8 %collective-permute-done.21.refs_22_ = bf16[3,96,768]{2,1,0:T(8,128)(2,1)S(1)} collective-permute-done((bf16[3,96,768]{2,1,0:T(8,128)(2,1)S(1)}, bf16[3,96,768]{2,1,0:T(8,128)(2,1)S(1)}, u32[]{:S(2)}, u32[]{:S(2)}) %collective-permute-start.21) | collective-permute-done | bytes 442400 | tf_op jit(solution)/shard_map/ppermute | solution.py:481
  63.2 4.7 %collective-permute-done.33.refs_33_ = bf16[3,96,768]{2,1,0:T(8,128)(2,1)S(1)} collective-permute-done((bf16[3,96,768]{2,1,0:T(8,128)(2,1)S(1)}, bf16[3,96,768]{2,1,0:T(8,128)(2,1)S(1)}, u32[]{:S(2)}, u32[]{:S(2)}) %collective-permute-start.33) | collective-permute-done | bytes 442400 | tf_op jit(solution)/shard_map/ppermute | solution.py:481
  80.9 3.8 %collective-permute-done.22.refs_23_ = bf16[3,48,768]{2,1,0:T(8,128)(2,1)} collective-permute-done((bf16[3,48,768]{2,1,0:T(8,128)(2,1)S(1)}, bf16[3,48,768]{2,1,0:T(8,128)(2,1)}, u32[]{:S(2)}, u32[]{:S(2)}) %collective-permute-start.22) | collective-permute-done | bytes 221216 | tf_op jit(solution)/shard_map/ppermute | solution.py:481
  92.7 14.0 %all-gather.1 = bf16[8,1,1152]{2,1,0:T(2,128)(2,1)S(1)} all-gather(bf16[1,1,1152]{2,1,0:T(2,128)(2,1)S(1)} %reshape.127), channel_id=2, replica_groups=mesh['dp'=4,'fsdp'=8] {'fsdp'}, dimensions={0}, use_global_device_ids=true | all-gather | bytes 20736 | tf_op jit(solution)/shard_map/all_gather | solution.py:554
  110.7 15.6 %attend_forward.1 = (bf16[512,768]{1,0:T(8,128)(2,1)}, bf16[512,768]{1,0:T(8,128)(2,1)}, bf16[512,768]{1,0:T(8,128)(2,1)}, bf16[512,768]{1,0:T(8,128)(2,1)}, bf1...) custom-call(s32[4]{0:T(128)} %pad_add_fusion.me_ref, s32[1]{0:T(128)S(6)} %copy.43.len_ref, bf16[512,768]{1,0:T(8,128)(2,1)} %bitcast.86, ...), custom_call_target="tpu_custom_call" | custom-call | flops 12000000000 | bytes 20000000 | tf_op jit(solution)/shard_map/attend_forward/pallas_call | solution.py:174
  127.3 23.8 %middle_forward.1 = (bf16[512,768]{1,0:T(8,128)(2,1)}, f32[512,768]{1,0:T(8,128)}, bf16[512,768]{1,0:T(8,128)(2,1)}, bf16[3072,512]{1,0:T(8,128)(2,1)}, bf16[512...) custom-call(s32[4]{0:T(128)} %pad_add_fusion.me_ref, ...), custom_call_target="tpu_custom_call" | custom-call | flops 12000000000 | bytes 30000000 | tf_op jit(solution)/shard_map/middle_forward/pallas_call | solution.py:310
  151.1 5.0 %weight_grad_outer.2 = bf16[4,4,96,768]{3,2,1,0:T(8,128)(2,1)} custom-call(s32[4]{0:T(128)} %pad_add_fusion.me_ref, bf16[3072,512]{1,0:T(8,128)(2,1)} %get-tuple-element.72.left_ref, bf16[512,768]{1,0:T(8,128)(2,1)} %get-tuple-element.51.low_ref.g_ref), custom_call_target="tpu_custom_call" | custom-call | flops 2000000000 | bytes 6000000 | tf_op jit(solution)/shard_map/weight_grad_outer/pallas_call | solution.py:469
  156.3 20.8 %middle_backward.1 = (bf16[4,512,768]{2,1,0:T(8,128)(2,1)}, f32[512,768]{1,0:T(8,128)}, bf16[512,768]{1,0:T(8,128)(2,1)}, bf16[512,768]{1,0:T(8,128)(2,1)}, f32[4,768]{1,0:T(4,128)}, /*index=5*/f32[8,768]{1,0:T(8,128)}) custom-call(s32[4]{0:T(128)} %pad_add_fusion.me_ref, bf16[512,768]{1,0:T(8,128)(2,1)} %get-tuple-element.51.low_ref.g_ref, ...), custom_call_target="tpu_custom_call" | custom-call | flops 8999999488 | bytes 25000000 | tf_op jit(solution)/shard_map/middle_backward/pallas_call | solution.py:383
  177.1 5.0 %weight_grad_inner.2 = bf16[4,4,96,768]{3,2,1,0:T(8,128)(2,1)} custom-call(s32[4]{0:T(128)} %pad_add_fusion.me_ref, bf16[768,512]{1,0:T(8,128)(2,1)} %get-tuple-element.68.left_ref, bf16[4,512,768]{2,1,0:T(8,128)(2,1)} %get-tuple-element.69.g_ref), custom_call_target="tpu_custom_call" | custom-call | flops 2000000000 | bytes 6000000 | tf_op jit(solution)/shard_map/weight_grad_inner/pallas_call | solution.py:469
  182.4 16.2 %attend_backward.1 = (bf16[4,512,768]{2,1,0:T(8,128)(2,1)}, f32[8,768]{1,0:T(8,128)}) custom-call(s32[1]{0:T(128)S(6)} %copy.43.len_ref, bf16[512,768]{1,0:T(8,128)(2,1)} %get-tuple-element.48.q_ref, bf16[512,768]{1,0:T(8,128)(2,1)} %get-tuple-element.49.k_ref, bf16[512,768]{1,0:T(8,128)(2,1)} %get-tuple-element.50.v_ref, ...), custom_call_target="tpu_custom_call" | custom-call | flops 16000000000 | bytes 9000000 | tf_op jit(solution)/shard_map/attend_backward/pallas_call | solution.py:230
  198.7 5.2 %weight_grad_attend.2 = bf16[4,4,96,768]{3,2,1,0:T(8,128)(2,1)} custom-call(s32[4]{0:T(128)} %pad_add_fusion.me_ref, bf16[2,768,512]{2,1,0:T(8,128)(2,1)} %get-tuple-element.61.left_ref, bf16[4,512,768]{2,1,0:T(8,128)(2,1)} %get-tuple-element.59.g_ref), custom_call_target="tpu_custom_call" | custom-call | flops 2000000000 | bytes 6000000 | tf_op jit(solution)/shard_map/weight_grad_attend/pallas_call | solution.py:469
  204.0 5.3 %weight_grad_outer.3 = (bf16[2,4,96,768]{3,2,1,0:T(8,128)(2,1)}, bf16[2,4,96,768]{3,2,1,0:T(8,128)(2,1)}) custom-call(s32[4]{0:T(128)} %pad_add_fusion.me_ref, bf16[3072,512]{1,0:T(8,128)(2,1)} %get-tuple-element.72.left_ref, bf16[512,768]{1,0:T(8,128)(2,1)} %get-tuple-element.51.low_ref.g_ref, bf16[4,4,96,768]{3,2,1,0:T(8,128)(2,1)} %collective-permute-done.58.refs_0_), custom_call_target="tpu_custom_call" | custom-call | flops 2000000000 | bytes 6000000 | tf_op jit(solution)/shard_map/weight_grad_outer/pallas_call | solution.py:469
  211.6 5.5 %weight_grad_inner.3 = (bf16[2,4,96,768]{3,2,1,0:T(8,128)(2,1)}, bf16[2,4,96,768]{3,2,1,0:T(8,128)(2,1)}) custom-call(s32[4]{0:T(128)} %pad_add_fusion.me_ref, bf16[768,512]{1,0:T(8,128)(2,1)} %get-tuple-element.68.left_ref, bf16[4,512,768]{2,1,0:T(8,128)(2,1)} %get-tuple-element.69.g_ref, bf16[4,4,96,768]{3,2,1,0:T(8,128)(2,1)} %collective-permute-done.50.refs_0_), custom_call_target="tpu_custom_call" | custom-call | flops 2000000000 | bytes 6000000 | tf_op jit(solution)/shard_map/weight_grad_inner/pallas_call | solution.py:469
  218.5 5.5 %weight_grad_attend.3 = (bf16[2,4,96,768]{3,2,1,0:T(8,128)(2,1)}, bf16[2,4,96,768]{3,2,1,0:T(8,128)(2,1)}) custom-call(s32[4]{0:T(128)} %pad_add_fusion.me_ref, bf16[2,768,512]{2,1,0:T(8,128)(2,1)} %get-tuple-element.61.left_ref, bf16[4,512,768]{2,1,0:T(8,128)(2,1)} %get-tuple-element.59.g_ref, bf16[4,4,96,768]{3,2,1,0:T(8,128)(2,1)} %collective-permute-done.42.refs_0_), custom_call_target="tpu_custom_call" | custom-call | flops 2000000000 | bytes 6000000 | tf_op jit(solution)/shard_map/weight_grad_attend/pallas_call | solution.py:469
  224.2 73.3 %psum.7 = f32[8,1152]{1,0:T(8,128)} all-reduce(f32[8,1152]{1,0:T(8,128)S(1)} %pad_maximum_fusion.3), channel_id=1, replica_groups=mesh['dp'=4,'fsdp'=8] {'dp','fsdp'}, use_global_device_ids=true, to_apply=%region_0.1 | all-reduce | flops 9216 | bytes 73728 | tf_op jit(solution)/shard_map/psum | solution.py:623
  297.5 8.5 %input_grad.1 = f32[512,768]{1,0:T(8,128)} custom-call(s32[4]{0:T(128)} %pad_add_fusion.me_ref, bf16[4,512,768]{2,1,0:T(8,128)(2,1)} %get-tuple-element.59.g_ref, f32[512,768]{1,0:T(8,128)} %get-tuple-element.60.fsg_ref, bf16[96,768]{1,0:T(8,128)(2,1)} %refs_0_.7, bf16[96,768]{1,0:T(8,128)(2,1)} %refs_1_.7, bf16[96,768]{1,0:T(8,128)(2,1)} %refs_2_.7, ...), custom_call_target="tpu_custom_call" | custom-call | flops 4000000000 | bytes 10000000 | tf_op jit(solution)/shard_map/input_grad/pallas_call | solution.py:428
  314.8 7.9 %collective-permute-done.60 = bf16[4,96,768]{2,1,0:T(8,128)(2,1)S(1)} collective-permute-done((bf16[4,96,768]{2,1,0:T(8,128)(2,1)S(1)}, bf16[4,96,768]{2,1,0:T(8,128)(2,1)S(1)}, u32[]{:S(2)}, u32[]{:S(2)}) %collective-permute-start.60) | collective-permute-done | bytes 589856 | tf_op jit(solution)/shard_map/ppermute | solution.py:481
  325.4 7.7 %collective-permute-done.44 = bf16[4,96,768]{2,1,0:T(8,128)(2,1)S(1)} collective-permute-done((bf16[4,96,768]{2,1,0:T(8,128)(2,1)S(1)}, bf16[4,96,768]{2,1,0:T(8,128)(2,1)S(1)}, u32[]{:S(2)}, u32[]{:S(2)}) %collective-permute-start.44) | collective-permute-done | bytes 589856 | tf_op jit(solution)/shard_map/ppermute | solution.py:481
  337.7 8.8 %collective-permute-done.45 = bf16[2,96,768]{2,1,0:T(8,128)(2,1)S(1)} collective-permute-done((bf16[2,96,768]{2,1,0:T(8,128)(2,1)S(1)}, bf16[2,96,768]{2,1,0:T(8,128)(2,1)S(1)}, u32[]{:S(2)}, u32[]{:S(2)}) %collective-permute-start.45) | collective-permute-done | bytes 294944 | tf_op jit(solution)/shard_map/ppermute | solution.py:481
  364.4 4.6 %collective-permute-start.48 = (bf16[96,768]{1,0:T(8,128)(2,1)S(1)}, bf16[96,768]{1,0:T(8,128)(2,1)S(1)}, u32[]{:S(2)}, u32[]{:S(2)}) collective-permute-start(bf16[96,768]{1,0:T(8,128)(2,1)S(1)} %fusion.8), channel_id=1, source_target_pairs={{0,16},{8,24},{16,0},{24,8},{1,17},{9,25},{17,1},{25,9},{2,18},{10... | collective-permute-start | bytes 442376 | tf_op jit(solution)/shard_map/ppermute | solution.py:481
  372.9 3.4 collective-permute-done.49
  (262 shorter events, 106.8 us)
Async XLA Ops:
  4.9 17.2 %collective-permute-start.5 = (bf16[96,768]{1,0:T(8,128)(2,1)S(1)}, bf16[96,768]{1,0:T(8,128)(2,1)S(1)}, u32[]{:S(2)}, u32[]{:S(2)}) collective-permute-start(bf16[96,768]{1,0:T(8,128)(2,1)S(1)} %select_select_fusion.8), channel_id=1, source_target_pairs={{0,4},{1,5},{2,6},{3,7},{4,0},{5,1},{6,2},{7,3},{8,12},{9,13},{10,... | collective-permute-start | bytes 442376 | tf_op jit(solution)/shard_map/ppermute | solution.py:481
  7.4 16.8 %collective-permute-start.6 = (bf16[96,768]{1,0:T(8,128)(2,1)S(1)}, bf16[96,768]{1,0:T(8,128)(2,1)S(1)}, u32[]{:S(2)}, u32[]{:S(2)}) collective-permute-start(bf16[96,768]{1,0:T(8,128)(2,1)S(1)} %select_select_fusion.8), channel_id=1, source_target_pairs={{0,6},{1,7},{2,4},{3,5},{4,2},{5,3},{6,0},{7,1},{8,14},{9,15},{10,... | collective-permute-start | bytes 442376 | tf_op jit(solution)/shard_map/ppermute | solution.py:481
  7.5 19.4 %collective-permute-start = (bf16[96,768]{1,0:T(8,128)(2,1)}, bf16[96,768]{1,0:T(8,128)(2,1)S(1)}, u32[]{:S(2)}, u32[]{:S(2)}) collective-permute-start(bf16[96,768]{1,0:T(8,128)(2,1)} %refs_0_.7), channel_id=1, source_target_pairs={{0,1},{1,0},{2,3},{3,2},{4,5},{5,4},{6,7},{7,6},{8,9},{9,8},{10,11... | collective-permute-start | bytes 442376 | tf_op jit(solution)/shard_map/ppermute | solution.py:481
  7.5 22.5 %collective-permute-start.1 = (bf16[96,768]{1,0:T(8,128)(2,1)}, bf16[96,768]{1,0:T(8,128)(2,1)S(1)}, u32[]{:S(2)}, u32[]{:S(2)}) collective-permute-start(bf16[96,768]{1,0:T(8,128)(2,1)} %refs_1_.7), channel_id=1, source_target_pairs={{0,1},{1,0},{2,3},{3,2},{4,5},{5,4},{6,7},{7,6},{8,9},{9,8},{10,11... | collective-permute-start | bytes 442376 | tf_op jit(solution)/shard_map/ppermute | solution.py:481
  10.7 20.8 %collective-permute-start.18 = (bf16[96,768]{1,0:T(8,128)(2,1)S(1)}, bf16[96,768]{1,0:T(8,128)(2,1)S(1)}, u32[]{:S(2)}, u32[]{:S(2)}) collective-permute-start(bf16[96,768]{1,0:T(8,128)(2,1)S(1)} %constant_dynamic-slice_fusion.2), channel_id=1, source_target_pairs={{0,4},{1,5},{2,6},{3,7},{4,0},{5,1},{6,2},{7,3},{8,12},{9,13},{10,... | collective-permute-start | bytes 442376 | tf_op jit(solution)/shard_map/ppermute | solution.py:481
  24.4 23.5 %collective-permute-start.7 = (bf16[3,96,768]{2,1,0:T(8,128)(2,1)S(1)}, bf16[3,96,768]{2,1,0:T(8,128)(2,1)S(1)}, u32[]{:S(2)}, u32[]{:S(2)}) collective-permute-start(bf16[3,96,768]{2,1,0:T(8,128)(2,1)S(1)} %pad_maximum_fusion.refs_8_), channel_id=1, source_target_pairs={{0,8},{8,0},{16,24},{24,16},{1,9},{9,1},{17,25},{25,17},{2,10},{10... | collective-permute-start | bytes 1327112 | tf_op jit(solution)/shard_map/ppermute | solution.py:481
  47.9 20.0 %collective-permute-start.33 = (bf16[3,96,768]{2,1,0:T(8,128)(2,1)S(1)}, bf16[3,96,768]{2,1,0:T(8,128)(2,1)S(1)}, u32[]{:S(2)}, u32[]{:S(2)}) collective-permute-start(bf16[3,96,768]{2,1,0:T(8,128)(2,1)S(1)} %pad_maximum_fusion.2.refs_32_), channel_id=1, source_target_pairs={{0,8},{8,0},{16,24},{24,16},{1,9},{9,1},{17,25},{25,17},{2,10},{10... | collective-permute-start | bytes 1327112 | tf_op jit(solution)/shard_map/ppermute | solution.py:481
  54.8 20.2 %collective-permute-start.16 = (bf16[96,3072]{1,0:T(8,128)(2,1)S(1)}, bf16[96,3072]{1,0:T(8,128)(2,1)S(1)}, u32[]{:S(2)}, u32[]{:S(2)}) collective-permute-start(bf16[96,3072]{1,0:T(8,128)(2,1)S(1)} %copy-done.14), channel_id=1, source_target_pairs={{0,1},{1,0},{2,3},{3,2},{4,5},{5,4},{6,7},{7,6},{8,9},{9,8},{10,11... | collective-permute-start | bytes 1769480 | tf_op jit(solution)/shard_map/ppermute | solution.py:481
  54.8 20.7 %collective-permute-start.29 = (bf16[384,768]{1,0:T(8,128)(2,1)S(1)}, bf16[384,768]{1,0:T(8,128)(2,1)S(1)}, u32[]{:S(2)}, u32[]{:S(2)}) collective-permute-start(bf16[384,768]{1,0:T(8,128)(2,1)S(1)} %copy-done.15), channel_id=1, source_target_pairs={{0,1},{1,0},{2,3},{3,2},{4,5},{5,4},{6,7},{7,6},{8,9},{9,8},{10,11... | collective-permute-start | bytes 1769480 | tf_op jit(solution)/shard_map/ppermute | solution.py:481
  79.8 29.5 %collective-permute-start.12 = (bf16[3,96,768]{2,1,0:T(8,128)(2,1)S(1)}, bf16[3,96,768]{2,1,0:T(8,128)(2,1)}, u32[]{:S(2)}, u32[]{:S(2)}) collective-permute-start(bf16[3,96,768]{2,1,0:T(8,128)(2,1)S(1)} %collective-permute-done.7.refs_9_), channel_id=1, source_target_pairs={{0,1},{1,0},{2,3},{3,2},{4,5},{5,4},{6,7},{7,6},{8,9},{9,8},{10,11... | collective-permute-start | bytes 1327112 | tf_op jit(solution)/shard_map/ppermute | solution.py:481
  80.9 28.8 %collective-permute-start.13 = (bf16[3,96,768]{2,1,0:T(8,128)(2,1)S(1)}, bf16[3,96,768]{2,1,0:T(8,128)(2,1)}, u32[]{:S(2)}, u32[]{:S(2)}) collective-permute-start(bf16[3,96,768]{2,1,0:T(8,128)(2,1)S(1)} %collective-permute-done.8.refs_10_), channel_id=1, source_target_pairs={{0,1},{1,0},{2,3},{3,2},{4,5},{5,4},{6,7},{7,6},{8,9},{9,8},{10,11... | collective-permute-start | bytes 1327112 | tf_op jit(solution)/shard_map/ppermute | solution.py:481
  90.6 19.3 %collective-permute-start.27 = (bf16[3,48,768]{2,1,0:T(8,128)(2,1)}, bf16[3,48,768]{2,1,0:T(8,128)(2,1)}, u32[]{:S(2)}, u32[]{:S(2)}) collective-permute-start(bf16[3,48,768]{2,1,0:T(8,128)(2,1)} %collective-permute-done.22.refs_23_), channel_id=1, source_target_pairs={{0,1},{1,0},{2,3},{3,2},{4,5},{5,4},{6,7},{7,6},{8,9},{9,8},{10,11... | collective-permute-start | bytes 663560 | tf_op jit(solution)/shard_map/ppermute | solution.py:481
  90.7 19.5 %collective-permute-start.28 = (bf16[3,48,768]{2,1,0:T(8,128)(2,1)}, bf16[3,48,768]{2,1,0:T(8,128)(2,1)}, u32[]{:S(2)}, u32[]{:S(2)}) collective-permute-start(bf16[3,48,768]{2,1,0:T(8,128)(2,1)} %collective-permute-done.23.refs_24_), channel_id=1, source_target_pairs={{0,1},{1,0},{2,3},{3,2},{4,5},{5,4},{6,7},{7,6},{8,9},{9,8},{10,11... | collective-permute-start | bytes 663560 | tf_op jit(solution)/shard_map/ppermute | solution.py:481
  92.1 18.3 %collective-permute-start.40 = (bf16[3,48,768]{2,1,0:T(8,128)(2,1)}, bf16[3,48,768]{2,1,0:T(8,128)(2,1)}, u32[]{:S(2)}, u32[]{:S(2)}) collective-permute-start(bf16[3,48,768]{2,1,0:T(8,128)(2,1)} %collective-permute-done.35.refs_35_), channel_id=1, source_target_pairs={{0,1},{1,0},{2,3},{3,2},{4,5},{5,4},{6,7},{7,6},{8,9},{9,8},{10,11... | collective-permute-start | bytes 663560 | tf_op jit(solution)/shard_map/ppermute | solution.py:481
  109.3 17.0 %collective-permute-start.25 = (bf16[3,96,768]{2,1,0:T(8,128)(2,1)S(1)}, bf16[3,96,768]{2,1,0:T(8,128)(2,1)S(1)}, u32[]{:S(2)}, u32[]{:S(2)}) collective-permute-start(bf16[3,96,768]{2,1,0:T(8,128)(2,1)S(1)} %collective-permute-done.20.refs_21_), channel_id=1, source_target_pairs={{0,1},{1,0},{2,3},{3,2},{4,5},{5,4},{6,7},{7,6},{8,9},{9,8},{10,11... | collective-permute-start | bytes 1327112 | tf_op jit(solution)/shard_map/ppermute | solution.py:481
  109.7 16.7 %collective-permute-start.26 = (bf16[3,96,768]{2,1,0:T(8,128)(2,1)S(1)}, bf16[3,96,768]{2,1,0:T(8,128)(2,1)S(1)}, u32[]{:S(2)}, u32[]{:S(2)}) collective-permute-start(bf16[3,96,768]{2,1,0:T(8,128)(2,1)S(1)} %collective-permute-done.21.refs_22_), channel_id=1, source_target_pairs={{0,1},{1,0},{2,3},{3,2},{4,5},{5,4},{6,7},{7,6},{8,9},{9,8},{10,11... | collective-permute-start | bytes 1327112 | tf_op jit(solution)/shard_map/ppermute | solution.py:481
  156.1 47.9 %collective-permute-start.58 = (bf16[4,4,96,768]{3,2,1,0:T(8,128)(2,1)}, bf16[4,4,96,768]{3,2,1,0:T(8,128)(2,1)}, u32[]{:S(2)}, u32[]{:S(2)}) collective-permute-start(bf16[4,4,96,768]{3,2,1,0:T(8,128)(2,1)} %weight_grad_outer.2), channel_id=1, source_target_pairs={{0,1},{1,0},{2,3},{3,2},{4,5},{5,4},{6,7},{7,6},{8,9},{9,8},{10,11... | collective-permute-start | bytes 7077896 | tf_op jit(solution)/shard_map/ppermute | solution.py:481
  182.1 29.5 %collective-permute-start.50 = (bf16[4,4,96,768]{3,2,1,0:T(8,128)(2,1)}, bf16[4,4,96,768]{3,2,1,0:T(8,128)(2,1)}, u32[]{:S(2)}, u32[]{:S(2)}) collective-permute-start(bf16[4,4,96,768]{3,2,1,0:T(8,128)(2,1)} %weight_grad_inner.2), channel_id=1, source_target_pairs={{0,1},{1,0},{2,3},{3,2},{4,5},{5,4},{6,7},{7,6},{8,9},{9,8},{10,11... | collective-permute-start | bytes 7077896 | tf_op jit(solution)/shard_map/ppermute | solution.py:481
  209.3 96.7 %collective-permute-start.59 = (bf16[2,4,96,768]{3,2,1,0:T(8,128)(2,1)}, bf16[2,4,96,768]{3,2,1,0:T(8,128)(2,1)S(1)}, u32[]{:S(2)}, u32[]{:S(2)}) collective-permute-start(bf16[2,4,96,768]{3,2,1,0:T(8,128)(2,1)} %get-tuple-element.74), channel_id=1, source_target_pairs={{0,8},{8,0},{16,24},{24,16},{1,9},{9,1},{17,25},{25,17},{2,10},{10... | collective-permute-start | bytes 3538952 | tf_op jit(solution)/shard_map/ppermute | solution.py:481
  217.0 91.5 %collective-permute-start.51 = (bf16[2,4,96,768]{3,2,1,0:T(8,128)(2,1)}, bf16[2,4,96,768]{3,2,1,0:T(8,128)(2,1)S(1)}, u32[]{:S(2)}, u32[]{:S(2)}) collective-permute-start(bf16[2,4,96,768]{3,2,1,0:T(8,128)(2,1)} %get-tuple-element.71), channel_id=1, source_target_pairs={{0,16},{8,24},{16,0},{24,8},{1,17},{9,25},{17,1},{25,9},{2,18},{10... | collective-permute-start | bytes 3538952 | tf_op jit(solution)/shard_map/ppermute | solution.py:481
  224.0 85.7 %collective-permute-start.43 = (bf16[2,4,96,768]{3,2,1,0:T(8,128)(2,1)}, bf16[2,4,96,768]{3,2,1,0:T(8,128)(2,1)}, u32[]{:S(2)}, u32[]{:S(2)}) collective-permute-start(bf16[2,4,96,768]{3,2,1,0:T(8,128)(2,1)} %get-tuple-element.63), channel_id=1, source_target_pairs={{0,8},{8,0},{16,24},{24,16},{1,9},{9,1},{17,25},{25,17},{2,10},{10... | collective-permute-start | bytes 3538952 | tf_op jit(solution)/shard_map/ppermute | solution.py:481
  310.9 22.2 %collective-permute-start.44 = (bf16[4,96,768]{2,1,0:T(8,128)(2,1)S(1)}, bf16[4,96,768]{2,1,0:T(8,128)(2,1)S(1)}, u32[]{:S(2)}, u32[]{:S(2)}) collective-permute-start(bf16[4,96,768]{2,1,0:T(8,128)(2,1)S(1)} %fusion.3), channel_id=1, source_target_pairs={{0,16},{8,24},{16,0},{24,8},{1,17},{9,25},{17,1},{25,9},{2,18},{10... | collective-permute-start | bytes 1769480 | tf_op jit(solution)/shard_map/ppermute | solution.py:481
  346.7 23.5 %collective-permute-start.63 = (bf16[96,768]{1,0:T(8,128)(2,1)S(1)}, bf16[96,768]{1,0:T(8,128)(2,1)S(1)}, u32[]{:S(2)}, u32[]{:S(2)}) collective-permute-start(bf16[96,768]{1,0:T(8,128)(2,1)S(1)} %fusion.6), channel_id=1, source_target_pairs={{0,8},{8,0},{16,24},{24,16},{1,9},{9,1},{17,25},{25,17},{2,10},{10... | collective-permute-start | bytes 442376 | tf_op jit(solution)/shard_map/ppermute | solution.py:481
  347.7 24.0 %collective-permute-start.64 = (bf16[96,768]{1,0:T(8,128)(2,1)S(1)}, bf16[96,768]{1,0:T(8,128)(2,1)S(1)}, u32[]{:S(2)}, u32[]{:S(2)}) collective-permute-start(bf16[96,768]{1,0:T(8,128)(2,1)S(1)} %fusion.6), channel_id=1, source_target_pairs={{0,16},{8,24},{16,0},{24,8},{1,17},{9,25},{17,1},{25,9},{2,18},{10... | collective-permute-start | bytes 442376 | tf_op jit(solution)/shard_map/ppermute | solution.py:481
  (86 other events, 1380.0 us)

commit v2 on v1

v2 whole, which is shorter than its diff:
```python
import functools
import math

import jax
import jax.numpy as jnp
from jax import lax
from jax.experimental import pallas as pl
from jax.experimental.pallas import tpu as pltpu
from jax.sharding import PartitionSpec as P

F32 = jnp.float32
BF16 = jnp.bfloat16
HD = 64
MASKED = -1e30
SCALE = HD ** -0.5
EPSILON = 1e-12
ROOT_HALF = math.sqrt(0.5)
INV_ROOT_TWO_PI = 1.0 / math.sqrt(2.0 * math.pi)

VM = pl.BlockSpec(memory_space=pltpu.VMEM)
SM = pl.BlockSpec(memory_space=pltpu.SMEM)
HB = pl.BlockSpec(memory_space=pl.ANY)


def shape(*dims, dtype=BF16):
    return jax.ShapeDtypeStruct(dims, dtype)


def local(*dims, dtype=BF16):
    return pltpu.VMEM(dims, dtype)


def stay(*values):
    return tuple(pltpu.with_memory_space_constraint(v, pltpu.VMEM) for v in values)


def far_off(*values):
    return tuple(pltpu.with_memory_space_constraint(v, pltpu.HBM) for v in values)


def limit(mebibytes):
    return pltpu.CompilerParams(vmem_limit_bytes=mebibytes << 20)


def dot_nn(a, b):
    return lax.dot_general(a, b, (((1,), (0,)), ((), ())), preferred_element_type=F32)


def dot_nt(a, b):
    return lax.dot_general(a, b, (((1,), (1,)), ((), ())), preferred_element_type=F32)


def flip(value):
    return value.astype(F32).T.astype(BF16)


def column_sum(value):
    return jnp.sum(value.astype(F32), axis=0, keepdims=True)


def row_mean(value):
    return jnp.mean(value, axis=-1, keepdims=True)


def aligned(start, size):
    return pl.ds(pl.multiple_of(start, size), size)


class Pieces:
    def __init__(self, held, arrays, own, sibling, far, far_sibling, stacked, packs=()):
        self.held, self.arrays, self.own, self.sibling, self.packs = held, arrays, own, sibling, packs
        self.far, self.far_sibling, self.stacked = far, far_sibling, stacked

    def count(self):
        return len(self.own)

    def place(self, target, block, z_at, c_at, offset, rows):
        if self.stacked:
            return target.at[block, aligned_rows((2 * z_at + c_at) * 96 + offset, rows), :]
        return target.at[aligned_rows((2 * z_at + c_at) * 384 + block * 96 + offset, rows), :]

    def copies(self, held, me_ref, target, sems, base):
        z, c = me_ref[1], me_ref[2]
        done = []
        for block, (position, row, lane) in enumerate(self.own):
            where = self.place(target, block, z, c, 0, 96)
            source = held[position].at[pl.ds(row, 96), pl.ds(lane, 768)]
            done.append(pltpu.make_async_copy(source, where, sems.at[base + block]))
        return done

    def fill(self, refs, me_ref, target):
        i, z, c = me_ref[0], me_ref[1], me_ref[2]
        for block, (position, row, lane) in enumerate(self.sibling):
            self.place(target, block, z, 1 - c, 0, 96)[...] = refs[position][row : row + 96, lane : lane + 768]
        for c_at, far in ((c, self.far), (1 - c, self.far_sibling)):
            for away, parts in enumerate(far):
                for position, row, rows, offset in parts:
                    for j in range(1, 4):
                        where = self.place(target, i ^ away, z ^ j, c_at, offset, rows)
                        where[...] = refs[position][j - 1, row : row + rows, :]

    def vectors(self, refs, me_ref, target):
        z, c = me_ref[1], me_ref[2]
        for c_at, spot, far in ((c, self.packs[0], self.far), (1 - c, self.packs[1], self.far_sibling)):
            target[2 * z + c_at] = refs[spot][96:104, :].astype(F32)
            for j in range(1, 4):
                target[2 * (z ^ j) + c_at] = refs[far[0][0][0]][j - 1, 96:104, :].astype(F32)


def aligned_rows(start, rows):
    return pl.ds(pl.multiple_of(start, 16), rows)


class Whole:
    def __init__(self, held, arrays, spots, stacked):
        self.held, self.arrays, self.spots, self.stacked = held, arrays, spots, stacked

    def count(self):
        return len(self.spots)

    def copies(self, held, me_ref, target, sems, base):
        done = []
        for block, (position, row, lane) in enumerate(self.spots):
            where = target.at[block] if self.stacked else target.at[pl.ds(block * 768, 768), :]
            source = held[position].at[pl.ds(row, 768), pl.ds(lane, 768)]
            done.append(pltpu.make_async_copy(source, where, sems.at[base + block]))
        return done

    def fill(self, refs, me_ref, target):
        pass

    def vectors(self, refs, me_ref, target):
        target[...] = refs[0][...].astype(F32)


def start_all(copies):
    for copy in copies:
        copy.start()


def wait_all(copies):
    for copy in copies:
        copy.wait()


def pair_masks(dims, axis):
    spot = lax.broadcasted_iota(jnp.int32, dims, axis)
    return spot < HD, spot >= HD


def keep(mask, value):
    return jnp.where(mask, value, jnp.zeros_like(value))


def attend_forward_body(group, part, me_ref, len_ref, x_ref, *refs):
    held, refs = refs[: len(group.held)], refs[len(group.held) :]
    sources = refs[: len(group.arrays)]
    q_ref, k_ref, v_ref, att_ref, left_ref, lse_ref, w_ref, vec_ref, ib_ref, packed, sems = refs[len(group.arrays) :]
    seq, width = x_ref.shape
    tile = min(256, seq)
    loads = group.copies(held, me_ref, w_ref, sems, 0)
    start_all(loads)
    group.fill(sources, me_ref, w_ref)
    group.vectors(sources, me_ref, packed)
    for f in range(packed.shape[0]):
        pack = packed[f]
        vec_ref[:, f * part : (f + 1) * part] = pack[:, :part]
        row, lane = divmod(f * 4 * part, width)
        ib_ref[row : row + 1, lane : lane + 4 * part] = pack[:1, 128 : 128 + 4 * part]
    for p in range(width // 128):
        left_ref[0, p * 128 : (p + 1) * 128, :] = flip(x_ref[:, p * 128 : (p + 1) * 128])
    wait_all(loads)

    def project(r, carry):
        rows = aligned(r * tile, tile)
        x = x_ref[rows, :]
        q_ref[rows, :] = (dot_nn(x, w_ref[0]) + vec_ref[0:1, :]).astype(BF16)
        k_ref[rows, :] = dot_nn(x, w_ref[1]).astype(BF16)
        v_ref[rows, :] = (dot_nn(x, w_ref[2]) + vec_ref[1:2, :]).astype(BF16)
        return carry

    lax.fori_loop(0, seq // tile, project, 0)
    length = len_ref[0]

    def pair(p, carry):
        lanes = aligned(p * 128, 128)
        k_pair = k_ref[:, lanes]
        q_t = (q_ref[:, lanes].astype(F32) * SCALE).T.astype(BF16)
        v_t = flip(v_ref[:, lanes])
        masks = pair_masks((128, seq), 0)
        allowed = lax.broadcasted_iota(jnp.int32, (seq, seq), 0) < length
        for e in range(2):
            s = dot_nn(k_pair, keep(masks[e], q_t))
            s = jnp.where(allowed, s, MASKED)
            top = jnp.max(s, axis=0, keepdims=True)
            p_t = jnp.exp(s - top)
            total = jnp.sum(p_t, axis=0, keepdims=True)
            o_t = dot_nn(v_t[e * HD : (e + 1) * HD, :], p_t.astype(BF16)) / total
            left_ref[1, aligned(p * 128 + e * HD, HD), :] = o_t.astype(BF16)
            lse_ref[pl.ds(p * 2 + e, 1), :] = top + jnp.log(total)
        att_ref[:, lanes] = flip(left_ref[1, aligned(p * 128, 128), :])
        return carry

    lax.fori_loop(0, width // 128, pair, 0)


def attend_forward(group, shards, blocks, me, length, x):
    seq, width = x.shape
    heads = width // HD
    return pl.pallas_call(
        functools.partial(attend_forward_body, group, width // shards),
        out_shape=(local(seq, width),) * 4
        + (local(2, width, seq), local(-(-heads // 8) * 8, seq, dtype=F32), local(4, width, width))
        + (local(8, width, dtype=F32), local(blocks, width, dtype=F32)),
        in_specs=[SM, SM, VM] + [HB] * len(group.held) + [VM] * len(group.arrays),
        out_specs=[VM] * 9,
        scratch_shapes=[pltpu.VMEM((shards, 8, width), F32), pltpu.SemaphoreType.DMA((group.count(),))],
        compiler_params=limit(10),
        cost_estimate=pl.CostEstimate(flops=12_000_000_000, bytes_accessed=20_000_000, transcendentals=3_200_000),
        name="attend_forward",
    )(me, length, x, *far_off(*group.held), *stay(*group.arrays))


def attend_backward_body(first, last, len_ref, q_ref, k_ref, v_ref, do_ref, lse_ref, branch_ref, *refs):
    g_ref, sum_ref = refs[-2:]
    seq, width = q_ref.shape
    length = len_ref[0]

    def pair(p, carry):
        lanes = aligned(p * 128, 128)
        q_pair = (q_ref[:, lanes].astype(F32) * SCALE).astype(BF16)
        k_pair = k_ref[:, lanes]
        v_pair = v_ref[:, lanes]
        do_pair = do_ref[:, lanes]
        q_t = flip(q_pair)
        k_t = (k_pair.astype(F32) * SCALE).T.astype(BF16)
        do_t = flip(do_pair)
        sub_masks = pair_masks((128, seq), 0)
        lane_masks = pair_masks((seq, 128), 1)
        allowed = lax.broadcasted_iota(jnp.int32, (seq, seq), 0) < length
        dk = jnp.zeros((seq, 128), F32)
        dv = jnp.zeros((seq, 128), F32)
        dq_t = []
        for e in range(2):
            s = dot_nn(k_pair, keep(sub_masks[e], q_t))
            s = jnp.where(allowed, s, MASKED)
            p_t = jnp.exp(s - lse_ref[pl.ds(p * 2 + e, 1), :])
            dp = dot_nn(v_pair, keep(sub_masks[e], do_t))
            dv = dv + dot_nn(p_t.astype(BF16), keep(lane_masks[e], do_pair))
            t = p_t * dp
            row = jnp.sum(t, axis=0, keepdims=True)
            ds = (t - p_t * row).astype(BF16)
            dk = dk + dot_nn(ds, keep(lane_masks[e], q_pair))
            dq_t.append(dot_nn(k_t[e * HD : (e + 1) * HD, :], ds))
        dq = jnp.concatenate(dq_t, axis=0).T.astype(BF16)
        dv = dv.astype(BF16)
        g_ref[0, :, lanes] = dq
        g_ref[1, :, lanes] = dk.astype(BF16)
        g_ref[2, :, lanes] = dv
        g_ref[3, :, lanes] = branch_ref[:, lanes]
        sum_ref[0:1, lanes] = column_sum(dq)
        sum_ref[1:2, lanes] = column_sum(dv)
        return carry

    lax.fori_loop(first, last, pair, 0)


def attend_backward(first, last, length, q, k, v, do, lse, branch, before=()):
    seq, width = q.shape
    return pl.pallas_call(
        functools.partial(attend_backward_body, first, last),
        out_shape=(local(4, seq, width), local(8, width, dtype=F32)),
        in_specs=[SM] + [VM] * 6 + [HB] * len(before),
        out_specs=[VM] * 2,
        input_output_aliases={7 + n: n for n in range(len(before))},
        compiler_params=limit(10),
        cost_estimate=pl.CostEstimate(flops=16_000_000_000, bytes_accessed=9_000_000, transcendentals=3_200_000),
        name="attend_backward",
    )(length, *stay(q, k, v, do, lse, branch, *before))


def gelu_parts(inner):
    cumulative = 0.5 * (1.0 + lax.erf(inner * ROOT_HALF))
    density = jnp.exp(-0.5 * inner * inner) * INV_ROOT_TWO_PI
    return inner * cumulative, cumulative + inner * density


def fill_body(groups, me_ref, *refs):
    sources = []
    for n, group in enumerate(groups):
        sources.append((refs[: len(group.held)], refs[len(group.held) : len(group.held) + len(group.arrays)]))
        refs = refs[len(group.held) + len(group.arrays) :]
    wi, wu, sems = refs
    loads, base = [], 0
    for group, (held, _), target in zip(groups, sources, (wi, wu), strict=True):
        loads += group.copies(held, me_ref, target, sems, base)
        base += group.count()
    start_all(loads)
    for group, (_, near), target in zip(groups, sources, (wi, wu), strict=True):
        group.fill(near, me_ref, target)
    wait_all(loads)


def fill(groups, me, width, blocks):
    operands, specs = [], []
    for g in groups:
        operands += [*far_off(*g.held), *stay(*g.arrays)]
        specs += [HB] * len(g.held) + [VM] * len(g.arrays)
    return pl.pallas_call(
        functools.partial(fill_body, groups),
        out_shape=(local(blocks, width, width), local(blocks * width, width)),
        in_specs=[SM] + specs,
        out_specs=[VM] * 2,
        scratch_shapes=[pltpu.SemaphoreType.DMA((sum(g.count() for g in groups),))],
        compiler_params=limit(2),
        cost_estimate=pl.CostEstimate(flops=0, bytes_accessed=9_000_000, transcendentals=0),
        name="fill",
    )(me, *operands)


def middle_forward_body(
    len_ref,
    x_ref,
    att_ref,
    cot_ref,
    vec_ref,
    ib_ref,
    wa,
    wi,
    wu,
    out_ref,
    ssg_ref,
    low_ref,
    actT_ref,
    slope_ref,
    norm_ref,
    rstd_ref,
    hidT_ref,
    sum_ref,
):
    seq, width = x_ref.shape
    blocks = wi.shape[0]
    tile = min(256, seq)
    length = len_ref[0]
    sum_ref[...] = jnp.zeros_like(sum_ref)

    def rows_step(r, carry):
        rows = aligned(r * tile, tile)
        first = x_ref[rows, :].astype(F32) + dot_nn(att_ref[rows, :], wa[3]) + vec_ref[2:3, :]
        center = first - row_mean(first)
        rstd = lax.rsqrt(row_mean(center * center) + EPSILON)
        normed = center * rstd
        norm_ref[rows, :] = normed
        rstd_ref[rows, :] = rstd
        hidden = normed * vec_ref[3:4, :] + vec_ref[4:5, :]
        low = hidden.astype(BF16)
        hidT_ref[:, rows] = low.astype(F32).T.astype(BF16)

        def block(f, second):
            inner = dot_nn(low, wi[f]) + ib_ref[pl.ds(f, 1), :]
            active, slope = gelu_parts(inner)
            active = active.astype(BF16)
            spot = aligned(f * width, width)
            slope_ref[rows, spot] = slope.astype(BF16)
            actT_ref[spot, rows] = flip(active)
            return second + dot_nn(active, wu[spot, :])

        second = lax.fori_loop(0, blocks, block, hidden + vec_ref[5:6, :])
        center = second - row_mean(second)
        rstd = lax.rsqrt(row_mean(center * center) + EPSILON)
        normed = center * rstd
        spot = r * tile + lax.broadcasted_iota(jnp.int32, (tile, width), 0)
        valid = spot < length
        result = normed * vec_ref[6:7, :] + vec_ref[7:8, :]
        out_ref[rows, :] = jnp.where(valid, result, 0.0).astype(BF16)
        grad = jnp.where(valid, cot_ref[rows, :].astype(F32), 0.0)
        sum_ref[7:8, :] += column_sum(grad)
        sum_ref[6:7, :] += column_sum(grad * normed)
        grad = grad * vec_ref[6:7, :]
        grad = rstd * (grad - row_mean(grad) - normed * row_mean(grad * normed))
        ssg_ref[rows, :] = grad
        low = grad.astype(BF16)
        low_ref[rows, :] = low
        sum_ref[5:6, :] += column_sum(low)
        return carry

    lax.fori_loop(0, seq // tile, rows_step, 0)


def middle_forward(length, x, att, cot, vec, ib, wa, wi, wu):
    seq, width = x.shape
    blocks = ib.shape[0]
    return pl.pallas_call(
        middle_forward_body,
        out_shape=(
            shape(seq, width),
            local(seq, width, dtype=F32),
            local(seq, width),
            local(blocks * width, seq),
            local(seq, blocks * width),
            local(seq, width, dtype=F32),
            local(seq, 1, dtype=F32),
            local(width, seq),
            local(8, width, dtype=F32),
        ),
        in_specs=[SM] + [VM] * 8,
        out_specs=[VM] * 9,
        compiler_params=limit(12),
        cost_estimate=pl.CostEstimate(flops=12_000_000_000, bytes_accessed=30_000_000, transcendentals=3_200_000),
        name="middle_forward",
    )(length, x, *stay(att), cot, *stay(vec, ib, wa, wi, wu))


def middle_backward_body(
    low_ref, ssg_ref, slope_ref, norm_ref, rstd_ref, vec_ref, wa, wi, wu, igl_ref, fsg_ref, branch_ref, att_ref, ib_ref, sum_ref
):
    seq, width = low_ref.shape
    blocks = wi.shape[0]
    tile = min(256, seq)
    sum_ref[...] = jnp.zeros_like(sum_ref)
    ib_ref[...] = jnp.zeros_like(ib_ref)

    def rows_step(r, carry):
        rows = aligned(r * tile, tile)
        low = low_ref[rows, :]

        def block(f, grad):
            spot = aligned(f * width, width)
            inner = (dot_nt(low, wu[spot, :]) * slope_ref[rows, spot].astype(F32)).astype(BF16)
            igl_ref[f, rows, :] = inner
            ib_ref[pl.ds(f, 1), :] += column_sum(inner)
            return grad + dot_nt(inner, wi[f])

        grad = lax.fori_loop(0, blocks, block, ssg_ref[rows, :])
        normed = norm_ref[rows, :]
        sum_ref[4:5, :] += column_sum(grad)
        sum_ref[3:4, :] += column_sum(grad * normed)
        grad = grad * vec_ref[3:4, :]
        grad = rstd_ref[rows, :] * (grad - row_mean(grad) - normed * row_mean(grad * normed))
        fsg_ref[rows, :] = grad
        branch = grad.astype(BF16)
        branch_ref[rows, :] = branch
        sum_ref[2:3, :] += column_sum(branch)
        att_ref[rows, :] = dot_nt(branch, wa[3]).astype(BF16)
        return carry

    lax.fori_loop(0, seq // tile, rows_step, 0)


def middle_backward(low, ssg, slope, norm, rstd, vec, wa, wi, wu):
    seq, width = low.shape
    blocks = wi.shape[0]
    return pl.pallas_call(
        middle_backward_body,
        out_shape=(
            local(blocks, seq, width),
            local(seq, width, dtype=F32),
            local(seq, width),
            local(seq, width),
            local(blocks, width, dtype=F32),
            local(8, width, dtype=F32),
        ),
        in_specs=[VM] * 9,
        out_specs=[VM] * 6,
        compiler_params=limit(10),
        cost_estimate=pl.CostEstimate(flops=9_000_000_000, bytes_accessed=25_000_000, transcendentals=0),
        name="middle_backward",
    )(*stay(low, ssg, slope, norm, rstd, vec, wa, wi, wu))


def input_grad_body(g_ref, fsg_ref, w_ref, out_ref):
    seq, width = fsg_ref.shape
    tile = min(256, seq)

    def rows_step(r, carry):
        rows = aligned(r * tile, tile)
        total = fsg_ref[rows, :]
        for n in range(3):
            total = total + dot_nt(g_ref[n, rows, :], w_ref[n])
        out_ref[rows, :] = total
        return carry

    lax.fori_loop(0, seq // tile, rows_step, 0)


def input_grad(g, fsg, wa):
    seq, width = fsg.shape
    return pl.pallas_call(
        input_grad_body,
        out_shape=shape(seq, width, dtype=F32),
        in_specs=[VM] * 3,
        out_specs=VM,
        compiler_params=limit(8),
        cost_estimate=pl.CostEstimate(flops=4_000_000_000, bytes_accessed=10_000_000, transcendentals=0),
        name="input_grad",
    )(*stay(g, fsg, wa))


Z_ORDER = (0, 2, 1, 3)


def weight_grad_body(kind, order, z_order, me_ref, left_ref, g_ref, *refs):
    sums, refs = (refs[:4], refs[4:]) if kind == "attend" else ((), refs)
    outs, left = refs[:2], refs[2]
    i, z, c = me_ref[0], me_ref[1], me_ref[2]
    part = 96
    if kind == "attend":
        extra = refs[3]
        one, two, three, ib = (r[...] for r in sums)
        row = lax.broadcasted_iota(jnp.int32, one.shape, 0)
        every = jnp.where(row < 2, three, jnp.where(row < 5, two, one))
        for f in range(8):
            extra[f] = jnp.zeros_like(extra[f])
            extra[f, :, :part] = every[:, f * part : (f + 1) * part]
            extra[f, 0:1, 128 : 128 + 4 * part] = ib[f // 2 : f // 2 + 1, f % 2 * 4 * part : (f % 2 + 1) * 4 * part]

    for c_at, out_ref in zip((1 - c, c), outs, strict=True):

        def block_step(spot, carry):
            block = i ^ pick(order, spot)
            for n, j in enumerate(z_order):
                f_at = 2 * (z ^ j) + c_at
                if kind == "outer":
                    rows = left_ref[aligned_rows(f_at * 384 + block * 96, 96), :]
                elif kind == "inner":
                    rows = left_ref[aligned_rows(f_at * 96, 96), :]
                else:
                    rows = left_ref[block // 3, aligned_rows(f_at * 96, 96), :]
                left[n * 96 : (n + 1) * 96, :] = rows
            right = g_ref[...] if kind == "outer" else g_ref[block]
            out_ref[spot, :, :96, :] = dot_nn(left[...], right).reshape(4, 96, 768).astype(BF16)
            if kind == "attend":
                for n, j in enumerate(z_order):
                    out_ref[spot, n, 96:104, :] = extra[2 * (z ^ j) + c_at].astype(BF16)
            return carry

        lax.fori_loop(0, 4, block_step, 0)


def weight_grad(kind, order, z_order, me, left, g, sums=()):
    rows = 104 if kind == "attend" else 96
    return pl.pallas_call(
        functools.partial(weight_grad_body, kind, order, z_order),
        out_shape=(local(4, 4, rows, 768),) * 2,
        in_specs=[SM] + [VM] * (2 + len(sums)),
        out_specs=[VM] * 2,
        scratch_shapes=[pltpu.VMEM((384, left.shape[-1]), BF16)] + [pltpu.VMEM((8, 8, 768), F32)] * (kind == "attend"),
        compiler_params=limit(6),
        cost_estimate=pl.CostEstimate(flops=4_000_000_000, bytes_accessed=6_000_000, transcendentals=0),
        name=f"weight_grad_{kind}",
    )(me, *stay(left, g, *sums))


def prepare_body(me_ref, *refs):
    vectors, weights = refs[:9], refs[9:15]
    first_ref, second_ref, pack_ref, *rows, sems = refs[15:]
    i = me_ref[0]
    part = vectors[0].shape[0]
    copies = [
        pltpu.make_async_copy(
            weights[4].at[:, pl.ds(pl.multiple_of(i * 768, 768), 768)], second_ref.at[pl.ds(0, 96), :], sems.at[0]
        ),
        pltpu.make_async_copy(weights[5].at[aligned_rows(i * 96, 96), :], second_ref.at[pl.ds(96, 96), :], sems.at[1]),
    ]
    for n in range(9):
        copies.append(pltpu.make_async_copy(vectors[n], rows[n], sems.at[3 + n]))
    for n in range(4):

        @pl.when(i == n)
        def _():
            pltpu.make_async_copy(weights[n], first_ref.at[pl.ds(0, 96), :], sems.at[2]).start()

    start_all(copies)
    pack_ref[...] = jnp.zeros_like(pack_ref)
    wait_all(copies[2:])
    for n in range(8):
        pack_ref[n : n + 1, :part] = rows[n][...].astype(F32).reshape(1, part)
    pack_ref[0:1, 128 : 128 + 4 * part] = rows[8][...].astype(F32).reshape(1, 4 * part)
    first_ref[96:104, :] = pack_ref[...].astype(BF16)
    pltpu.make_async_copy(weights[0], first_ref.at[pl.ds(0, 96), :], sems.at[2]).wait()
    wait_all(copies[:2])


def prepare(me, vectors, weights):
    return pl.pallas_call(
        prepare_body,
        out_shape=(local(104, 768), local(192, 768)),
        in_specs=[SM] + [HB] * 15,
        out_specs=[VM] * 2,
        scratch_shapes=[pltpu.VMEM((8, 768), F32)]
        + [pltpu.VMEM(v.shape, BF16) for v in vectors]
        + [pltpu.SemaphoreType.DMA((12,))],
        compiler_params=limit(2),
        cost_estimate=pl.CostEstimate(flops=0, bytes_accessed=1_000_000, transcendentals=0),
        name="prepare",
    )(me, *far_off(*vectors, *weights))


def after(value, *others):
    def body(*refs):
        pass

    return pl.pallas_call(
        body,
        out_shape=jax.ShapeDtypeStruct(value.shape, value.dtype),
        in_specs=[HB] * (1 + len(others)),
        out_specs=HB,
        input_output_aliases={0: 0},
        compiler_params=limit(1),
        cost_estimate=pl.CostEstimate(flops=0, bytes_accessed=0, transcendentals=0),
        name="after",
    )(value, *others)


def swap(value, axis, size, mask):
    return lax.ppermute(value, axis, [(n, n ^ mask) for n in range(size)])


def gather_z(piece, fsdp):
    return [swap(piece, "fsdp", fsdp, 2 * j) for j in (1, 2, 3)]


def gather_plane(mine, dp):
    over_x = swap(mine, "dp", dp, 1)
    over_y = swap(mine, "dp", dp, 2)
    return over_x, over_y


def total(*terms):
    result = terms[0].astype(F32)
    for term in terms[1:]:
        result = result + term.astype(F32)
    return result.astype(BF16)


def scatter_z(value, fsdp):
    got = swap(value[2:], "fsdp", fsdp, 2)
    onward = swap(total(value[1], got[1]), "fsdp", fsdp, 4)
    return total(value[0], got[0], onward)


def direct_z(value, fsdp):
    return total(value[0], *[swap(value[j], "fsdp", fsdp, 2 * j) for j in (1, 2, 3)])


def spread(value, dp):
    return (value,) + tuple(swap(value, "dp", dp, m) for m in (1, 2, 3))


def pick(pieces, index):
    return jnp.where(index == 0, pieces[0], jnp.where(index == 1, pieces[1], jnp.where(index == 2, pieces[2], pieces[3])))


def in_order(pieces, i):
    return [pick(pieces, n ^ i) for n in range(4)]


def on_device(
    sizes,
    tokens,
    lengths,
    cotangent,
    query_weight,
    query_bias,
    key_weight,
    value_weight,
    value_bias,
    output_weight,
    output_bias,
    first_gain,
    first_shift,
    inner_weight,
    inner_bias,
    outer_weight,
    outer_bias,
    second_gain,
    second_shift,
):
    dp, fsdp = sizes
    docs, seq, width = tokens.shape
    blocks = inner_weight.shape[1] // width
    direct = dp == 4 and fsdp == 8 and docs == 1 and query_weight.shape == (96, 768) and blocks == 4
    i = lax.axis_index("dp")
    f = lax.axis_index("fsdp")
    me = jnp.stack([i, f // 2, f % 2, jnp.zeros_like(i)]).astype(jnp.int32)

    small = (query_bias, value_bias, output_bias, first_gain, first_shift, outer_bias, second_gain, second_shift, inner_bias)
    part = query_bias.shape[0]

    if direct:
        mine = (query_weight, key_weight, value_weight, output_weight)
        piece_a, piece_m = prepare(me, small, mine + (inner_weight, outer_weight))
        z_a = gather_z(piece_a, fsdp)
        theirs = tuple(swap(w, "fsdp", fsdp, 1) for w in mine + (piece_a,))
        mine_a = jnp.stack(z_a)
        plane_a = gather_plane(mine_a, dp)
        z_m = gather_z(after(piece_m, mine_a), fsdp)
        parts_a = (plane_a[0][:, :48], plane_a[1][:, 48:96])
        rest_a = (swap(parts_a[0], "dp", dp, 2), swap(parts_a[1], "dp", dp, 1))
        near_a = (mine_a,) + plane_a + rest_a
        far_a = tuple(swap(w, "fsdp", fsdp, 1) for w in near_a)
        z_m[0] = after(z_m[0], *parts_a)
        mine_m = jnp.stack(z_m)
        plane_m = gather_plane(mine_m, dp)
        inner_other = swap(inner_weight, "fsdp", fsdp, 1)
        outer_other = swap(outer_weight, "fsdp", fsdp, 1)

        def far_at(base, row, halves):
            return [[(base + n, row, 96, 0)] for n in range(3)] + [[(base + n, 0, rows, off) for n, rows, off in halves]]

        split = ((3, 48, 0), (4, 48, 48))
        group_a = Pieces(
            mine,
            theirs + near_a + far_a + (piece_a,),
            [(n, 0, 0) for n in range(4)],
            [(n, 0, 0) for n in range(4)],
            far_at(5, 0, split),
            far_at(10, 0, split),
            True,
            (15, 4),
        )
        x = tokens.reshape(seq, width)
        q, k, v, att, left_a, lse, wa, vec, ib = attend_forward(group_a, fsdp, blocks, me, lengths, after(x, mine_m))
        plane_m = (after(plane_m[0], att), after(plane_m[1], att))
        rest_m = (swap(plane_m[0][:, :96], "dp", dp, 2), swap(plane_m[1][:, 96:], "dp", dp, 1))
        near_m = (mine_m,) + plane_m + rest_m
        far_m = tuple(swap(w, "fsdp", fsdp, 1) for w in near_m)
        group_i = Pieces(
            (inner_weight,),
            (inner_other,) + near_m[:4] + far_m[:4],
            [(0, 0, 768 * n) for n in range(4)],
            [(0, 0, 768 * n) for n in range(4)],
            far_at(1, 0, ((3, 96, 0),)),
            far_at(5, 0, ((3, 96, 0),)),
            True,
        )
        group_u = Pieces(
            (outer_weight,),
            (outer_other,) + near_m[:3] + near_m[4:] + far_m[:3] + far_m[4:],
            [(0, 96 * n, 0) for n in range(4)],
            [(0, 96 * n, 0) for n in range(4)],
            far_at(1, 96, ((3, 96, 0),)),
            far_at(5, 96, ((3, 96, 0),)),
            False,
        )
    else:
        whole = tuple(
            lax.all_gather(w, "fsdp", axis=0, tiled=True)
            for w in (query_weight, key_weight, value_weight, output_weight, inner_weight, outer_weight)
        )
        packs = jnp.pad(jnp.stack(small[:8]), ((0, 0), (0, width - part)))
        packs = packs + jnp.pad(inner_bias[None], ((0, 7), (128, width - 128 - 4 * part)))
        packs = lax.all_gather(packs, "fsdp", axis=0, tiled=False)
        group_a = Whole(whole[:4], (packs,), [(n, 0, 0) for n in range(4)], True)
        group_i = Whole(whole[4:5], (), [(0, 0, width * n) for n in range(blocks)], True)
        group_u = Whole(whole[5:6], (), [(0, width * n, 0) for n in range(blocks)], False)
        x = tokens.reshape(seq, width)
        q, k, v, att, left_a, lse, wa, vec, ib = attend_forward(group_a, fsdp, blocks, me, lengths, x)

    cot = cotangent.reshape(seq, width)
    wi, wu = fill((group_i, group_u), me, width, blocks)
    out, ssg, low, act_t, slope, norm, rstd, hid_t, sum_one = middle_forward(lengths, x, att, cot, vec, ib, wa, wi, wu)
    pairs = width // 128
    attend = functools.partial(attend_backward, length=lengths, q=q, k=k, v=v, lse=lse)
    if direct:
        sent_u, kept_u = weight_grad("outer", (1, 3, 0, 2), Z_ORDER, me, act_t, low)
        got_u = swap(sent_u, "fsdp", fsdp, 1)
        low = after(low, sent_u)
    igl, fsg, branch, att_g, ib_sum, sum_two = middle_backward(low, ssg, slope, norm, rstd, vec, wa, wi, wu)
    if direct:
        first_u = total(kept_u[:2], got_u[:2])
        over_u = swap(first_u, "dp", dp, 1)
        sent_i, kept_i = weight_grad("inner", (2, 3, 0, 1), Z_ORDER, me, hid_t, after(igl, first_u))
        got_i = swap(sent_i, "fsdp", fsdp, 1)
        half = attend(0, pairs // 2, do=after(att_g, sent_i), branch=branch)
        first_i = total(kept_i[:2], got_i[:2])
        over_i = swap(first_i, "dp", dp, 2)
        g, sum_three = attend(pairs // 2, pairs, do=after(att_g, first_i), branch=branch, before=half)
    else:
        g, sum_three = attend(0, pairs, do=att_g, branch=branch)
        in_grad = input_grad(g, fsg, wa)

    if direct:
        sent_a, kept_a = weight_grad(
            "attend", (0, 1, 2, 3), (0, 1, 2, 3), me, left_a, g, (sum_one, sum_two, sum_three, ib_sum)
        )
        got_a = swap(sent_a, "fsdp", fsdp, 1)
        in_grad = input_grad(g, after(fsg, sent_a), wa)
        ready_a = [total(kept_a[m], got_a[m]) for m in (1, 2, 3)]
        over_a = [swap(ready_a[m - 1], "dp", dp, m) for m in (1, 2, 3)]
        over_u = after(over_u, *ready_a)
        onward_u = swap(total(kept_u[3], got_u[3], over_u[1]), "dp", dp, 2)
        onward_i = swap(total(kept_i[3], got_i[3], over_i[1]), "dp", dp, 1)
        plane_u = total(kept_u[2], got_u[2], over_u[0], onward_u)
        plane_i = total(kept_i[2], got_i[2], over_i[0], onward_i)
        plane_m = jnp.concatenate([plane_u, plane_i], axis=1)
        over_a[0] = after(over_a[0], plane_m)
        own_a = direct_z(total(kept_a[0], got_a[0], *over_a), fsdp)
        both = spread(scatter_z(plane_m, fsdp), dp)
        small_own = own_a[96:104].astype(F32)
        small_grads = [small_own[n, :part] for n in range(8)] + [small_own[0, 128 : 128 + blocks * part]]
        q_g, k_g, v_g, o_g = (w.astype(F32) for w in in_order(spread(own_a[:96], dp), i))
        u_g = jnp.concatenate(in_order([w[:96] for w in both], i), axis=0).astype(F32)
        i_g = jnp.concatenate(in_order([w[96:] for w in both], i), axis=1).astype(F32)
    else:
        vec_sum = jnp.concatenate([sum_three[:2], sum_two[2:5], sum_one[5:8]])
        vec_sum = vec_sum.reshape(8, fsdp, part).transpose(1, 0, 2).reshape(fsdp, 8 * part)
        ib_part = ib_sum.reshape(fsdp, blocks * part)
        small_sum = lax.psum(jnp.concatenate([vec_sum, ib_part], axis=1), ("dp", "fsdp"))
        small_own = lax.dynamic_index_in_dim(small_sum, f, 0, keepdims=False)
        small_grads = [small_own[n * part : (n + 1) * part] for n in range(8)] + [small_own[8 * part :]]
        x_t, att_t = left_a[0], left_a[1]
        locals_ = (
            dot_nn(x_t, g[0]),
            dot_nn(x_t, g[1]),
            dot_nn(x_t, g[2]),
            dot_nn(att_t, g[3]),
            jnp.concatenate([dot_nn(hid_t, igl[n]) for n in range(blocks)], axis=1),
            dot_nn(act_t, low),
        )
        owned = [lax.psum_scatter(w, "fsdp", scatter_dimension=0, tiled=True) for w in locals_]
        q_g, k_g, v_g, o_g, i_g, u_g = (lax.psum(w.astype(BF16), "dp").astype(F32) for w in owned)

    qb, vb, ob, g1, s1, ub, g2, s2, ibg = small_grads
    return (
        out.reshape(docs, seq, width),
        in_grad.reshape(docs, seq, width),
        q_g,
        qb,
        k_g,
        v_g,
        vb,
        o_g,
        ob,
        g1,
        s1,
        i_g,
        ibg,
        u_g,
        ub,
        g2,
        s2,
    )


def solution(mesh):
    rows, row = P("fsdp", None), P("fsdp")
    docs = P(("dp", "fsdp"), None, None)
    in_specs = (docs, P(("dp", "fsdp")), docs, rows, row, rows, rows, row, rows, row, row, row, rows, row, rows, row, row, row)
    out_specs = (docs, docs, rows, row, rows, rows, row, rows, row, row, row, rows, row, rows, row, row, row)
    sizes = (mesh.shape["dp"], mesh.shape["fsdp"])
    return jax.shard_map(
        functools.partial(on_device, sizes), mesh=mesh, in_specs=in_specs, out_specs=out_specs, check_vma=False
    )
```

time: 378 us -> 284 us (0.75)
  blocking collectives: 87.3 us -> 0 us
  waiting for transfers between devices: 89.1 us -> 147 us
  Pallas kernels: 116 us -> 69.1 us
  starting transfers between devices: 63.6 us -> 43.1 us
  other arithmetic: 8.74 us -> 12.8 us
    psum x1 -> x0, blocking collectives: 73.3 us -> none  [on_device(): small_sum = lax.psum(small_sum, ('dp', 'fsdp'))]
    ppermute x66 -> x52, waiting for transfers between devices: 89.1 us -> 147 us  [swap(): return lax.ppermute(value, axis, [(n, n ^ mask) for n in range(size)])]
    pallas_call x11 -> x23, Pallas kernels: 116 us -> 69.1 us  [the longest x3 13.5 us: weight_grad(): pl.pallas_call(functools.partial(weight_grad_body, kind, order, z_order),...]
    ppermute x66 -> x52, starting transfers between devices: 63.6 us -> 43.1 us  [swap(): return lax.ppermute(value, axis, [(n, n ^ mask) for n in range(size)])]
    all_gather x1 -> x0, blocking collectives: 14 us -> none  [on_device(): lax.all_gather(jnp.concatenate(small), 'fsdp', axis=0, tiled=False)]
    unnamed x90 -> x56, local copies, waits for them, and re-layouts: 3.02 us -> 8.89 us
    convert_element_type x15, other arithmetic: 6.76 us -> 12.2 us  [the longest x11 8.94 us: total(): return result.astype(BF16)]
  transfers between devices with their start and end apart: 66 -> 52, of which waited for: 23 -> 23; matrix products, arithmetic and copies ran while one was open for 4% -> 4% of each run, Pallas kernels for 23% -> 11%
where the time goes in v2:
time: 284 us
  waiting for transfers between devices  147 us (52%)
  Pallas kernels  69.1 us (24%)
  starting transfers between devices  43.1 us (15%)
  other arithmetic  12.8 us (5%)
  local copies, waits for them, and re-layouts  10.2 us (4%)
    ppermute x52, waiting for transfers between devices, swap(): return lax.ppermute(value, axis, [(n, n ^ mask) for n in range(size)])  147 us
    ppermute x52, starting transfers between devices, swap(): return lax.ppermute(value, axis, [(n, n ^ mask) for n in range(size)])  43.1 us
    pallas_call x3, Pallas kernels, weight_grad(): pl.pallas_call(functools.partial(weight_grad_body, kind, order, z_order),...  13.5 us
    pallas_call x1, Pallas kernels, middle_forward(): pl.pallas_call(middle_forward_body, out_shape=(shape(seq, width), local(s...  13.4 us
    pallas_call x2, Pallas kernels, attend_backward(): pl.pallas_call(functools.partial(attend_backward_body, first, last), out_...  12.8 us
    pallas_call x1, Pallas kernels, attend_forward(): pl.pallas_call(functools.partial(attend_forward_body, group, width // sha...  12.2 us
    pallas_call x1, Pallas kernels, middle_backward(): pl.pallas_call(middle_backward_body, out_shape=(local(blocks, seq, width)...  10.1 us
    convert_element_type x11, other arithmetic, total(): return result.astype(BF16)  8.94 us
  transfers between devices with their start and end apart: 52, of which 23 were waited for; matrix products, arithmetic and copies ran while one was open for 4% of the time, Pallas kernels for 11%

profile of v2, /device:TPU:0, one launch (start us, length us, event | category | flops | bytes accessed | tf_op | source)
XLA Modules:
  0.0 283.7 jit_solution(5743492334986889137)
XLA Ops:
  2.5 5.1 %collective-permute-start.2 = (bf16[104,768]{1,0:T(8,128)(2,1)S(1)}, bf16[104,768]{1,0:T(8,128)(2,1)S(1)}, u32[]{:S(2)}, u32[]{:S(2)}) collective-permute-start(bf16[104,768]{1,0:T(8,128)(2,1)S(1)} %get-tuple-element.56.refs_19_), channel_id=1, source_target_pairs={{0,6},{1,7},{2,4},{3,5},{4,2},{5,3},{6,0},{7,1},{8,14},{9,15},{10,... | collective-permute-start | bytes 479240 | tf_op jit(solution)/shard_map/ppermute | solution.py:616
  8.8 3.9 %collective-permute-done.2 = bf16[104,768]{1,0:T(8,128)(2,1)S(1)} collective-permute-done((bf16[104,768]{1,0:T(8,128)(2,1)S(1)}, bf16[104,768]{1,0:T(8,128)(2,1)S(1)}, u32[]{:S(2)}, u32[]{:S(2)}) %collective-permute-start.2) | collective-permute-done | bytes 159776 | tf_op jit(solution)/shard_map/ppermute | solution.py:616
  12.6 8.5 %collective-permute-done.1 = bf16[104,768]{1,0:T(8,128)(2,1)S(1)} collective-permute-done((bf16[104,768]{1,0:T(8,128)(2,1)S(1)}, bf16[104,768]{1,0:T(8,128)(2,1)S(1)}, u32[]{:S(2)}, u32[]{:S(2)}) %collective-permute-start.1) | collective-permute-done | bytes 159776 | tf_op jit(solution)/shard_map/ppermute | solution.py:616
  30.1 7.4 %collective-permute-done.7 = bf16[192,768]{1,0:T(8,128)(2,1)S(1)} collective-permute-done((bf16[192,768]{1,0:T(8,128)(2,1)S(1)}, bf16[192,768]{1,0:T(8,128)(2,1)S(1)}, u32[]{:S(2)}, u32[]{:S(2)}) %collective-permute-start.7) | collective-permute-done | bytes 294944 | tf_op jit(solution)/shard_map/ppermute | solution.py:616
  38.1 14.7 %collective-permute-done.6 = bf16[192,768]{1,0:T(8,128)(2,1)S(1)} collective-permute-done((bf16[192,768]{1,0:T(8,128)(2,1)S(1)}, bf16[192,768]{1,0:T(8,128)(2,1)S(1)}, u32[]{:S(2)}, u32[]{:S(2)}) %collective-permute-start.6) | collective-permute-done | bytes 294944 | tf_op jit(solution)/shard_map/ppermute | solution.py:616
  53.8 5.6 %collective-permute-done.13.refs_12_ = bf16[3,48,768]{2,1,0:T(8,128)(2,1)S(1)} collective-permute-done((bf16[3,48,768]{2,1,0:T(8,128)(2,1)S(1)}, bf16[3,48,768]{2,1,0:T(8,128)(2,1)S(1)}, u32[]{:S(2)}, u32[]{:S(2)}) %collective-permute-start.13) | collective-permute-done | bytes 221216 | tf_op jit(solution)/shard_map/ppermute | solution.py:616
  64.3 12.2 %attend_forward.1 = (bf16[512,768]{1,0:T(8,128)(2,1)S(1)}, bf16[512,768]{1,0:T(8,128)(2,1)S(1)}, bf16[512,768]{1,0:T(8,128)(2,1)S(1)}, bf16[512,768]{1,0:T(8,128...) custom-call(s32[4]{0:T(128)S(1)} %pad_add_fusion.me_ref, ...), custom_call_target="tpu_custom_call" | custom-call | flops 12000000000 | bytes 20000000 | tf_op jit(solution)/shard_map/attend_forward/pallas_call | solution.py:210
  76.6 7.6 %collective-permute-done.21.refs_0_ = bf16[3,192,768]{2,1,0:T(8,128)(2,1)S(1)} collective-permute-done((bf16[3,192,768]{2,1,0:T(8,128)(2,1)S(1)}, bf16[3,192,768]{2,1,0:T(8,128)(2,1)S(1)}, u32[]{:S(2)}, u32[]{:S(2)}) %collective-permute-start.21) | collective-permute-done | bytes 884768 | tf_op jit(solution)/shard_map/ppermute | solution.py:616
  87.6 9.6 %collective-permute-done.23.refs_5_ = bf16[3,96,768]{2,1,0:T(8,128)(2,1)S(1)} collective-permute-done((bf16[3,96,768]{2,1,0:T(8,128)(2,1)S(1)}, bf16[3,96,768]{2,1,0:T(8,128)(2,1)S(1)}, u32[]{:S(2)}, u32[]{:S(2)}) %collective-permute-start.23) | collective-permute-done | bytes 442400 | tf_op jit(solution)/shard_map/ppermute | solution.py:616
  102.1 13.4 %middle_forward.1 = (bf16[512,768]{1,0:T(8,128)(2,1)}, f32[512,768]{1,0:T(8,128)S(1)}, bf16[512,768]{1,0:T(8,128)(2,1)S(1)}, bf16[3072,512]{1,0:T(8,128)(2,1)S(1...) custom-call(s32[1]{0:T(128)S(6)} %copy.63.len_ref, ...), custom_call_target="tpu_custom_call" | custom-call | flops 12000000000 | bytes 30000000 | tf_op jit(solution)/shard_map/middle_forward/pallas_call | solution.py:393
  115.5 4.4 %weight_grad_outer.1 = (bf16[4,4,96,768]{3,2,1,0:T(8,128)(2,1)S(1)}, bf16[4,4,96,768]{3,2,1,0:T(8,128)(2,1)S(1)}) custom-call(s32[4]{0:T(128)S(1)} %pad_add_fusion.me_ref, bf16[3072,512]{1,0:T(8,128)(2,1)S(1)} %get-tuple-element.68.left_ref, bf16[512,768]{1,0:T(8,128)(2,1)S(1)} %get-tuple-element.67.g_ref.refs_0_), custom_call_target="tpu_custom_call" | custom-call | flops 4000000000 | bytes 6000000 | tf_op jit(solution)/shard_map/weight_grad_outer/pallas_call | solution.py:542
  120.2 10.1 %middle_backward.1 = (bf16[4,512,768]{2,1,0:T(8,128)(2,1)S(1)}, f32[512,768]{1,0:T(8,128)S(1)}, bf16[512,768]{1,0:T(8,128)(2,1)S(1)}, bf16[512,768]{1,0:T(8,128)...) custom-call(bf16[512,768]{1,0:T(8,128)(2,1)S(1)} %after.17.low_ref, f32[512,768]{1,0:T(8,128)S(1)} %get-tuple-element.70.ssg_ref, ...), custom_call_target="tpu_custom_call" | custom-call | flops 8999999488 | bytes 25000000 | tf_op jit(solution)/shard_map/middle_backward/pallas_call | solution.py:453
  131.5 4.5 %weight_grad_inner.1 = (bf16[4,4,96,768]{3,2,1,0:T(8,128)(2,1)S(1)}, bf16[4,4,96,768]{3,2,1,0:T(8,128)(2,1)S(1)}) custom-call(s32[4]{0:T(128)S(1)} %pad_add_fusion.me_ref, bf16[768,512]{1,0:T(8,128)(2,1)S(1)} %get-tuple-element.75.left_ref, bf16[4,512,768]{2,1,0:T(8,128)(2,1)S(1)} %after.18.g_ref), custom_call_target="tpu_custom_call" | custom-call | flops 4000000000 | bytes 6000000 | tf_op jit(solution)/shard_map/weight_grad_inner/pallas_call | solution.py:542
  136.5 6.3 %attend_backward.2 = (bf16[4,512,768]{2,1,0:T(8,128)(2,1)S(1)}, f32[8,768]{1,0:T(8,128)S(1)}) custom-call(s32[1]{0:T(128)S(6)} %copy.63.len_ref, bf16[512,768]{1,0:T(8,128)(2,1)S(1)} %get-tuple-element.64.q_ref, bf16[512,768]{1,0:T(8,128)(2,1)S(1)} %get-tuple-element.65.k_ref, bf16[512,768]{1,0:T(8,128)(2,1)S(1)} %get-tuple-element.66.v_ref, ...), custom_call_target="tpu_custom_call" | custom-call | flops 16000000000 | bytes 9000000 | tf_op jit(solution)/shard_map/attend_backward/pallas_call | solution.py:270
  143.1 6.5 %attend_backward.3 = (bf16[4,512,768]{2,1,0:T(8,128)(2,1)S(1)}, f32[8,768]{1,0:T(8,128)S(1)}) custom-call(s32[1]{0:T(128)S(6)} %copy.63.len_ref, bf16[512,768]{1,0:T(8,128)(2,1)S(1)} %get-tuple-element.64.q_ref, bf16[512,768]{1,0:T(8,128)(2,1)S(1)} %get-tuple-element.65.k_ref, ...), custom_call_target="tpu_custom_call", output_to_operand_aliasing={{0}: (7, {}), {1}: (8, {})} | custom-call | flops 16000000000 | bytes 9000000 | tf_op jit(solution)/shard_map/attend_backward/pallas_call | solution.py:270
  149.6 4.5 %weight_grad_attend.1 = (bf16[4,4,104,768]{3,2,1,0:T(8,128)(2,1)S(1)}, bf16[4,4,104,768]{3,2,1,0:T(8,128)(2,1)S(1)}) custom-call(s32[4]{0:T(128)S(1)} %pad_add_fusion.me_ref, bf16[2,768,512]{2,1,0:T(8,128)(2,1)S(1)} %get-tuple-element.86.left_ref, bf16[4,512,768]{2,1,0:T(8,128)(2,1)S(1)} %get-tuple-element.84.g_ref, f32[8,768]{1,0:T(8,128)S(1)} %get-tuple-element.87.refs_0_, ...), custom_call_target="tpu_custom_call" | custom-call | flops 4000000000 | bytes 6000000 | tf_op jit(solution)/shard_map/weight_grad_attend/pallas_call | solution.py:542
  158.4 26.0 %collective-permute-done.37 = bf16[2,4,96,768]{3,2,1,0:T(8,128)(2,1)S(1)} collective-permute-done((bf16[2,4,96,768]{3,2,1,0:T(8,128)(2,1)S(1)}, bf16[2,4,96,768]{3,2,1,0:T(8,128)(2,1)S(1)}, u32[]{:S(2)}, u32[]{:S(2)}) %collective-permute-start.37) | collective-permute-done | bytes 1179680 | tf_op jit(solution)/shard_map/ppermute | solution.py:616
  204.0 16.0 %collective-permute-done.36 = bf16[4,96,768]{2,1,0:T(8,128)(2,1)} collective-permute-done((bf16[4,96,768]{2,1,0:T(8,128)(2,1)}, bf16[4,96,768]{2,1,0:T(8,128)(2,1)}, u32[]{:S(2)}, u32[]{:S(2)}) %collective-permute-start.36) | collective-permute-done | bytes 589856 | tf_op jit(solution)/shard_map/ppermute | solution.py:616
  221.9 6.4 %collective-permute-done.34.refs_0_ = bf16[4,104,768]{2,1,0:T(8,128)(2,1)S(1)} collective-permute-done((bf16[4,104,768]{2,1,0:T(8,128)(2,1)S(1)}, bf16[4,104,768]{2,1,0:T(8,128)(2,1)S(1)}, u32[]{:S(2)}, u32[]{:S(2)}) %collective-permute-start.34) | collective-permute-done | bytes 639008 | tf_op jit(solution)/shard_map/ppermute | solution.py:616
  228.3 3.8 %collective-permute-done.39 = bf16[4,104,768]{2,1,0:T(8,128)(2,1)S(1)} collective-permute-done((bf16[4,104,768]{2,1,0:T(8,128)(2,1)S(1)}, bf16[4,104,768]{2,1,0:T(8,128)(2,1)S(1)}, u32[]{:S(2)}, u32[]{:S(2)}) %collective-permute-start.39) | collective-permute-done | bytes 639008 | tf_op jit(solution)/shard_map/ppermute | solution.py:616
  242.8 4.6 %collective-permute-done.42 = bf16[104,768]{1,0:T(8,128)(2,1)S(1)} collective-permute-done((bf16[104,768]{1,0:T(8,128)(2,1)S(1)}, bf16[104,768]{1,0:T(8,128)(2,1)S(1)}, u32[]{:S(2)}, u32[]{:S(2)}) %collective-permute-start.42) | collective-permute-done | bytes 159776 | tf_op jit(solution)/shard_map/ppermute | solution.py:616
  252.1 13.2 %collective-permute-done.48 = bf16[192,768]{1,0:T(8,128)(2,1)S(1)} collective-permute-done((bf16[192,768]{1,0:T(8,128)(2,1)S(1)}, bf16[192,768]{1,0:T(8,128)(2,1)S(1)}, u32[]{:S(2)}, u32[]{:S(2)}) %collective-permute-start.48) | collective-permute-done | bytes 294944 | tf_op jit(solution)/shard_map/ppermute | solution.py:616
  270.7 5.6 %collective-permute-done.51 = bf16[192,768]{1,0:T(8,128)(2,1)S(1)} collective-permute-done((bf16[192,768]{1,0:T(8,128)(2,1)S(1)}, bf16[192,768]{1,0:T(8,128)(2,1)S(1)}, u32[]{:S(2)}, u32[]{:S(2)}) %collective-permute-start.51) | collective-permute-done | bytes 294944 | tf_op jit(solution)/shard_map/ppermute | solution.py:616
  276.3 5.0 %collective-permute-done.50 = bf16[192,768]{1,0:T(8,128)(2,1)S(1)} collective-permute-done((bf16[192,768]{1,0:T(8,128)(2,1)S(1)}, bf16[192,768]{1,0:T(8,128)(2,1)S(1)}, u32[]{:S(2)}, u32[]{:S(2)}) %collective-permute-start.50) | collective-permute-done | bytes 294944 | tf_op jit(solution)/shard_map/ppermute | solution.py:616
  (191 shorter events, 77.0 us)
Async XLA Ops:
  8.3 16.6 %collective-permute-start.9 = (bf16[96,768]{1,0:T(8,128)(2,1)S(1)}, bf16[96,768]{1,0:T(8,128)(2,1)S(1)}, u32[]{:S(2)}, u32[]{:S(2)}) collective-permute-start(bf16[96,768]{1,0:T(8,128)(2,1)S(1)} %copy-done.22), channel_id=1, source_target_pairs={{0,1},{1,0},{2,3},{3,2},{4,5},{5,4},{6,7},{7,6},{8,9},{9,8},{10,11... | collective-permute-start | bytes 442376 | tf_op jit(solution)/shard_map/ppermute | solution.py:616
  21.2 16.3 %collective-permute-start.4 = (bf16[3,104,768]{2,1,0:T(8,128)(2,1)S(1)}, bf16[3,104,768]{2,1,0:T(8,128)(2,1)S(1)}, u32[]{:S(2)}, u32[]{:S(2)}) collective-permute-start(bf16[3,104,768]{2,1,0:T(8,128)(2,1)S(1)} %pad_maximum_fusion.2.refs_1_.refs_9_), channel_id=1, source_target_pairs={{0,8},{8,0},{16,24},{24,16},{1,9},{9,1},{17,25},{25,17},{2,10},{10... | collective-permute-start | bytes 1437704 | tf_op jit(solution)/shard_map/ppermute | solution.py:616
  28.1 24.6 %collective-permute-start.6 = (bf16[192,768]{1,0:T(8,128)(2,1)S(1)}, bf16[192,768]{1,0:T(8,128)(2,1)S(1)}, u32[]{:S(2)}, u32[]{:S(2)}) collective-permute-start(bf16[192,768]{1,0:T(8,128)(2,1)S(1)} %after.12), channel_id=1, source_target_pairs={{0,4},{1,5},{2,6},{3,7},{4,0},{5,1},{6,2},{7,3},{8,12},{9,13},{10,... | collective-permute-start | bytes 884744 | tf_op jit(solution)/shard_map/ppermute | solution.py:616
  28.2 25.1 %collective-permute-start.3 = (bf16[192,768]{1,0:T(8,128)(2,1)S(1)}, bf16[192,768]{1,0:T(8,128)(2,1)S(1)}, u32[]{:S(2)}, u32[]{:S(2)}) collective-permute-start(bf16[192,768]{1,0:T(8,128)(2,1)S(1)} %after.12), channel_id=1, source_target_pairs={{0,2},{1,3},{2,0},{3,1},{4,6},{5,7},{6,4},{7,5},{8,10},{9,11},{10,... | collective-permute-start | bytes 884744 | tf_op jit(solution)/shard_map/ppermute | solution.py:616
  37.5 23.4 %collective-permute-start.15 = (bf16[3,104,768]{2,1,0:T(8,128)(2,1)S(1)}, bf16[3,104,768]{2,1,0:T(8,128)(2,1)S(1)}, u32[]{:S(2)}, u32[]{:S(2)}) collective-permute-start(bf16[3,104,768]{2,1,0:T(8,128)(2,1)S(1)} %pad_maximum_fusion.2.refs_1_.refs_9_), channel_id=1, source_target_pairs={{0,1},{1,0},{2,3},{3,2},{4,5},{5,4},{6,7},{7,6},{8,9},{9,8},{10,11... | collective-permute-start | bytes 1437704 | tf_op jit(solution)/shard_map/ppermute | solution.py:616
  37.5 25.4 %collective-permute-start.16 = (bf16[3,104,768]{2,1,0:T(8,128)(2,1)S(1)}, bf16[3,104,768]{2,1,0:T(8,128)(2,1)S(1)}, u32[]{:S(2)}, u32[]{:S(2)}) collective-permute-start(bf16[3,104,768]{2,1,0:T(8,128)(2,1)S(1)} %collective-permute-done.4.refs_10_), channel_id=1, source_target_pairs={{0,1},{1,0},{2,3},{3,2},{4,5},{5,4},{6,7},{7,6},{8,9},{9,8},{10,11... | collective-permute-start | bytes 1437704 | tf_op jit(solution)/shard_map/ppermute | solution.py:616
  38.0 26.3 %collective-permute-start.17 = (bf16[3,104,768]{2,1,0:T(8,128)(2,1)S(1)}, bf16[3,104,768]{2,1,0:T(8,128)(2,1)S(1)}, u32[]{:S(2)}, u32[]{:S(2)}) collective-permute-start(bf16[3,104,768]{2,1,0:T(8,128)(2,1)S(1)} %collective-permute-done.5.refs_11_), channel_id=1, source_target_pairs={{0,1},{1,0},{2,3},{3,2},{4,5},{5,4},{6,7},{7,6},{8,9},{9,8},{10,11... | collective-permute-start | bytes 1437704 | tf_op jit(solution)/shard_map/ppermute | solution.py:616
  61.9 23.0 %collective-permute-start.20 = (bf16[96,3072]{1,0:T(8,128)(2,1)S(1)}, bf16[96,3072]{1,0:T(8,128)(2,1)S(1)}, u32[]{:S(2)}, u32[]{:S(2)}) collective-permute-start(bf16[96,3072]{1,0:T(8,128)(2,1)S(1)} %copy-done.15), channel_id=1, source_target_pairs={{0,1},{1,0},{2,3},{3,2},{4,5},{5,4},{6,7},{7,6},{8,9},{9,8},{10,11... | collective-permute-start | bytes 1769480 | tf_op jit(solution)/shard_map/ppermute | solution.py:616
  62.1 24.3 %collective-permute-start.28 = (bf16[384,768]{1,0:T(8,128)(2,1)S(1)}, bf16[384,768]{1,0:T(8,128)(2,1)S(1)}, u32[]{:S(2)}, u32[]{:S(2)}) collective-permute-start(bf16[384,768]{1,0:T(8,128)(2,1)S(1)} %copy-done.16), channel_id=1, source_target_pairs={{0,1},{1,0},{2,3},{3,2},{4,5},{5,4},{6,7},{7,6},{8,9},{9,8},{10,11... | collective-permute-start | bytes 1769480 | tf_op jit(solution)/shard_map/ppermute | solution.py:616
  62.4 21.8 %collective-permute-start.21 = (bf16[3,192,768]{2,1,0:T(8,128)(2,1)S(1)}, bf16[3,192,768]{2,1,0:T(8,128)(2,1)S(1)}, u32[]{:S(2)}, u32[]{:S(2)}) collective-permute-start(bf16[3,192,768]{2,1,0:T(8,128)(2,1)S(1)} %pad_maximum_fusion.1.refs_1_.refs_2_.refs_12_), channel_id=1, source_target_pairs={{0,8},{8,0},{16,24},{24,16},{1,9},{9,1},{17,25},{25,17},{2,10},{10... | collective-permute-start | bytes 2654216 | tf_op jit(solution)/shard_map/ppermute | solution.py:616
  62.9 21.5 %collective-permute-start.22 = (bf16[3,192,768]{2,1,0:T(8,128)(2,1)S(1)}, bf16[3,192,768]{2,1,0:T(8,128)(2,1)S(1)}, u32[]{:S(2)}, u32[]{:S(2)}) collective-permute-start(bf16[3,192,768]{2,1,0:T(8,128)(2,1)S(1)} %pad_maximum_fusion.1.refs_1_.refs_2_.refs_12_), channel_id=1, source_target_pairs={{0,16},{8,24},{16,0},{24,8},{1,17},{9,25},{17,1},{25,9},{2,18},{10... | collective-permute-start | bytes 2654216 | tf_op jit(solution)/shard_map/ppermute | solution.py:616
  64.3 34.0 %collective-permute-start.24 = (bf16[3,192,768]{2,1,0:T(8,128)(2,1)S(1)}, bf16[3,192,768]{2,1,0:T(8,128)(2,1)S(1)}, u32[]{:S(2)}, u32[]{:S(2)}) collective-permute-start(bf16[3,192,768]{2,1,0:T(8,128)(2,1)S(1)} %pad_maximum_fusion.1.refs_1_.refs_2_.refs_12_), channel_id=1, source_target_pairs={{0,1},{1,0},{2,3},{3,2},{4,5},{5,4},{6,7},{7,6},{8,9},{9,8},{10,11... | collective-permute-start | bytes 2654216 | tf_op jit(solution)/shard_map/ppermute | solution.py:616
  154.2 32.9 %collective-permute-start.33 = (bf16[4,4,104,768]{3,2,1,0:T(8,128)(2,1)S(1)}, bf16[4,4,104,768]{3,2,1,0:T(8,128)(2,1)S(1)}, u32[]{:S(2)}, u32[]{:S(2)}) collective-permute-start(bf16[4,4,104,768]{3,2,1,0:T(8,128)(2,1)S(1)} %get-tuple-element.91.refs_1_), channel_id=1, source_target_pairs={{0,1},{1,0},{2,3},{3,2},{4,5},{5,4},{6,7},{7,6},{8,9},{9,8},{10,11... | collective-permute-start | bytes 7667720 | tf_op jit(solution)/shard_map/ppermute | solution.py:616
  156.0 28.4 %collective-permute-start.37 = (bf16[2,4,96,768]{3,2,1,0:T(8,128)(2,1)S(1)}, bf16[2,4,96,768]{3,2,1,0:T(8,128)(2,1)S(1)}, u32[]{:S(2)}, u32[]{:S(2)}) collective-permute-start(bf16[2,4,96,768]{3,2,1,0:T(8,128)(2,1)S(1)} %add_convert_fusion.refs_1_), channel_id=1, source_target_pairs={{0,16},{8,24},{16,0},{24,8},{1,17},{9,25},{17,1},{25,9},{2,18},{10... | collective-permute-start | bytes 3538952 | tf_op jit(solution)/shard_map/ppermute | solution.py:616
  156.9 31.8 %collective-permute-start.35 = (bf16[2,4,96,768]{3,2,1,0:T(8,128)(2,1)S(1)}, bf16[2,4,96,768]{3,2,1,0:T(8,128)(2,1)S(1)}, u32[]{:S(2)}, u32[]{:S(2)}) collective-permute-start(bf16[2,4,96,768]{3,2,1,0:T(8,128)(2,1)S(1)} %add_convert_fusion.1.refs_1_), channel_id=1, source_target_pairs={{0,8},{8,0},{16,24},{24,16},{1,9},{9,1},{17,25},{25,17},{2,10},{10... | collective-permute-start | bytes 3538952 | tf_op jit(solution)/shard_map/ppermute | solution.py:616
  185.6 16.5 %collective-permute-start.38 = (bf16[4,96,768]{2,1,0:T(8,128)(2,1)}, bf16[4,96,768]{2,1,0:T(8,128)(2,1)}, u32[]{:S(2)}, u32[]{:S(2)}) collective-permute-start(bf16[4,96,768]{2,1,0:T(8,128)(2,1)} %fusion.9), channel_id=1, source_target_pairs={{0,8},{8,0},{16,24},{24,16},{1,9},{9,1},{17,25},{25,17},{2,10},{10... | collective-permute-start | bytes 1769480 | tf_op jit(solution)/shard_map/ppermute | solution.py:616
  189.7 30.3 %collective-permute-start.36 = (bf16[4,96,768]{2,1,0:T(8,128)(2,1)}, bf16[4,96,768]{2,1,0:T(8,128)(2,1)}, u32[]{:S(2)}, u32[]{:S(2)}) collective-permute-start(bf16[4,96,768]{2,1,0:T(8,128)(2,1)} %fusion.8), channel_id=1, source_target_pairs={{0,16},{8,24},{16,0},{24,8},{1,17},{9,25},{17,1},{25,9},{2,18},{10... | collective-permute-start | bytes 1769480 | tf_op jit(solution)/shard_map/ppermute | solution.py:616
  194.9 33.4 %collective-permute-start.40 = (bf16[4,104,768]{2,1,0:T(8,128)(2,1)S(1)}, bf16[4,104,768]{2,1,0:T(8,128)(2,1)S(1)}, u32[]{:S(2)}, u32[]{:S(2)}) collective-permute-start(bf16[4,104,768]{2,1,0:T(8,128)(2,1)S(1)} %get-tuple-element.94.refs_3_), channel_id=1, source_target_pairs={{0,24},{8,16},{16,8},{24,0},{1,25},{9,17},{17,9},{25,1},{2,26},{10... | collective-permute-start | bytes 1916936 | tf_op jit(solution)/shard_map/ppermute | solution.py:616
  196.0 36.1 %collective-permute-start.39 = (bf16[4,104,768]{2,1,0:T(8,128)(2,1)S(1)}, bf16[4,104,768]{2,1,0:T(8,128)(2,1)S(1)}, u32[]{:S(2)}, u32[]{:S(2)}) collective-permute-start(bf16[4,104,768]{2,1,0:T(8,128)(2,1)S(1)} %get-tuple-element.95.refs_2_), channel_id=1, source_target_pairs={{0,16},{8,24},{16,0},{24,8},{1,17},{9,25},{17,1},{25,9},{2,18},{10... | collective-permute-start | bytes 1916936 | tf_op jit(solution)/shard_map/ppermute | solution.py:616
  196.9 31.4 %collective-permute-start.34 = (bf16[4,104,768]{2,1,0:T(8,128)(2,1)S(1)}, bf16[4,104,768]{2,1,0:T(8,128)(2,1)S(1)}, u32[]{:S(2)}, u32[]{:S(2)}) collective-permute-start(bf16[4,104,768]{2,1,0:T(8,128)(2,1)S(1)} %get-tuple-element.93.refs_1_), channel_id=1, source_target_pairs={{0,8},{8,0},{16,24},{24,16},{1,9},{9,1},{17,25},{25,17},{2,10},{10... | collective-permute-start | bytes 1916936 | tf_op jit(solution)/shard_map/ppermute | solution.py:616
  221.7 29.3 %collective-permute-start.47 = (bf16[2,192,768]{2,1,0:T(8,128)(2,1)S(1)}, bf16[2,192,768]{2,1,0:T(8,128)(2,1)S(1)}, u32[]{:S(2)}, u32[]{:S(2)}) collective-permute-start(bf16[2,192,768]{2,1,0:T(8,128)(2,1)S(1)} %fusion.10), channel_id=1, source_target_pairs={{0,2},{1,3},{2,0},{3,1},{4,6},{5,7},{6,4},{7,5},{8,10},{9,11},{10,... | collective-permute-start | bytes 1769480 | tf_op jit(solution)/shard_map/ppermute | solution.py:616
  247.5 20.0 %collective-permute-start.44 = (bf16[96,768]{1,0:T(8,128)(2,1)S(1)}, bf16[96,768]{1,0:T(8,128)(2,1)S(1)}, u32[]{:S(2)}, u32[]{:S(2)}) collective-permute-start(bf16[96,768]{1,0:T(8,128)(2,1)S(1)} %slice.246), channel_id=1, source_target_pairs={{0,8},{8,0},{16,24},{24,16},{1,9},{9,1},{17,25},{25,17},{2,10},{10... | collective-permute-start | bytes 442376 | tf_op jit(solution)/shard_map/ppermute | solution.py:616
  248.1 21.4 %collective-permute-start.45 = (bf16[96,768]{1,0:T(8,128)(2,1)S(1)}, bf16[96,768]{1,0:T(8,128)(2,1)S(1)}, u32[]{:S(2)}, u32[]{:S(2)}) collective-permute-start(bf16[96,768]{1,0:T(8,128)(2,1)S(1)} %slice.246), channel_id=1, source_target_pairs={{0,16},{8,24},{16,0},{24,8},{1,17},{9,25},{17,1},{25,9},{2,18},{10... | collective-permute-start | bytes 442376 | tf_op jit(solution)/shard_map/ppermute | solution.py:616
  249.0 20.6 %collective-permute-start.46 = (bf16[96,768]{1,0:T(8,128)(2,1)S(1)}, bf16[96,768]{1,0:T(8,128)(2,1)S(1)}, u32[]{:S(2)}, u32[]{:S(2)}) collective-permute-start(bf16[96,768]{1,0:T(8,128)(2,1)S(1)} %slice.246), channel_id=1, source_target_pairs={{0,24},{8,16},{16,8},{24,0},{1,25},{9,17},{17,9},{25,1},{2,26},{10... | collective-permute-start | bytes 442376 | tf_op jit(solution)/shard_map/ppermute | solution.py:616
  (55 other events, 780.6 us)

commit v3 on v2

--- a/solution.py
+++ b/solution.py
@@ -20,6 +20,7 @@
 VM = pl.BlockSpec(memory_space=pltpu.VMEM)
 SM = pl.BlockSpec(memory_space=pltpu.SMEM)
 HB = pl.BlockSpec(memory_space=pl.ANY)
+FREE = pl.CostEstimate(flops=0, bytes_accessed=0, transcendentals=0)
 
 
 def shape(*dims, dtype=BF16):
@@ -90,21 +91,59 @@
 
     def fill(self, refs, me_ref, target):
         i, z, c = me_ref[0], me_ref[1], me_ref[2]
-        for block, (position, row, lane) in enumerate(self.sibling):
-            self.place(target, block, z, 1 - c, 0, 96)[...] = refs[position][row : row + 96, lane : lane + 768]
+        for block, (position, tile) in enumerate(self.sibling):
+            self.place(target, block, z, 1 - c, 0, 96)[...] = refs[position][tile]
         for c_at, far in ((c, self.far), (1 - c, self.far_sibling)):
             for away, parts in enumerate(far):
-                for position, row, rows, offset in parts:
+                for position, tile, row, rows, offset in parts:
                     for j in range(1, 4):
                         where = self.place(target, i ^ away, z ^ j, c_at, offset, rows)
-                        where[...] = refs[position][j - 1, row : row + rows, :]
+                        where[...] = refs[position][tile + j - 1, row : row + rows, :]
 
     def vectors(self, refs, me_ref, target):
         z, c = me_ref[1], me_ref[2]
-        for c_at, spot, far in ((c, self.packs[0], self.far), (1 - c, self.packs[1], self.far_sibling)):
-            target[2 * z + c_at] = refs[spot][96:104, :].astype(F32)
-            for j in range(1, 4):
-                target[2 * (z ^ j) + c_at] = refs[far[0][0][0]][j - 1, 96:104, :].astype(F32)
+        own, mine, other = (refs[n] for n in self.packs)
+        for j in range(4):
+            target[2 * (z ^ j) + c] = (mine[j - 1, 96:104, :] if j else own[96:104, :]).astype(F32)
+            target[2 * (z ^ j) + 1 - c] = other[13, 8 * j : 8 * j + 8, :].astype(F32)
+
+
+def bundle_body(group_count, held, me_ref, *refs):
+    sources, near = refs[: len(held)], refs[len(held) : -2]
+    out_ref, sems = refs[-2:]
+    own = [(n, row, lane) for n, spots in enumerate(held) for row, lane in spots]
+    loads = []
+    for tile, (n, row, lane) in enumerate(own):
+        source = sources[n].at[pl.ds(row, 96), pl.ds(lane, 768)]
+        loads.append(pltpu.make_async_copy(source, out_ref.at[tile], sems.at[tile]))
+    start_all(loads)
+    tile = len(own)
+    for away in range(3):
+        for group in range(group_count):
+            for j in range(3):
+                out_ref[tile] = near[away][j, group * 96 : (group + 1) * 96, :]
+                tile += 1
+    if group_count == 1:
+        out_ref[tile, 0:8, :] = near[3][96:104, :]
+        for j in range(3):
+            out_ref[tile, 8 * j + 8 : 8 * j + 16, :] = near[0][j, 96:104, :]
+        out_ref[tile, 32:, :] = jnp.zeros((64, 768), BF16)
+    wait_all(loads)
+
+
+def bundle(group_count, sources, held, near):
+    own = sum(len(spots) for spots in held)
+    tiles = own + 9 * group_count + (group_count == 1)
+    return pl.pallas_call(
+        functools.partial(bundle_body, group_count, held),
+        out_shape=local(tiles, 96, 768),
+        in_specs=[SM] + [HB] * len(sources) + [VM] * len(near),
+        out_specs=VM,
+        scratch_shapes=[pltpu.SemaphoreType.DMA((own,))],
+        compiler_params=limit(2),
+        cost_estimate=FREE,
+        name="bundle",
+    )(jnp.zeros((1,), jnp.int32), *far_off(*sources), *stay(*near))
 
 
 def aligned_rows(start, rows):
@@ -216,7 +255,7 @@
         out_specs=[VM] * 9,
         scratch_shapes=[pltpu.VMEM((shards, 8, width), F32), pltpu.SemaphoreType.DMA((group.count(),))],
         compiler_params=limit(10),
-        cost_estimate=pl.CostEstimate(flops=12_000_000_000, bytes_accessed=20_000_000, transcendentals=3_200_000),
+        cost_estimate=FREE,
         name="attend_forward",
     )(me, length, x, *far_off(*group.held), *stay(*group.arrays))
 
@@ -274,7 +313,7 @@
         out_specs=[VM] * 2,
         input_output_aliases={7 + n: n for n in range(len(before))},
         compiler_params=limit(10),
-        cost_estimate=pl.CostEstimate(flops=16_000_000_000, bytes_accessed=9_000_000, transcendentals=3_200_000),
+        cost_estimate=FREE,
         name="attend_backward",
     )(length, *stay(q, k, v, do, lse, branch, *before))
 
@@ -285,37 +324,26 @@
     return inner * cumulative, cumulative + inner * density
 
 
-def fill_body(groups, me_ref, *refs):
-    sources = []
-    for n, group in enumerate(groups):
-        sources.append((refs[: len(group.held)], refs[len(group.held) : len(group.held) + len(group.arrays)]))
-        refs = refs[len(group.held) + len(group.arrays) :]
-    wi, wu, sems = refs
-    loads, base = [], 0
-    for group, (held, _), target in zip(groups, sources, (wi, wu), strict=True):
-        loads += group.copies(held, me_ref, target, sems, base)
-        base += group.count()
+def fill_body(group, me_ref, *refs):
+    held, near = refs[: len(group.held)], refs[len(group.held) : len(group.held) + len(group.arrays)]
+    target, sems = refs[-2:]
+    loads = group.copies(held, me_ref, target, sems, 0)
     start_all(loads)
-    for group, (_, near), target in zip(groups, sources, (wi, wu), strict=True):
-        group.fill(near, me_ref, target)
+    group.fill(near, me_ref, target)
     wait_all(loads)
 
 
-def fill(groups, me, width, blocks):
-    operands, specs = [], []
-    for g in groups:
-        operands += [*far_off(*g.held), *stay(*g.arrays)]
-        specs += [HB] * len(g.held) + [VM] * len(g.arrays)
-    return pl.pallas_call(
-        functools.partial(fill_body, groups),
-        out_shape=(local(blocks, width, width), local(blocks * width, width)),
-        in_specs=[SM] + specs,
-        out_specs=[VM] * 2,
-        scratch_shapes=[pltpu.SemaphoreType.DMA((sum(g.count() for g in groups),))],
+def fill(group, me, *dims):
+    return pl.pallas_call(
+        functools.partial(fill_body, group),
+        out_shape=local(*dims),
+        in_specs=[SM] + [HB] * len(group.held) + [VM] * len(group.arrays),
+        out_specs=VM,
+        scratch_shapes=[pltpu.SemaphoreType.DMA((group.count(),))],
         compiler_params=limit(2),
-        cost_estimate=pl.CostEstimate(flops=0, bytes_accessed=9_000_000, transcendentals=0),
+        cost_estimate=FREE,
         name="fill",
-    )(me, *operands)
+    )(me, *far_off(*group.held), *stay(*group.arrays))
 
 
 def middle_forward_body(
@@ -406,7 +434,7 @@
         in_specs=[SM] + [VM] * 8,
         out_specs=[VM] * 9,
         compiler_params=limit(12),
-        cost_estimate=pl.CostEstimate(flops=12_000_000_000, bytes_accessed=30_000_000, transcendentals=3_200_000),
+        cost_estimate=FREE,
         name="middle_forward",
     )(length, x, *stay(att), cot, *stay(vec, ib, wa, wi, wu))
 
@@ -463,7 +491,7 @@
         in_specs=[VM] * 9,
         out_specs=[VM] * 6,
         compiler_params=limit(10),
-        cost_estimate=pl.CostEstimate(flops=9_000_000_000, bytes_accessed=25_000_000, transcendentals=0),
+        cost_estimate=FREE,
         name="middle_backward",
     )(*stay(low, ssg, slope, norm, rstd, vec, wa, wi, wu))
 
@@ -491,7 +519,7 @@
         in_specs=[VM] * 3,
         out_specs=VM,
         compiler_params=limit(8),
-        cost_estimate=pl.CostEstimate(flops=4_000_000_000, bytes_accessed=10_000_000, transcendentals=0),
+        cost_estimate=FREE,
         name="input_grad",
     )(*stay(g, fsg, wa))
 
@@ -501,11 +529,12 @@
 
 def weight_grad_body(kind, order, z_order, me_ref, left_ref, g_ref, *refs):
     sums, refs = (refs[:4], refs[4:]) if kind == "attend" else ((), refs)
-    outs, left = refs[:2], refs[2]
+    sent = len(order) if kind == "attend" else 1
+    outs, left = refs[: sent + 1], refs[sent + 1]
     i, z, c = me_ref[0], me_ref[1], me_ref[2]
     part = 96
     if kind == "attend":
-        extra = refs[3]
+        extra = refs[sent + 2]
         one, two, three, ib = (r[...] for r in sums)
         row = lax.broadcasted_iota(jnp.int32, one.shape, 0)
         every = jnp.where(row < 2, three, jnp.where(row < 5, two, one))
@@ -514,39 +543,50 @@
             extra[f, :, :part] = every[:, f * part : (f + 1) * part]
             extra[f, 0:1, 128 : 128 + 4 * part] = ib[f // 2 : f // 2 + 1, f % 2 * 4 * part : (f % 2 + 1) * 4 * part]
 
-    for c_at, out_ref in zip((1 - c, c), outs, strict=True):
-
-        def block_step(spot, carry):
-            block = i ^ pick(order, spot)
+    def one_block(spot, away, c_at, out_ref):
+        block = i ^ away
+        for n, j in enumerate(z_order):
+            f_at = 2 * (z ^ j) + c_at
+            if kind == "outer":
+                rows = left_ref[aligned_rows(f_at * 384 + block * 96, 96), :]
+            elif kind == "inner":
+                rows = left_ref[aligned_rows(f_at * 96, 96), :]
+            else:
+                rows = left_ref[block // 3, aligned_rows(f_at * 96, 96), :]
+            left[n * 96 : (n + 1) * 96, :] = rows
+        right = g_ref[...] if kind == "outer" else g_ref[block]
+        grads = dot_nn(left[...], right).reshape(4, 96, 768).astype(BF16)
+        if kind == "outer":
+            out_ref[:, spot] = grads
+        else:
+            out_ref[spot, :, :96, :] = grads
+        if kind == "attend":
             for n, j in enumerate(z_order):
-                f_at = 2 * (z ^ j) + c_at
-                if kind == "outer":
-                    rows = left_ref[aligned_rows(f_at * 384 + block * 96, 96), :]
-                elif kind == "inner":
-                    rows = left_ref[aligned_rows(f_at * 96, 96), :]
-                else:
-                    rows = left_ref[block // 3, aligned_rows(f_at * 96, 96), :]
-                left[n * 96 : (n + 1) * 96, :] = rows
-            right = g_ref[...] if kind == "outer" else g_ref[block]
-            out_ref[spot, :, :96, :] = dot_nn(left[...], right).reshape(4, 96, 768).astype(BF16)
-            if kind == "attend":
-                for n, j in enumerate(z_order):
-                    out_ref[spot, n, 96:104, :] = extra[2 * (z ^ j) + c_at].astype(BF16)
-            return carry
-
-        lax.fori_loop(0, 4, block_step, 0)
+                out_ref[spot, n, 96:104, :] = extra[2 * (z ^ j) + c_at].astype(BF16)
+
+    def block_step(c_at, out_ref, spot, carry):
+        one_block(spot, pick(order, spot), c_at, out_ref)
+        return carry
+
+    if kind == "attend":
+        for spot, away in enumerate(order):
+            one_block(0, away, 1 - c, outs[spot])
+    else:
+        lax.fori_loop(0, 4, functools.partial(block_step, 1 - c, outs[0]), 0)
+    lax.fori_loop(0, 4, functools.partial(block_step, c, outs[-1]), 0)
 
 
 def weight_grad(kind, order, z_order, me, left, g, sums=()):
     rows = 104 if kind == "attend" else 96
+    sent = (local(1, 4, rows, 768),) * 4 if kind == "attend" else (local(4, 4, rows, 768),)
     return pl.pallas_call(
         functools.partial(weight_grad_body, kind, order, z_order),
-        out_shape=(local(4, 4, rows, 768),) * 2,
+        out_shape=sent + (local(4, 4, rows, 768),),
         in_specs=[SM] + [VM] * (2 + len(sums)),
-        out_specs=[VM] * 2,
+        out_specs=[VM] * (len(sent) + 1),
         scratch_shapes=[pltpu.VMEM((384, left.shape[-1]), BF16)] + [pltpu.VMEM((8, 8, 768), F32)] * (kind == "attend"),
         compiler_params=limit(6),
-        cost_estimate=pl.CostEstimate(flops=4_000_000_000, bytes_accessed=6_000_000, transcendentals=0),
+        cost_estimate=FREE,
         name=f"weight_grad_{kind}",
     )(me, *stay(left, g, *sums))
 
@@ -591,7 +631,7 @@
         + [pltpu.VMEM(v.shape, BF16) for v in vectors]
         + [pltpu.SemaphoreType.DMA((12,))],
         compiler_params=limit(2),
-        cost_estimate=pl.CostEstimate(flops=0, bytes_accessed=1_000_000, transcendentals=0),
+        cost_estimate=FREE,
         name="prepare",
     )(me, *far_off(*vectors, *weights))
 
@@ -607,7 +647,7 @@
         out_specs=HB,
         input_output_aliases={0: 0},
         compiler_params=limit(1),
-        cost_estimate=pl.CostEstimate(flops=0, bytes_accessed=0, transcendentals=0),
+        cost_estimate=FREE,
         name="after",
     )(value, *others)
 
@@ -620,27 +660,102 @@
     return [swap(piece, "fsdp", fsdp, 2 * j) for j in (1, 2, 3)]
 
 
-def gather_plane(mine, dp):
-    over_x = swap(mine, "dp", dp, 1)
-    over_y = swap(mine, "dp", dp, 2)
-    return over_x, over_y
-
-
-def total(*terms):
-    result = terms[0].astype(F32)
-    for term in terms[1:]:
-        result = result + term.astype(F32)
-    return result.astype(BF16)
-
-
-def scatter_z(value, fsdp):
-    got = swap(value[2:], "fsdp", fsdp, 2)
-    onward = swap(total(value[1], got[1]), "fsdp", fsdp, 4)
-    return total(value[0], got[0], onward)
-
-
-def direct_z(value, fsdp):
-    return total(value[0], *[swap(value[j], "fsdp", fsdp, 2 * j) for j in (1, 2, 3)])
+def combine(*outs):
+    arrays = []
+    for _, _, *lists in outs:
+        for terms in lists:
+            arrays += [a for n, (a, _) in enumerate(terms) if not any(a is b for b in arrays)]
+
+    def find(array):
+        return next(n for n, b in enumerate(arrays) if b is array)
+
+    def body(*refs):
+        for out_ref, (lead, rows, *lists) in zip(refs[len(arrays) :], outs, strict=True):
+            size = rows // len(lists)
+
+            def tile(index):
+                for n, terms in enumerate(lists):
+                    if len(terms) == 1:
+                        value = refs[find(terms[0][0])][terms[0][1](*index)]
+                    else:
+                        value = sum(refs[find(array)][at(*index)].astype(F32) for array, at in terms).astype(BF16)
+                    out_ref[(*index, slice(n * size, (n + 1) * size), slice(None))] = value
+
+            def step(front, last, carry):
+                tile((*front, last))
+                return carry
+
+            if not lead:
+                tile(())
+            elif len(lead) == 1:
+                lax.fori_loop(0, lead[0], functools.partial(step, ()), 0)
+            else:
+                for front in range(lead[0]):
+                    lax.fori_loop(0, lead[1], functools.partial(step, (front,)), 0)
+
+    return pl.pallas_call(
+        body,
+        out_shape=tuple(local(*lead, rows, 768) for lead, rows, *_ in outs),
+        in_specs=[VM] * len(arrays),
+        out_specs=[VM] * len(outs),
+        compiler_params=limit(2),
+        cost_estimate=FREE,
+        name="combine",
+    )(*stay(*arrays))
+
+
+def stack_three(parts):
+    rows = parts[0].shape[0]
+
+    def body(*refs):
+        for n in range(3):
+            refs[3][n] = refs[n][...]
+
+    return pl.pallas_call(
+        body,
+        out_shape=local(3, rows, 768),
+        in_specs=[VM] * 3,
+        out_specs=VM,
+        compiler_params=limit(2),
+        cost_estimate=FREE,
+        name="stack_three",
+    )(*stay(*parts))
+
+
+def halves(over_x, over_y):
+    return (
+        combine(((3,), 48, [(over_x, lambda n: (n, slice(0, 48)))]))[0],
+        combine(((3,), 48, [(over_y, lambda n: (n, slice(48, 96)))]))[0],
+    )
+
+
+def first_sum(kept, got):
+    at = lambda a, b: (2 + a, b)
+    return combine(((2, 4), 96, [(kept, at), (got, at)]))[0]
+
+
+def second_sum(kept, got, over):
+    here, there = (lambda b: (1, b)), (lambda b: (1, b))
+    return combine(((4,), 96, [(kept, here), (got, here), (over, there)]))[0]
+
+
+def finish(terms, beside):
+    def body(*refs):
+        terms, (beside_ref, own_ref, small_ref) = refs[:-3], refs[-3:]
+        value = sum(r[...].astype(F32) for r in terms)
+        own_ref[:96, :] = value[:96].astype(BF16)
+        own_ref[96:, :] = beside_ref[...]
+        small_ref[...] = value[96:]
+
+    return pl.pallas_call(
+        body,
+        out_shape=(local(192, 768), local(8, 768, dtype=F32)),
+        in_specs=[VM] * (len(terms) + 1),
+        out_specs=[VM] * 2,
+        compiler_params=limit(2),
+        cost_estimate=FREE,
+        name="finish",
+    )(*stay(*terms, beside))
 
 
 def spread(value, dp):
@@ -691,56 +806,57 @@
         mine = (query_weight, key_weight, value_weight, output_weight)
         piece_a, piece_m = prepare(me, small, mine + (inner_weight, outer_weight))
         z_a = gather_z(piece_a, fsdp)
-        theirs = tuple(swap(w, "fsdp", fsdp, 1) for w in mine + (piece_a,))
-        mine_a = jnp.stack(z_a)
-        plane_a = gather_plane(mine_a, dp)
-        z_m = gather_z(after(piece_m, mine_a), fsdp)
-        parts_a = (plane_a[0][:, :48], plane_a[1][:, 48:96])
+        z_m = gather_z(piece_m, fsdp)
+        mine_a = stack_three(z_a)
+        plane_a = (swap(mine_a, "dp", dp, 1), swap(mine_a, "dp", dp, 2))
+        parts_a = halves(*plane_a)
         rest_a = (swap(parts_a[0], "dp", dp, 2), swap(parts_a[1], "dp", dp, 1))
-        near_a = (mine_a,) + plane_a + rest_a
-        far_a = tuple(swap(w, "fsdp", fsdp, 1) for w in near_a)
-        z_m[0] = after(z_m[0], *parts_a)
-        mine_m = jnp.stack(z_m)
-        plane_m = gather_plane(mine_m, dp)
-        inner_other = swap(inner_weight, "fsdp", fsdp, 1)
-        outer_other = swap(outer_weight, "fsdp", fsdp, 1)
-
-        def far_at(base, row, halves):
-            return [[(base + n, row, 96, 0)] for n in range(3)] + [[(base + n, 0, rows, off) for n, rows, off in halves]]
-
-        split = ((3, 48, 0), (4, 48, 48))
+        z_m[0] = after(z_m[0], *rest_a)
+        mine_m = stack_three(z_m)
+        plane_m = (swap(mine_m, "dp", dp, 1), swap(mine_m, "dp", dp, 2))
+        near_a = bundle(1, mine, ((((0, 0)),),) * 4, (after(mine_a, mine_m),) + plane_a + (piece_a,))
+        far_a = (swap(near_a, "fsdp", fsdp, 1),) + tuple(swap(v, "fsdp", fsdp, 1) for v in rest_a)
+
+        def far_at(base, row=0):
+            return [[(base + n, 0, row, 96, 0)] for n in range(3)]
+
         group_a = Pieces(
             mine,
-            theirs + near_a + far_a + (piece_a,),
+            (mine_a,) + plane_a + rest_a + far_a + (piece_a,),
             [(n, 0, 0) for n in range(4)],
-            [(n, 0, 0) for n in range(4)],
-            far_at(5, 0, split),
-            far_at(10, 0, split),
+            [(5, n) for n in range(4)],
+            far_at(0) + [[(3, 0, 0, 48, 0), (4, 0, 0, 48, 48)]],
+            [[(5, 4 + 3 * n, 0, 96, 0)] for n in range(3)] + [[(6, 0, 0, 48, 0), (7, 0, 0, 48, 48)]],
             True,
-            (15, 4),
+            (8, 0, 5),
         )
         x = tokens.reshape(seq, width)
         q, k, v, att, left_a, lse, wa, vec, ib = attend_forward(group_a, fsdp, blocks, me, lengths, after(x, mine_m))
         plane_m = (after(plane_m[0], att), after(plane_m[1], att))
-        rest_m = (swap(plane_m[0][:, :96], "dp", dp, 2), swap(plane_m[1][:, 96:], "dp", dp, 1))
-        near_m = (mine_m,) + plane_m + rest_m
-        far_m = tuple(swap(w, "fsdp", fsdp, 1) for w in near_m)
+        parts_m = (
+            combine(((3,), 96, [(plane_m[0], lambda n: (n, slice(0, 96)))]))[0],
+            combine(((3,), 96, [(plane_m[1], lambda n: (n, slice(96, 192)))]))[0],
+        )
+        rest_m = (swap(parts_m[0], "dp", dp, 2), swap(parts_m[1], "dp", dp, 1))
+        spots = (tuple((0, 768 * n) for n in range(4)), tuple((96 * n, 0) for n in range(4)))
+        near_m = bundle(2, (inner_weight, outer_weight), spots, (mine_m,) + plane_m)
+        far_m = (swap(near_m, "fsdp", fsdp, 1),) + tuple(swap(v, "fsdp", fsdp, 1) for v in rest_m)
         group_i = Pieces(
             (inner_weight,),
-            (inner_other,) + near_m[:4] + far_m[:4],
+            (mine_m,) + plane_m + (rest_m[0], far_m[0], far_m[1]),
             [(0, 0, 768 * n) for n in range(4)],
-            [(0, 0, 768 * n) for n in range(4)],
-            far_at(1, 0, ((3, 96, 0),)),
-            far_at(5, 0, ((3, 96, 0),)),
+            [(4, n) for n in range(4)],
+            far_at(0) + [[(3, 0, 0, 96, 0)]],
+            [[(4, 8 + 6 * n, 0, 96, 0)] for n in range(3)] + [[(5, 0, 0, 96, 0)]],
             True,
         )
         group_u = Pieces(
             (outer_weight,),
-            (outer_other,) + near_m[:3] + near_m[4:] + far_m[:3] + far_m[4:],
+            (mine_m,) + plane_m + (rest_m[1], far_m[0], far_m[2]),
             [(0, 96 * n, 0) for n in range(4)],
-            [(0, 96 * n, 0) for n in range(4)],
-            far_at(1, 96, ((3, 96, 0),)),
-            far_at(5, 96, ((3, 96, 0),)),
+            [(4, 4 + n) for n in range(4)],
+            far_at(0, 96) + [[(3, 0, 0, 96, 0)]],
+            [[(4, 11 + 6 * n, 0, 96, 0)] for n in range(3)] + [[(5, 0, 0, 96, 0)]],
             False,
         )
     else:
@@ -758,50 +874,102 @@
         q, k, v, att, left_a, lse, wa, vec, ib = attend_forward(group_a, fsdp, blocks, me, lengths, x)
 
     cot = cotangent.reshape(seq, width)
-    wi, wu = fill((group_i, group_u), me, width, blocks)
+    wi = fill(group_i, me, blocks, width, width)
+    wu = fill(group_u, me, blocks * width, width)
     out, ssg, low, act_t, slope, norm, rstd, hid_t, sum_one = middle_forward(lengths, x, att, cot, vec, ib, wa, wi, wu)
     pairs = width // 128
     attend = functools.partial(attend_backward, length=lengths, q=q, k=k, v=v, lse=lse)
     if direct:
-        sent_u, kept_u = weight_grad("outer", (1, 3, 0, 2), Z_ORDER, me, act_t, low)
+        sent_u, kept_u = weight_grad("outer", (0, 1, 2, 3), Z_ORDER, me, act_t, low)
         got_u = swap(sent_u, "fsdp", fsdp, 1)
         low = after(low, sent_u)
     igl, fsg, branch, att_g, ib_sum, sum_two = middle_backward(low, ssg, slope, norm, rstd, vec, wa, wi, wu)
     if direct:
-        first_u = total(kept_u[:2], got_u[:2])
-        over_u = swap(first_u, "dp", dp, 1)
-        sent_i, kept_i = weight_grad("inner", (2, 3, 0, 1), Z_ORDER, me, hid_t, after(igl, first_u))
+        first_u = first_sum(kept_u, got_u)
+        over_u = swap(first_u, "fsdp", fsdp, 2)
+        sent_i, kept_i = weight_grad("inner", (0, 1, 2, 3), Z_ORDER, me, hid_t, after(igl, first_u))
         got_i = swap(sent_i, "fsdp", fsdp, 1)
         half = attend(0, pairs // 2, do=after(att_g, sent_i), branch=branch)
-        first_i = total(kept_i[:2], got_i[:2])
-        over_i = swap(first_i, "dp", dp, 2)
-        g, sum_three = attend(pairs // 2, pairs, do=after(att_g, first_i), branch=branch, before=half)
+        got_i = after(got_i, half[0])
+        upper, lower = slice(0, 48), slice(48, 96)
+        (first_x,) = combine(((2, 4), 48, [(v, lambda a, b: (2 * a + 1, b, upper)) for v in (kept_i, got_i)]))
+        (first_y,) = combine(((2, 4), 48, [(v, lambda a, b: (a + 2, b, lower)) for v in (kept_i, got_i)]))
+        over_x, over_y = swap(first_x, "dp", dp, 1), swap(first_y, "dp", dp, 2)
+        do = after(att_g, first_x, first_y)
+        g, sum_three = attend(pairs // 2, pairs, do=do, branch=branch, before=half)
     else:
         g, sum_three = attend(0, pairs, do=att_g, branch=branch)
         in_grad = input_grad(g, fsg, wa)
 
     if direct:
-        sent_a, kept_a = weight_grad(
-            "attend", (0, 1, 2, 3), (0, 1, 2, 3), me, left_a, g, (sum_one, sum_two, sum_three, ib_sum)
+        *sent_a, kept_a = weight_grad(
+            "attend", (1, 2, 3, 0), (0, 1, 2, 3), me, left_a, g, (sum_one, sum_two, sum_three, ib_sum)
         )
-        got_a = swap(sent_a, "fsdp", fsdp, 1)
-        in_grad = input_grad(g, after(fsg, sent_a), wa)
-        ready_a = [total(kept_a[m], got_a[m]) for m in (1, 2, 3)]
+        over_x = after(over_x, kept_a)
+        (second_x,) = combine(
+            ((4,), 48, [(v, lambda b: (2, b, upper)) for v in (kept_i, got_i)] + [(over_x, lambda b: (1, b))])
+        )
+        (second_y,) = combine(
+            ((4,), 48, [(v, lambda b: (1, b, lower)) for v in (kept_i, got_i)] + [(over_y, lambda b: (1, b))])
+        )
+        onward_x, onward_y = swap(second_x, "dp", dp, 2), swap(second_y, "dp", dp, 1)
+        over_u = after(over_u, second_x, second_y)
+        second_u = second_sum(kept_u, got_u, over_u)
+        onward_u = swap(second_u, "fsdp", fsdp, 4)
+        sent_a[3] = after(sent_a[3], second_x)
+        got_a = [swap(v, "fsdp", fsdp, 1) for v in sent_a]
+        got_a[0] = after(got_a[0], second_u)
+        ready_a = [combine(((4,), 104, [(kept_a, lambda b, n=n: (n, b)), (got_a[n], lambda b: (0, b))]))[0] for n in range(4)]
         over_a = [swap(ready_a[m - 1], "dp", dp, m) for m in (1, 2, 3)]
-        over_u = after(over_u, *ready_a)
-        onward_u = swap(total(kept_u[3], got_u[3], over_u[1]), "dp", dp, 2)
-        onward_i = swap(total(kept_i[3], got_i[3], over_i[1]), "dp", dp, 1)
-        plane_u = total(kept_u[2], got_u[2], over_u[0], onward_u)
-        plane_i = total(kept_i[2], got_i[2], over_i[0], onward_i)
-        plane_m = jnp.concatenate([plane_u, plane_i], axis=1)
-        over_a[0] = after(over_a[0], plane_m)
-        own_a = direct_z(total(kept_a[0], got_a[0], *over_a), fsdp)
-        both = spread(scatter_z(plane_m, fsdp), dp)
-        small_own = own_a[96:104].astype(F32)
+        in_grad = input_grad(g, after(fsg, *ready_a), wa)
+
+        tile, front, here = (lambda b: (b,)), (lambda b: (0, b)), (lambda: ())
+
+        def plane_at(first):
+            def terms(rows, over, onward):
+                held = [(v, lambda b: (0, first + b, rows)) for v in (kept_i, got_i)]
+                return held + [(over, lambda b: (0, first + b)), (onward, lambda b: (first + b,))]
+
+            return (2,), 96, terms(upper, over_x, onward_x), terms(lower, over_y, onward_y)
+
+        onward_x = after(onward_x, in_grad)
+        keep_i, send_i = combine(plane_at(0), plane_at(2))
+        near_i = swap(send_i, "fsdp", fsdp, 2)
+
+        onward_u = after(onward_u, keep_i)
+        (line_u,) = combine(((4,), 96, [(kept_u, front), (got_u, front), (over_u, front), (onward_u, tile)]))
+        beside_u = swap(line_u, "dp", dp, 1)
+
+        near_i = after(near_i, line_u)
+        (next_i,) = combine(((), 96, [(keep_i, lambda: (1,)), (near_i, lambda: (1,))]))
+        last_i = swap(next_i, "fsdp", fsdp, 4)
+
+        over_a[0] = after(over_a[0], next_i)
+        whole_a = combine(
+            *[((), 104, [(ready_a[3], lambda j=j: (j,))] + [(v, lambda j=j: (j,)) for v in over_a]) for j in range(4)]
+        )
+        far_a = [swap(whole_a[j], "fsdp", fsdp, 2 * j) for j in (1, 2, 3)]
+
+        beside_u = after(beside_u, whole_a[0])
+        (pair_u,) = combine(((4,), 96, [(line_u, tile), (beside_u, lambda b: (b ^ 1,))]))
+        across_u = swap(pair_u, "dp", dp, 2)
+
+        last_i = after(last_i, pair_u)
+        (own_i,) = combine(((), 96, [(keep_i, lambda: (0,)), (near_i, lambda: (0,)), (last_i, here)]))
+
+        far_a[0] = after(far_a[0], own_i)
+        own, small_rows = finish((whole_a[0], *far_a), own_i)
+        every = spread(own, dp)
+        all_a = [v[:96] for v in every]
+        all_i = [v[96:] for v in every]
+
+        across_u = after(across_u, *every)
+        (all_u,) = combine(((4,), 96, [(pair_u, tile), (across_u, lambda b: (b ^ 2,))]))
+        small_own = small_rows
         small_grads = [small_own[n, :part] for n in range(8)] + [small_own[0, 128 : 128 + blocks * part]]
-        q_g, k_g, v_g, o_g = (w.astype(F32) for w in in_order(spread(own_a[:96], dp), i))
-        u_g = jnp.concatenate(in_order([w[:96] for w in both], i), axis=0).astype(F32)
-        i_g = jnp.concatenate(in_order([w[96:] for w in both], i), axis=1).astype(F32)
+        q_g, k_g, v_g, o_g = (w.astype(F32) for w in in_order(all_a, i))
+        i_g = jnp.concatenate(in_order(all_i, i), axis=1).astype(F32)
+        u_g = jnp.concatenate(in_order([all_u[n] for n in range(4)], i), axis=0).astype(F32)
     else:
         vec_sum = jnp.concatenate([sum_three[:2], sum_two[2:5], sum_one[5:8]])
         vec_sum = vec_sum.reshape(8, fsdp, part).transpose(1, 0, 2).reshape(fsdp, 8 * part)

time: 284 us -> 248 us (0.87)
  waiting for transfers between devices: 147 us -> 117 us
  other arithmetic: 12.8 us -> 4.79 us
  local copies, waits for them, and re-layouts: 10.2 us -> 2.69 us
  Pallas kernels: 69.1 us -> 76 us
    ppermute x52 -> x45, waiting for transfers between devices: 147 us -> 117 us  [swap(): return lax.ppermute(value, axis, [(n, n ^ mask) for n in range(size)])]
    convert_element_type x15 -> x3, other arithmetic: 12.2 us -> 3.08 us  [the longest x1 1.11 us: on_device(): i_g = jnp.concatenate(in_order(all_i, i), axis=1).astype(F32)]
    pallas_call x1 -> x28, Pallas kernels: 1.96 us -> 9.43 us  [the longest x2 3.42 us: fill(): pl.pallas_call(functools.partial(fill_body, group), out_shape=local(*dims...]
    unnamed x56 -> x9, local copies, waits for them, and re-layouts: 8.89 us -> 1.56 us
    ppermute x52 -> x45, starting transfers between devices: 43.1 us -> 45.6 us  [swap(): return lax.ppermute(value, axis, [(n, n ^ mask) for n in range(size)])]
  transfers between devices with their start and end apart: 52 -> 45, of which waited for: 23 -> 27; matrix products, arithmetic and copies ran while one was open for 4% -> 2% of each run, Pallas kernels for 11% -> 19%
where the time goes in v3:
time: 248 us; the launch traced here: 247 us
  waiting for transfers between devices  117 us (47%)
  Pallas kernels  76 us (31%)
  starting transfers between devices  45.6 us (18%)
  other arithmetic  4.79 us (2%)
  local copies, waits for them, and re-layouts  2.69 us (1%)
    ppermute x45, waiting for transfers between devices, swap(): return lax.ppermute(value, axis, [(n, n ^ mask) for n in range(size)])  117 us
    ppermute x45, starting transfers between devices, swap(): return lax.ppermute(value, axis, [(n, n ^ mask) for n in range(size)])  45.6 us
    pallas_call x1, Pallas kernels, middle_forward(): pl.pallas_call(middle_forward_body, out_shape=(shape(seq, width), local(s...  13.5 us
    pallas_call x2, Pallas kernels, attend_backward(): pl.pallas_call(functools.partial(attend_backward_body, first, last), out_...  12.7 us
    pallas_call x3, Pallas kernels, weight_grad(): pl.pallas_call(functools.partial(weight_grad_body, kind, order, z_order),...  12.7 us
    pallas_call x1, Pallas kernels, attend_forward(): pl.pallas_call(functools.partial(attend_forward_body, group, width // sha...  12.2 us
    pallas_call x1, Pallas kernels, middle_backward(): pl.pallas_call(middle_backward_body, out_shape=(local(blocks, seq, width)...  10.2 us
  transfers between devices with their start and end apart: 45, of which 27 were waited for; matrix products, arithmetic and copies ran while one was open for 2% of the time, Pallas kernels for 19%

profile of v3, /device:TPU:0, one launch (start us, length us, event | category | flops | bytes accessed | tf_op | source)
XLA Modules:
  0.0 247.5 jit_solution(3090464401946497876)
XLA Ops:
  8.1 3.9 %collective-permute-done.1.refs_0_ = bf16[104,768]{1,0:T(8,128)(2,1)S(1)} collective-permute-done((bf16[104,768]{1,0:T(8,128)(2,1)S(1)}, bf16[104,768]{1,0:T(8,128)(2,1)S(1)}, u32[]{:S(2)}, u32[]{:S(2)}) %collective-permute-start.1) | collective-permute-done | bytes 159776 | tf_op jit(solution)/shard_map/ppermute | solution.py:656
  12.0 8.3 %collective-permute-done.2.refs_1_ = bf16[104,768]{1,0:T(8,128)(2,1)S(1)} collective-permute-done((bf16[104,768]{1,0:T(8,128)(2,1)S(1)}, bf16[104,768]{1,0:T(8,128)(2,1)S(1)}, u32[]{:S(2)}, u32[]{:S(2)}) %collective-permute-start.2) | collective-permute-done | bytes 159776 | tf_op jit(solution)/shard_map/ppermute | solution.py:656
  39.9 9.6 %collective-permute-done.8.refs_1_ = bf16[192,768]{1,0:T(8,128)(2,1)S(1)} collective-permute-done((bf16[192,768]{1,0:T(8,128)(2,1)S(1)}, bf16[192,768]{1,0:T(8,128)(2,1)S(1)}, u32[]{:S(2)}, u32[]{:S(2)}) %collective-permute-start.8) | collective-permute-done | bytes 294944 | tf_op jit(solution)/shard_map/ppermute | solution.py:656
  55.6 12.2 %attend_forward.1 = (bf16[512,768]{1,0:T(8,128)(2,1)S(1)}, bf16[512,768]{1,0:T(8,128)(2,1)S(1)}, bf16[512,768]{1,0:T(8,128)(2,1)S(1)}, bf16[512,768]{1,0:T(8,128...) custom-call(s32[4]{0:T(128)S(1)} %pad_add_fusion.me_ref, ...), custom_call_target="tpu_custom_call" | custom-call | tf_op jit(solution)/shard_map/attend_forward/pallas_call | solution.py:249
  67.8 5.1 %collective-permute-done.13.refs_0_ = bf16[3,192,768]{2,1,0:T(8,128)(2,1)S(1)} collective-permute-done((bf16[3,192,768]{2,1,0:T(8,128)(2,1)S(1)}, bf16[3,192,768]{2,1,0:T(8,128)(2,1)S(1)}, u32[]{:S(2)}, u32[]{:S(2)}) %collective-permute-start.13) | collective-permute-done | bytes 884768 | tf_op jit(solution)/shard_map/ppermute | solution.py:656
  76.9 10.5 %collective-permute-done.15.refs_4_ = bf16[3,96,768]{2,1,0:T(8,128)(2,1)S(1)} collective-permute-done((bf16[3,96,768]{2,1,0:T(8,128)(2,1)S(1)}, bf16[3,96,768]{2,1,0:T(8,128)(2,1)S(1)}, u32[]{:S(2)}, u32[]{:S(2)}) %collective-permute-start.15) | collective-permute-done | bytes 442400 | tf_op jit(solution)/shard_map/ppermute | solution.py:656
  92.7 13.5 %middle_forward.1 = (bf16[512,768]{1,0:T(8,128)(2,1)}, f32[512,768]{1,0:T(8,128)S(1)}, bf16[512,768]{1,0:T(8,128)(2,1)S(1)}, bf16[3072,512]{1,0:T(8,128)(2,1)S(1...) custom-call(s32[1]{0:T(128)S(6)} %copy.85.len_ref, ...), custom_call_target="tpu_custom_call" | custom-call | tf_op jit(solution)/shard_map/middle_forward/pallas_call | solution.py:421
  106.2 4.3 %weight_grad_outer.1 = (bf16[4,4,96,768]{3,2,1,0:T(8,128)(2,1)S(1)}, bf16[4,4,96,768]{3,2,1,0:T(8,128)(2,1)S(1)}) custom-call(s32[4]{0:T(128)S(1)} %pad_add_fusion.me_ref, bf16[3072,512]{1,0:T(8,128)(2,1)S(1)} %get-tuple-element.75.left_ref, bf16[512,768]{1,0:T(8,128)(2,1)S(1)} %get-tuple-element.74.g_ref.refs_0_), custom_call_target="tpu_custom_call" | custom-call | tf_op jit(solution)/shard_map/weight_grad_outer/pallas_call | solution.py:582
  110.8 10.2 %middle_backward.1 = (bf16[4,512,768]{2,1,0:T(8,128)(2,1)S(1)}, f32[512,768]{1,0:T(8,128)S(1)}, bf16[512,768]{1,0:T(8,128)(2,1)S(1)}, bf16[512,768]{1,0:T(8,128)...) custom-call(bf16[512,768]{1,0:T(8,128)(2,1)S(1)} %after.28.low_ref, f32[512,768]{1,0:T(8,128)S(1)} %get-tuple-element.77.ssg_ref, ...), custom_call_target="tpu_custom_call" | custom-call | tf_op jit(solution)/shard_map/middle_backward/pallas_call | solution.py:481
  121.3 4.5 %weight_grad_inner.1 = (bf16[4,4,96,768]{3,2,1,0:T(8,128)(2,1)S(1)}, bf16[4,4,96,768]{3,2,1,0:T(8,128)(2,1)S(1)}) custom-call(s32[4]{0:T(128)S(1)} %pad_add_fusion.me_ref, bf16[768,512]{1,0:T(8,128)(2,1)S(1)} %get-tuple-element.82.left_ref, bf16[4,512,768]{2,1,0:T(8,128)(2,1)S(1)} %after.29.g_ref), custom_call_target="tpu_custom_call" | custom-call | tf_op jit(solution)/shard_map/weight_grad_inner/pallas_call | solution.py:582
  126.3 3.7 %collective-permute-start.23 = (bf16[2,4,96,768]{3,2,1,0:T(8,128)(2,1)S(1)}, bf16[2,4,96,768]{3,2,1,0:T(8,128)(2,1)S(1)}, u32[]{:S(2)}, u32[]{:S(2)}) collective-permute-start(bf16[2,4,96,768]{3,2,1,0:T(8,128)(2,1)S(1)} %combine.25.refs_1_), channel_id=1, source_target_pairs={{0,2},{1,3},{2,0},{3,1},{4,6},{5,7},{6,4},{7,5},{8,10},{9,11},{10,... | collective-permute-start | bytes 3538952 | tf_op jit(solution)/shard_map/ppermute | solution.py:656
  130.1 6.5 %attend_backward.2 = (bf16[4,512,768]{2,1,0:T(8,128)(2,1)S(1)}, f32[8,768]{1,0:T(8,128)S(1)}) custom-call(s32[1]{0:T(128)S(6)} %copy.85.len_ref, bf16[512,768]{1,0:T(8,128)(2,1)S(1)} %get-tuple-element.71.q_ref, bf16[512,768]{1,0:T(8,128)(2,1)S(1)} %get-tuple-element.72.k_ref, bf16[512,768]{1,0:T(8,128)(2,1)S(1)} %get-tuple-element.73.v_ref, ...), custom_call_target="tpu_custom_call" | custom-call | tf_op jit(solution)/shard_map/attend_backward/pallas_call | solution.py:309
  139.0 6.3 %attend_backward.3 = (bf16[4,512,768]{2,1,0:T(8,128)(2,1)S(1)}, f32[8,768]{1,0:T(8,128)S(1)}) custom-call(s32[1]{0:T(128)S(6)} %copy.85.len_ref, bf16[512,768]{1,0:T(8,128)(2,1)S(1)} %get-tuple-element.71.q_ref, bf16[512,768]{1,0:T(8,128)(2,1)S(1)} %get-tuple-element.72.k_ref, ...), custom_call_target="tpu_custom_call", output_to_operand_aliasing={{0}: (7, {}), {1}: (8, {})} | custom-call | tf_op jit(solution)/shard_map/attend_backward/pallas_call | solution.py:309
  145.3 3.9 %weight_grad_attend.1 = (bf16[1,4,104,768]{3,2,1,0:T(8,128)(2,1)S(1)}, bf16[1,4,104,768]{3,2,1,0:T(8,128)(2,1)S(1)}, bf16[1,4,104,768]{3,2,1,0:T(8,128)(2,1)S(1)...) custom-call(s32[4]{0:T(128)S(1)} %pad_add_fusion.me_ref, ...), custom_call_target="tpu_custom_call" | custom-call | tf_op jit(solution)/shard_map/weight_grad_attend/pallas_call | solution.py:582
  162.7 4.8 %collective-permute-done.30.refs_0_ = bf16[4,48,768]{2,1,0:T(8,128)(2,1)S(1)} collective-permute-done((bf16[4,48,768]{2,1,0:T(8,128)(2,1)S(1)}, bf16[4,48,768]{2,1,0:T(8,128)(2,1)S(1)}, u32[]{:S(2)}, u32[]{:S(2)}) %collective-permute-start.30) | collective-permute-done | bytes 294944 | tf_op jit(solution)/shard_map/ppermute | solution.py:656
  170.6 3.4 %input_grad.1.refs_1_ = f32[512,768]{1,0:T(8,128)} custom-call(bf16[4,512,768]{2,1,0:T(8,128)(2,1)S(1)} %get-tuple-element.91.g_ref, f32[512,768]{1,0:T(8,128)S(1)} %after.37.fsg_ref, bf16[4,768,768]{2,1,0:T(8,128)(2,1)S(1)} %get-tuple-element.69.wa.w_ref), custom_call_target="tpu_custom_call" | custom-call | tf_op jit(solution)/shard_map/input_grad/pallas_call | solution.py:516
  175.8 9.2 %collective-permute-done.33.refs_0_ = bf16[4,96,768]{2,1,0:T(8,128)(2,1)S(1)} collective-permute-done((bf16[4,96,768]{2,1,0:T(8,128)(2,1)S(1)}, bf16[4,96,768]{2,1,0:T(8,128)(2,1)S(1)}, u32[]{:S(2)}, u32[]{:S(2)}) %collective-permute-start.33) | collective-permute-done | bytes 589856 | tf_op jit(solution)/shard_map/ppermute | solution.py:656
  186.9 7.7 %collective-permute-done.32.refs_0_ = bf16[2,96,768]{2,1,0:T(8,128)(2,1)S(1)} collective-permute-done((bf16[2,96,768]{2,1,0:T(8,128)(2,1)S(1)}, bf16[2,96,768]{2,1,0:T(8,128)(2,1)S(1)}, u32[]{:S(2)}, u32[]{:S(2)}) %collective-permute-start.32) | collective-permute-done | bytes 294944 | tf_op jit(solution)/shard_map/ppermute | solution.py:656
  194.7 3.7 %collective-permute-done.35.refs_3_ = bf16[4,104,768]{2,1,0:T(8,128)(2,1)S(1)} collective-permute-done((bf16[4,104,768]{2,1,0:T(8,128)(2,1)S(1)}, bf16[4,104,768]{2,1,0:T(8,128)(2,1)S(1)}, u32[]{:S(2)}, u32[]{:S(2)}) %collective-permute-start.35) | collective-permute-done | bytes 639008 | tf_op jit(solution)/shard_map/ppermute | solution.py:656
  203.1 4.6 %collective-permute-done.38.refs_0_ = bf16[4,96,768]{2,1,0:T(8,128)(2,1)S(1)} collective-permute-done((bf16[4,96,768]{2,1,0:T(8,128)(2,1)S(1)}, bf16[4,96,768]{2,1,0:T(8,128)(2,1)S(1)}, u32[]{:S(2)}, u32[]{:S(2)}) %collective-permute-start.38) | collective-permute-done | bytes 589856 | tf_op jit(solution)/shard_map/ppermute | solution.py:656
  207.9 10.5 %collective-permute-done.37.refs_0_ = bf16[96,768]{1,0:T(8,128)(2,1)S(1)} collective-permute-done((bf16[96,768]{1,0:T(8,128)(2,1)S(1)}, bf16[96,768]{1,0:T(8,128)(2,1)S(1)}, u32[]{:S(2)}, u32[]{:S(2)}) %collective-permute-start.37) | collective-permute-done | bytes 147488 | tf_op jit(solution)/shard_map/ppermute | solution.py:656
  223.8 5.7 %collective-permute-done.43.refs_4_ = bf16[192,768]{1,0:T(8,128)(2,1)S(1)} collective-permute-done((bf16[192,768]{1,0:T(8,128)(2,1)S(1)}, bf16[192,768]{1,0:T(8,128)(2,1)S(1)}, u32[]{:S(2)}, u32[]{:S(2)}) %collective-permute-start.43) | collective-permute-done | bytes 294944 | tf_op jit(solution)/shard_map/ppermute | solution.py:656
  229.5 4.1 %collective-permute-done.42.refs_3_ = bf16[192,768]{1,0:T(8,128)(2,1)S(1)} collective-permute-done((bf16[192,768]{1,0:T(8,128)(2,1)S(1)}, bf16[192,768]{1,0:T(8,128)(2,1)S(1)}, u32[]{:S(2)}, u32[]{:S(2)}) %collective-permute-start.42) | collective-permute-done | bytes 294944 | tf_op jit(solution)/shard_map/ppermute | solution.py:656
  237.1 9.0 %collective-permute-done.44.refs_0_ = bf16[4,96,768]{2,1,0:T(8,128)(2,1)S(1)} collective-permute-done((bf16[4,96,768]{2,1,0:T(8,128)(2,1)S(1)}, bf16[4,96,768]{2,1,0:T(8,128)(2,1)S(1)}, u32[]{:S(2)}, u32[]{:S(2)}) %collective-permute-start.44) | collective-permute-done | bytes 589856 | tf_op jit(solution)/shard_map/ppermute | solution.py:656
  (146 shorter events, 80.4 us)
Async XLA Ops:
  5.6 14.8 %collective-permute-start.2 = (bf16[104,768]{1,0:T(8,128)(2,1)S(1)}, bf16[104,768]{1,0:T(8,128)(2,1)S(1)}, u32[]{:S(2)}, u32[]{:S(2)}) collective-permute-start(bf16[104,768]{1,0:T(8,128)(2,1)S(1)} %get-tuple-element.65.refs_7_.refs_12_), channel_id=1, source_target_pairs={{0,4},{1,5},{2,6},{3,7},{4,0},{5,1},{6,2},{7,3},{8,12},{9,13},{10,... | collective-permute-start | bytes 479240 | tf_op jit(solution)/shard_map/ppermute | solution.py:656
  23.5 12.5 %collective-permute-start = (bf16[192,768]{1,0:T(8,128)(2,1)S(1)}, bf16[192,768]{1,0:T(8,128)(2,1)S(1)}, u32[]{:S(2)}, u32[]{:S(2)}) collective-permute-start(bf16[192,768]{1,0:T(8,128)(2,1)S(1)} %get-tuple-element.64), channel_id=1, source_target_pairs={{0,2},{1,3},{2,0},{3,1},{4,6},{5,7},{6,4},{7,5},{8,10},{9,11},{10,... | collective-permute-start | bytes 884744 | tf_op jit(solution)/shard_map/ppermute | solution.py:656
  26.0 23.5 %collective-permute-start.8 = (bf16[192,768]{1,0:T(8,128)(2,1)S(1)}, bf16[192,768]{1,0:T(8,128)(2,1)S(1)}, u32[]{:S(2)}, u32[]{:S(2)}) collective-permute-start(bf16[192,768]{1,0:T(8,128)(2,1)S(1)} %get-tuple-element.64), channel_id=1, source_target_pairs={{0,4},{1,5},{2,6},{3,7},{4,0},{5,1},{6,2},{7,3},{8,12},{9,13},{10,... | collective-permute-start | bytes 884744 | tf_op jit(solution)/shard_map/ppermute | solution.py:656
  27.0 22.5 %collective-permute-start.9 = (bf16[192,768]{1,0:T(8,128)(2,1)S(1)}, bf16[192,768]{1,0:T(8,128)(2,1)S(1)}, u32[]{:S(2)}, u32[]{:S(2)}) collective-permute-start(bf16[192,768]{1,0:T(8,128)(2,1)S(1)} %get-tuple-element.64), channel_id=1, source_target_pairs={{0,6},{1,7},{2,4},{3,5},{4,2},{5,3},{6,0},{7,1},{8,14},{9,15},{10,... | collective-permute-start | bytes 884744 | tf_op jit(solution)/shard_map/ppermute | solution.py:656
  50.9 22.1 %collective-permute-start.13 = (bf16[3,192,768]{2,1,0:T(8,128)(2,1)S(1)}, bf16[3,192,768]{2,1,0:T(8,128)(2,1)S(1)}, u32[]{:S(2)}, u32[]{:S(2)}) collective-permute-start(bf16[3,192,768]{2,1,0:T(8,128)(2,1)S(1)} %stack_three.3.refs_1_.refs_2_), channel_id=1, source_target_pairs={{0,8},{8,0},{16,24},{24,16},{1,9},{9,1},{17,25},{25,17},{2,10},{10... | collective-permute-start | bytes 2654216 | tf_op jit(solution)/shard_map/ppermute | solution.py:656
  51.5 21.7 %collective-permute-start.14 = (bf16[3,192,768]{2,1,0:T(8,128)(2,1)S(1)}, bf16[3,192,768]{2,1,0:T(8,128)(2,1)S(1)}, u32[]{:S(2)}, u32[]{:S(2)}) collective-permute-start(bf16[3,192,768]{2,1,0:T(8,128)(2,1)S(1)} %stack_three.3.refs_1_.refs_2_), channel_id=1, source_target_pairs={{0,16},{8,24},{16,0},{24,8},{1,17},{9,25},{17,1},{25,9},{2,18},{10... | collective-permute-start | bytes 2654216 | tf_op jit(solution)/shard_map/ppermute | solution.py:656
  74.7 14.5 %collective-permute-start.16 = (bf16[26,96,768]{2,1,0:T(8,128)(2,1)S(1)}, bf16[26,96,768]{2,1,0:T(8,128)(2,1)S(1)}, u32[]{:S(2)}, u32[]{:S(2)}) collective-permute-start(bf16[26,96,768]{2,1,0:T(8,128)(2,1)S(1)} %bundle.3), channel_id=1, source_target_pairs={{0,1},{1,0},{2,3},{3,2},{4,5},{5,4},{6,7},{7,6},{8,9},{9,8},{10,11... | collective-permute-start | bytes 11501576 | tf_op jit(solution)/shard_map/ppermute | solution.py:656
  74.8 12.6 %collective-permute-start.15 = (bf16[3,96,768]{2,1,0:T(8,128)(2,1)S(1)}, bf16[3,96,768]{2,1,0:T(8,128)(2,1)S(1)}, u32[]{:S(2)}, u32[]{:S(2)}) collective-permute-start(bf16[3,96,768]{2,1,0:T(8,128)(2,1)S(1)} %combine.23), channel_id=1, source_target_pairs={{0,16},{8,24},{16,0},{24,8},{1,17},{9,25},{17,1},{25,9},{2,18},{10... | collective-permute-start | bytes 1327112 | tf_op jit(solution)/shard_map/ppermute | solution.py:656
  126.3 30.0 %collective-permute-start.23 = (bf16[2,4,96,768]{3,2,1,0:T(8,128)(2,1)S(1)}, bf16[2,4,96,768]{3,2,1,0:T(8,128)(2,1)S(1)}, u32[]{:S(2)}, u32[]{:S(2)}) collective-permute-start(bf16[2,4,96,768]{3,2,1,0:T(8,128)(2,1)S(1)} %combine.25.refs_1_), channel_id=1, source_target_pairs={{0,2},{1,3},{2,0},{3,1},{4,6},{5,7},{6,4},{7,5},{8,10},{9,11},{10,... | collective-permute-start | bytes 3538952 | tf_op jit(solution)/shard_map/ppermute | solution.py:656
  136.7 15.2 %collective-permute-start.24 = (bf16[2,4,48,768]{3,2,1,0:T(8,128)(2,1)S(1)}, bf16[2,4,48,768]{3,2,1,0:T(8,128)(2,1)S(1)}, u32[]{:S(2)}, u32[]{:S(2)}) collective-permute-start(bf16[2,4,48,768]{3,2,1,0:T(8,128)(2,1)S(1)} %combine.26.refs_1_), channel_id=1, source_target_pairs={{0,8},{8,0},{16,24},{24,16},{1,9},{9,1},{17,25},{25,17},{2,10},{10... | collective-permute-start | bytes 1769480 | tf_op jit(solution)/shard_map/ppermute | solution.py:656
  138.5 14.9 %collective-permute-start.25 = (bf16[2,4,48,768]{3,2,1,0:T(8,128)(2,1)S(1)}, bf16[2,4,48,768]{3,2,1,0:T(8,128)(2,1)S(1)}, u32[]{:S(2)}, u32[]{:S(2)}) collective-permute-start(bf16[2,4,48,768]{3,2,1,0:T(8,128)(2,1)S(1)} %combine.27.refs_2_), channel_id=1, source_target_pairs={{0,16},{8,24},{16,0},{24,8},{1,17},{9,25},{17,1},{25,9},{2,18},{10... | collective-permute-start | bytes 1769480 | tf_op jit(solution)/shard_map/ppermute | solution.py:656
  153.3 14.7 %collective-permute-start.28 = (bf16[1,4,104,768]{3,2,1,0:T(8,128)(2,1)S(1)}, bf16[1,4,104,768]{3,2,1,0:T(8,128)(2,1)S(1)}, u32[]{:S(2)}, u32[]{:S(2)}) collective-permute-start(bf16[1,4,104,768]{3,2,1,0:T(8,128)(2,1)S(1)} %after.36), channel_id=1, source_target_pairs={{0,1},{1,0},{2,3},{3,2},{4,5},{5,4},{6,7},{7,6},{8,9},{9,8},{10,11... | collective-permute-start | bytes 1916936 | tf_op jit(solution)/shard_map/ppermute | solution.py:656
  156.5 28.5 %collective-permute-start.33 = (bf16[4,96,768]{2,1,0:T(8,128)(2,1)S(1)}, bf16[4,96,768]{2,1,0:T(8,128)(2,1)S(1)}, u32[]{:S(2)}, u32[]{:S(2)}) collective-permute-start(bf16[4,96,768]{2,1,0:T(8,128)(2,1)S(1)} %combine.30.refs_1_), channel_id=1, source_target_pairs={{0,4},{1,5},{2,6},{3,7},{4,0},{5,1},{6,2},{7,3},{8,12},{9,13},{10,... | collective-permute-start | bytes 1769480 | tf_op jit(solution)/shard_map/ppermute | solution.py:656
  160.1 15.4 %collective-permute-start.31 = (bf16[4,48,768]{2,1,0:T(8,128)(2,1)S(1)}, bf16[4,48,768]{2,1,0:T(8,128)(2,1)S(1)}, u32[]{:S(2)}, u32[]{:S(2)}) collective-permute-start(bf16[4,48,768]{2,1,0:T(8,128)(2,1)S(1)} %combine.29.refs_2_), channel_id=1, source_target_pairs={{0,8},{8,0},{16,24},{24,16},{1,9},{9,1},{17,25},{25,17},{2,10},{10... | collective-permute-start | bytes 884744 | tf_op jit(solution)/shard_map/ppermute | solution.py:656
  161.9 32.7 %collective-permute-start.29 = (bf16[4,104,768]{2,1,0:T(8,128)(2,1)S(1)}, bf16[4,104,768]{2,1,0:T(8,128)(2,1)S(1)}, u32[]{:S(2)}, u32[]{:S(2)}) collective-permute-start(bf16[4,104,768]{2,1,0:T(8,128)(2,1)S(1)} %combine.31.refs_1_), channel_id=1, source_target_pairs={{0,8},{8,0},{16,24},{24,16},{1,9},{9,1},{17,25},{25,17},{2,10},{10... | collective-permute-start | bytes 1916936 | tf_op jit(solution)/shard_map/ppermute | solution.py:656
  167.5 27.2 %collective-permute-start.34 = (bf16[4,104,768]{2,1,0:T(8,128)(2,1)S(1)}, bf16[4,104,768]{2,1,0:T(8,128)(2,1)S(1)}, u32[]{:S(2)}, u32[]{:S(2)}) collective-permute-start(bf16[4,104,768]{2,1,0:T(8,128)(2,1)S(1)} %combine.32.refs_2_), channel_id=1, source_target_pairs={{0,16},{8,24},{16,0},{24,8},{1,17},{9,25},{17,1},{25,9},{2,18},{10... | collective-permute-start | bytes 1916936 | tf_op jit(solution)/shard_map/ppermute | solution.py:656
  168.0 30.4 %collective-permute-start.35 = (bf16[4,104,768]{2,1,0:T(8,128)(2,1)S(1)}, bf16[4,104,768]{2,1,0:T(8,128)(2,1)S(1)}, u32[]{:S(2)}, u32[]{:S(2)}) collective-permute-start(bf16[4,104,768]{2,1,0:T(8,128)(2,1)S(1)} %combine.33.refs_3_), channel_id=1, source_target_pairs={{0,24},{8,16},{16,8},{24,0},{1,25},{9,17},{17,9},{25,1},{2,26},{10... | collective-permute-start | bytes 1916936 | tf_op jit(solution)/shard_map/ppermute | solution.py:656
  185.3 22.4 %collective-permute-start.38 = (bf16[4,96,768]{2,1,0:T(8,128)(2,1)S(1)}, bf16[4,96,768]{2,1,0:T(8,128)(2,1)S(1)}, u32[]{:S(2)}, u32[]{:S(2)}) collective-permute-start(bf16[4,96,768]{2,1,0:T(8,128)(2,1)S(1)} %combine.36.refs_1_.refs_0_), channel_id=1, source_target_pairs={{0,8},{8,0},{16,24},{24,16},{1,9},{9,1},{17,25},{25,17},{2,10},{10... | collective-permute-start | bytes 1769480 | tf_op jit(solution)/shard_map/ppermute | solution.py:656
  198.7 19.8 %collective-permute-start.36 = (bf16[104,768]{1,0:T(8,128)(2,1)S(1)}, bf16[104,768]{1,0:T(8,128)(2,1)S(1)}, u32[]{:S(2)}, u32[]{:S(2)}) collective-permute-start(bf16[104,768]{1,0:T(8,128)(2,1)S(1)} %get-tuple-element.106), channel_id=1, source_target_pairs={{0,2},{1,3},{2,0},{3,1},{4,6},{5,7},{6,4},{7,5},{8,10},{9,11},{10,... | collective-permute-start | bytes 479240 | tf_op jit(solution)/shard_map/ppermute | solution.py:656
  199.0 19.5 %collective-permute-start.39 = (bf16[104,768]{1,0:T(8,128)(2,1)S(1)}, bf16[104,768]{1,0:T(8,128)(2,1)S(1)}, u32[]{:S(2)}, u32[]{:S(2)}) collective-permute-start(bf16[104,768]{1,0:T(8,128)(2,1)S(1)} %get-tuple-element.107), channel_id=1, source_target_pairs={{0,4},{1,5},{2,6},{3,7},{4,0},{5,1},{6,2},{7,3},{8,12},{9,13},{10,... | collective-permute-start | bytes 479240 | tf_op jit(solution)/shard_map/ppermute | solution.py:656
  200.5 18.0 %collective-permute-start.40 = (bf16[104,768]{1,0:T(8,128)(2,1)S(1)}, bf16[104,768]{1,0:T(8,128)(2,1)S(1)}, u32[]{:S(2)}, u32[]{:S(2)}) collective-permute-start(bf16[104,768]{1,0:T(8,128)(2,1)S(1)} %get-tuple-element.108), channel_id=1, source_target_pairs={{0,6},{1,7},{2,4},{3,5},{4,2},{5,3},{6,0},{7,1},{8,14},{9,15},{10,... | collective-permute-start | bytes 479240 | tf_op jit(solution)/shard_map/ppermute | solution.py:656
  203.1 15.3 %collective-permute-start.37 = (bf16[96,768]{1,0:T(8,128)(2,1)S(1)}, bf16[96,768]{1,0:T(8,128)(2,1)S(1)}, u32[]{:S(2)}, u32[]{:S(2)}) collective-permute-start(bf16[96,768]{1,0:T(8,128)(2,1)S(1)} %combine.37.refs_1_), channel_id=1, source_target_pairs={{0,4},{1,5},{2,6},{3,7},{4,0},{5,1},{6,2},{7,3},{8,12},{9,13},{10,... | collective-permute-start | bytes 442376 | tf_op jit(solution)/shard_map/ppermute | solution.py:656
  220.1 13.5 %collective-permute-start.42 = (bf16[192,768]{1,0:T(8,128)(2,1)S(1)}, bf16[192,768]{1,0:T(8,128)(2,1)S(1)}, u32[]{:S(2)}, u32[]{:S(2)}) collective-permute-start(bf16[192,768]{1,0:T(8,128)(2,1)S(1)} %get-tuple-element.109.refs_1_), channel_id=1, source_target_pairs={{0,16},{8,24},{16,0},{24,8},{1,17},{9,25},{17,1},{25,9},{2,18},{10... | collective-permute-start | bytes 884744 | tf_op jit(solution)/shard_map/ppermute | solution.py:656
  222.2 24.0 %collective-permute-start.44 = (bf16[4,96,768]{2,1,0:T(8,128)(2,1)S(1)}, bf16[4,96,768]{2,1,0:T(8,128)(2,1)S(1)}, u32[]{:S(2)}, u32[]{:S(2)}) collective-permute-start(bf16[4,96,768]{2,1,0:T(8,128)(2,1)S(1)} %combine.39.refs_1_.refs_0_), channel_id=1, source_target_pairs={{0,16},{8,24},{16,0},{24,8},{1,17},{9,25},{17,1},{25,9},{2,18},{10... | collective-permute-start | bytes 1769480 | tf_op jit(solution)/shard_map/ppermute | solution.py:656
  (24 other events, 182.6 us)

commit v4 on v3

--- a/solution.py
+++ b/solution.py
@@ -22,6 +22,8 @@
 HB = pl.BlockSpec(memory_space=pl.ANY)
 FREE = pl.CostEstimate(flops=0, bytes_accessed=0, transcendentals=0)
 
+LONG = pl.CostEstimate(flops=60_000_000_000, bytes_accessed=0, transcendentals=0)
+
 
 def shape(*dims, dtype=BF16):
     return jax.ShapeDtypeStruct(dims, dtype)
@@ -89,12 +91,13 @@
             done.append(pltpu.make_async_copy(source, where, sems.at[base + block]))
         return done
 
-    def fill(self, refs, me_ref, target):
+    def fill(self, refs, me_ref, target, rest=(0, 1, 2, 3)):
         i, z, c = me_ref[0], me_ref[1], me_ref[2]
-        for block, (position, tile) in enumerate(self.sibling):
+        for block, (position, tile) in enumerate(self.sibling if 0 in rest else ()):
             self.place(target, block, z, 1 - c, 0, 96)[...] = refs[position][tile]
         for c_at, far in ((c, self.far), (1 - c, self.far_sibling)):
-            for away, parts in enumerate(far):
+            for away in rest:
+                parts = far[away]
                 for position, tile, row, rows, offset in parts:
                     for j in range(1, 4):
                         where = self.place(target, i ^ away, z ^ j, c_at, offset, rows)
@@ -165,7 +168,7 @@
             done.append(pltpu.make_async_copy(source, where, sems.at[base + block]))
         return done
 
-    def fill(self, refs, me_ref, target):
+    def fill(self, refs, me_ref, target, rest=()):
         pass
 
     def vectors(self, refs, me_ref, target):
@@ -324,26 +327,32 @@
     return inner * cumulative, cumulative + inner * density
 
 
-def fill_body(group, me_ref, *refs):
+def fill_body(group, early, me_ref, *refs):
     held, near = refs[: len(group.held)], refs[len(group.held) : len(group.held) + len(group.arrays)]
+    if not early:
+        group.fill(near, me_ref, refs[-1], (3,))
+        return
     target, sems = refs[-2:]
     loads = group.copies(held, me_ref, target, sems, 0)
     start_all(loads)
-    group.fill(near, me_ref, target)
+    group.fill(near, me_ref, target, (0, 1, 2))
     wait_all(loads)
 
 
-def fill(group, me, *dims):
-    return pl.pallas_call(
-        functools.partial(fill_body, group),
+def fill(group, me, *dims, before=None):
+    early = before is None
+    more = () if early else (before,)
+    return pl.pallas_call(
+        functools.partial(fill_body, group, early),
         out_shape=local(*dims),
-        in_specs=[SM] + [HB] * len(group.held) + [VM] * len(group.arrays),
+        in_specs=[SM] + [HB] * len(group.held) + [VM] * len(group.arrays) + [HB] * len(more),
         out_specs=VM,
-        scratch_shapes=[pltpu.SemaphoreType.DMA((group.count(),))],
+        scratch_shapes=[pltpu.SemaphoreType.DMA((group.count(),))] * early,
+        input_output_aliases={} if early else {1 + len(group.held) + len(group.arrays): 0},
         compiler_params=limit(2),
         cost_estimate=FREE,
         name="fill",
-    )(me, *far_off(*group.held), *stay(*group.arrays))
+    )(me, *far_off(*group.held), *stay(*group.arrays, *more))
 
 
 def middle_forward_body(
@@ -496,8 +505,9 @@
     )(*stay(low, ssg, slope, norm, rstd, vec, wa, wi, wu))
 
 
-def input_grad_body(g_ref, fsg_ref, w_ref, out_ref):
+def input_grad_body(g_ref, fsg_ref, w_ref, out_ref, token_ref):
     seq, width = fsg_ref.shape
+    token_ref[...] = jnp.zeros_like(token_ref)
     tile = min(256, seq)
 
     def rows_step(r, carry):
@@ -515,9 +525,9 @@
     seq, width = fsg.shape
     return pl.pallas_call(
         input_grad_body,
-        out_shape=shape(seq, width, dtype=F32),
+        out_shape=(shape(seq, width, dtype=F32), local(8, 128, dtype=F32)),
         in_specs=[VM] * 3,
-        out_specs=VM,
+        out_specs=[VM] * 2,
         compiler_params=limit(8),
         cost_estimate=FREE,
         name="input_grad",
@@ -529,12 +539,11 @@
 
 def weight_grad_body(kind, order, z_order, me_ref, left_ref, g_ref, *refs):
     sums, refs = (refs[:4], refs[4:]) if kind == "attend" else ((), refs)
-    sent = len(order) if kind == "attend" else 1
-    outs, left = refs[: sent + 1], refs[sent + 1]
+    outs, left = refs[:2], refs[2]
     i, z, c = me_ref[0], me_ref[1], me_ref[2]
     part = 96
     if kind == "attend":
-        extra = refs[sent + 2]
+        extra = refs[3]
         one, two, three, ib = (r[...] for r in sums)
         row = lax.broadcasted_iota(jnp.int32, one.shape, 0)
         every = jnp.where(row < 2, three, jnp.where(row < 5, two, one))
@@ -556,10 +565,7 @@
             left[n * 96 : (n + 1) * 96, :] = rows
         right = g_ref[...] if kind == "outer" else g_ref[block]
         grads = dot_nn(left[...], right).reshape(4, 96, 768).astype(BF16)
-        if kind == "outer":
-            out_ref[:, spot] = grads
-        else:
-            out_ref[spot, :, :96, :] = grads
+        out_ref[spot, :, :96, :] = grads
         if kind == "attend":
             for n, j in enumerate(z_order):
                 out_ref[spot, n, 96:104, :] = extra[2 * (z ^ j) + c_at].astype(BF16)
@@ -568,22 +574,17 @@
         one_block(spot, pick(order, spot), c_at, out_ref)
         return carry
 
-    if kind == "attend":
-        for spot, away in enumerate(order):
-            one_block(0, away, 1 - c, outs[spot])
-    else:
-        lax.fori_loop(0, 4, functools.partial(block_step, 1 - c, outs[0]), 0)
-    lax.fori_loop(0, 4, functools.partial(block_step, c, outs[-1]), 0)
+    lax.fori_loop(0, 4, functools.partial(block_step, 1 - c, outs[0]), 0)
+    lax.fori_loop(0, 4, functools.partial(block_step, c, outs[1]), 0)
 
 
 def weight_grad(kind, order, z_order, me, left, g, sums=()):
     rows = 104 if kind == "attend" else 96
-    sent = (local(1, 4, rows, 768),) * 4 if kind == "attend" else (local(4, 4, rows, 768),)
     return pl.pallas_call(
         functools.partial(weight_grad_body, kind, order, z_order),
-        out_shape=sent + (local(4, 4, rows, 768),),
+        out_shape=(local(4, 4, rows, 768),) * 2,
         in_specs=[SM] + [VM] * (2 + len(sums)),
-        out_specs=[VM] * (len(sent) + 1),
+        out_specs=[VM] * 2,
         scratch_shapes=[pltpu.VMEM((384, left.shape[-1]), BF16)] + [pltpu.VMEM((8, 8, 768), F32)] * (kind == "attend"),
         compiler_params=limit(6),
         cost_estimate=FREE,
@@ -660,26 +661,26 @@
     return [swap(piece, "fsdp", fsdp, 2 * j) for j in (1, 2, 3)]
 
 
-def combine(*outs):
+def combine(*outs, cost=FREE):
     arrays = []
-    for _, _, *lists in outs:
-        for terms in lists:
-            arrays += [a for n, (a, _) in enumerate(terms) if not any(a is b for b in arrays)]
+    for _, parts in outs:
+        for _, terms in parts:
+            arrays += [a for a, _ in terms if not any(a is b for b in arrays)]
 
     def find(array):
         return next(n for n, b in enumerate(arrays) if b is array)
 
     def body(*refs):
-        for out_ref, (lead, rows, *lists) in zip(refs[len(arrays) :], outs, strict=True):
-            size = rows // len(lists)
+        for out_ref, (lead, parts) in zip(refs[len(arrays) :], outs, strict=True):
 
             def tile(index):
-                for n, terms in enumerate(lists):
-                    if len(terms) == 1:
-                        value = refs[find(terms[0][0])][terms[0][1](*index)]
-                    else:
-                        value = sum(refs[find(array)][at(*index)].astype(F32) for array, at in terms).astype(BF16)
-                    out_ref[(*index, slice(n * size, (n + 1) * size), slice(None))] = value
+                start = 0
+                for rows, terms in parts:
+                    found = [(find(array), at(*index)) for array, at in terms]
+                    values = [refs[n][spot] for n, spot in found if spot is not None]
+                    value = values[0] if len(values) == 1 else sum(v.astype(F32) for v in values).astype(BF16)
+                    out_ref[(*index, slice(start, start + rows), slice(None))] = value
+                    start += rows
 
             def step(front, last, carry):
                 tile((*front, last))
@@ -695,11 +696,11 @@
 
     return pl.pallas_call(
         body,
-        out_shape=tuple(local(*lead, rows, 768) for lead, rows, *_ in outs),
+        out_shape=tuple(local(*lead, sum(rows for rows, _ in parts), 768) for lead, parts in outs),
         in_specs=[VM] * len(arrays),
         out_specs=[VM] * len(outs),
         compiler_params=limit(2),
-        cost_estimate=FREE,
+        cost_estimate=cost,
         name="combine",
     )(*stay(*arrays))
 
@@ -722,40 +723,67 @@
     )(*stay(*parts))
 
 
-def halves(over_x, over_y):
-    return (
-        combine(((3,), 48, [(over_x, lambda n: (n, slice(0, 48)))]))[0],
-        combine(((3,), 48, [(over_y, lambda n: (n, slice(48, 96)))]))[0],
-    )
-
-
-def first_sum(kept, got):
-    at = lambda a, b: (2 + a, b)
-    return combine(((2, 4), 96, [(kept, at), (got, at)]))[0]
-
-
-def second_sum(kept, got, over):
-    here, there = (lambda b: (1, b)), (lambda b: (1, b))
-    return combine(((4,), 96, [(kept, here), (got, here), (over, there)]))[0]
-
-
-def finish(terms, beside):
+def rows_of(value, start, rows):
+    (part,) = combine(((value.shape[0],), [(rows, [(value, lambda n: (n, slice(start, start + rows)))])]))
+    return part
+
+
+UPPER = slice(0, 48)
+
+
+def held(pair, block, rows):
+    return [(v, lambda b: (block, b, rows)) for v in pair]
+
+
+def first_pair(pair, total):
+    def sums(blocks, rows, size):
+        terms = []
+        for n, block in enumerate(blocks):
+            for array, at in held(pair, block, rows):
+                terms.append((array, lambda a, b, n=n, at=at: at(b) if a == n else None))
+        return combine(((2, 4), [(size, terms)]))[0]
+
+    return sums((1, 3), UPPER, 48), sums((2, 3), slice(48, total), total - 48)
+
+
+def second_pair(pair, over_x, over_y, total):
+    (x,) = combine(((4,), [(48, held(pair, 2, UPPER) + [(over_x, lambda b: (1, b))])]))
+    (y,) = combine(((4,), [(total - 48, held(pair, 1, slice(48, total)) + [(over_y, lambda b: (1, b))])]))
+    return x, y
+
+
+def last_terms(pair, overs, onwards, total, tile):
+    parts = []
+    for rows, size, over, onward in (
+        (UPPER, 48, overs[0], onwards[0]),
+        (slice(48, total), total - 48, overs[1], onwards[1]),
+    ):
+        terms = [(array, lambda *n, at=at: at(tile(*n))) for array, at in held(pair, 0, rows)]
+        terms += [(over, lambda *n: (0, tile(*n))), (onward, lambda *n: (tile(*n),))]
+        parts.append((size, terms))
+    return parts
+
+
+def last_pair(pair, overs, onwards, cost=FREE):
+    return combine(*[((2,), last_terms(pair, overs, onwards, 96, lambda b, k=k: k + b)) for k in (0, 2)], cost=cost)
+
+
+def finish(terms):
     def body(*refs):
-        terms, (beside_ref, own_ref, small_ref) = refs[:-3], refs[-3:]
+        terms, (own_ref, small_ref) = refs[:-2], refs[-2:]
         value = sum(r[...].astype(F32) for r in terms)
-        own_ref[:96, :] = value[:96].astype(BF16)
-        own_ref[96:, :] = beside_ref[...]
+        own_ref[...] = value[:96].astype(BF16)
         small_ref[...] = value[96:]
 
     return pl.pallas_call(
         body,
-        out_shape=(local(192, 768), local(8, 768, dtype=F32)),
-        in_specs=[VM] * (len(terms) + 1),
+        out_shape=(local(96, 768), local(8, 768, dtype=F32)),
+        in_specs=[VM] * len(terms),
         out_specs=[VM] * 2,
         compiler_params=limit(2),
         cost_estimate=FREE,
         name="finish",
-    )(*stay(*terms, beside))
+    )(*stay(*terms))
 
 
 def spread(value, dp):
@@ -809,7 +837,7 @@
         z_m = gather_z(piece_m, fsdp)
         mine_a = stack_three(z_a)
         plane_a = (swap(mine_a, "dp", dp, 1), swap(mine_a, "dp", dp, 2))
-        parts_a = halves(*plane_a)
+        parts_a = (rows_of(plane_a[0], 0, 48), rows_of(plane_a[1], 48, 48))
         rest_a = (swap(parts_a[0], "dp", dp, 2), swap(parts_a[1], "dp", dp, 1))
         z_m[0] = after(z_m[0], *rest_a)
         mine_m = stack_three(z_m)
@@ -833,32 +861,37 @@
         x = tokens.reshape(seq, width)
         q, k, v, att, left_a, lse, wa, vec, ib = attend_forward(group_a, fsdp, blocks, me, lengths, after(x, mine_m))
         plane_m = (after(plane_m[0], att), after(plane_m[1], att))
-        parts_m = (
-            combine(((3,), 96, [(plane_m[0], lambda n: (n, slice(0, 96)))]))[0],
-            combine(((3,), 96, [(plane_m[1], lambda n: (n, slice(96, 192)))]))[0],
-        )
+        parts_m = (rows_of(plane_m[0], 0, 96), rows_of(plane_m[1], 96, 96))
         rest_m = (swap(parts_m[0], "dp", dp, 2), swap(parts_m[1], "dp", dp, 1))
         spots = (tuple((0, 768 * n) for n in range(4)), tuple((96 * n, 0) for n in range(4)))
         near_m = bundle(2, (inner_weight, outer_weight), spots, (mine_m,) + plane_m)
         far_m = (swap(near_m, "fsdp", fsdp, 1),) + tuple(swap(v, "fsdp", fsdp, 1) for v in rest_m)
-        group_i = Pieces(
+        four = range(4)
+        early_i = Pieces(
             (inner_weight,),
-            (mine_m,) + plane_m + (rest_m[0], far_m[0], far_m[1]),
-            [(0, 0, 768 * n) for n in range(4)],
-            [(4, n) for n in range(4)],
-            far_at(0) + [[(3, 0, 0, 96, 0)]],
-            [[(4, 8 + 6 * n, 0, 96, 0)] for n in range(3)] + [[(5, 0, 0, 96, 0)]],
+            (mine_m,) + plane_m + (far_m[0],),
+            [(0, 0, 768 * n) for n in four],
+            [(3, n) for n in four],
+            far_at(0),
+            [[(3, 8 + 6 * n, 0, 96, 0)] for n in range(3)],
             True,
         )
-        group_u = Pieces(
+        early_u = Pieces(
             (outer_weight,),
-            (mine_m,) + plane_m + (rest_m[1], far_m[0], far_m[2]),
-            [(0, 96 * n, 0) for n in range(4)],
-            [(4, 4 + n) for n in range(4)],
-            far_at(0, 96) + [[(3, 0, 0, 96, 0)]],
-            [[(4, 11 + 6 * n, 0, 96, 0)] for n in range(3)] + [[(5, 0, 0, 96, 0)]],
+            (mine_m,) + plane_m + (far_m[0],),
+            [(0, 96 * n, 0) for n in four],
+            [(3, 4 + n) for n in four],
+            far_at(0, 96),
+            [[(3, 11 + 6 * n, 0, 96, 0)] for n in range(3)],
             False,
         )
+        none = [None] * 3
+        late_i = Pieces((), (rest_m[0], far_m[1]), (), (), none + [[(0, 0, 0, 96, 0)]], none + [[(1, 0, 0, 96, 0)]], True)
+        late_u = Pieces((), (rest_m[1], far_m[2]), (), (), none + [[(0, 0, 0, 96, 0)]], none + [[(1, 0, 0, 96, 0)]], False)
+        wi = fill(early_i, me, blocks, width, width)
+        wu = fill(early_u, me, blocks * width, width)
+        wi = fill(late_i, me, blocks, width, width, before=wi)
+        wu = fill(late_u, me, blocks * width, width, before=wu)
     else:
         whole = tuple(
             lax.all_gather(w, "fsdp", axis=0, tiled=True)
@@ -872,10 +905,10 @@
         group_u = Whole(whole[5:6], (), [(0, width * n, 0) for n in range(blocks)], False)
         x = tokens.reshape(seq, width)
         q, k, v, att, left_a, lse, wa, vec, ib = attend_forward(group_a, fsdp, blocks, me, lengths, x)
+        wi = fill(group_i, me, blocks, width, width)
+        wu = fill(group_u, me, blocks * width, width)
 
     cot = cotangent.reshape(seq, width)
-    wi = fill(group_i, me, blocks, width, width)
-    wu = fill(group_u, me, blocks * width, width)
     out, ssg, low, act_t, slope, norm, rstd, hid_t, sum_one = middle_forward(lengths, x, att, cot, vec, ib, wa, wi, wu)
     pairs = width // 128
     attend = functools.partial(attend_backward, length=lengths, q=q, k=k, v=v, lse=lse)
@@ -885,91 +918,85 @@
         low = after(low, sent_u)
     igl, fsg, branch, att_g, ib_sum, sum_two = middle_backward(low, ssg, slope, norm, rstd, vec, wa, wi, wu)
     if direct:
-        first_u = first_sum(kept_u, got_u)
-        over_u = swap(first_u, "fsdp", fsdp, 2)
-        sent_i, kept_i = weight_grad("inner", (0, 1, 2, 3), Z_ORDER, me, hid_t, after(igl, first_u))
+        pair_u = (kept_u, got_u)
+        first_u = first_pair(pair_u, 96)
+        over_u = [swap(first_u[0], "dp", dp, 1), swap(first_u[1], "dp", dp, 2)]
+        sent_i, kept_i = weight_grad("inner", (0, 1, 2, 3), Z_ORDER, me, hid_t, after(igl, *first_u))
         got_i = swap(sent_i, "fsdp", fsdp, 1)
         half = attend(0, pairs // 2, do=after(att_g, sent_i), branch=branch)
-        got_i = after(got_i, half[0])
-        upper, lower = slice(0, 48), slice(48, 96)
-        (first_x,) = combine(((2, 4), 48, [(v, lambda a, b: (2 * a + 1, b, upper)) for v in (kept_i, got_i)]))
-        (first_y,) = combine(((2, 4), 48, [(v, lambda a, b: (a + 2, b, lower)) for v in (kept_i, got_i)]))
-        over_x, over_y = swap(first_x, "dp", dp, 1), swap(first_y, "dp", dp, 2)
-        do = after(att_g, first_x, first_y)
-        g, sum_three = attend(pairs // 2, pairs, do=do, branch=branch, before=half)
+        pair_i = (kept_i, after(got_i, half[0]))
+        first_i = first_pair(pair_i, 96)
+        over_i = [swap(first_i[0], "dp", dp, 1), swap(first_i[1], "dp", dp, 2)]
+        g, sum_three = attend(pairs // 2, pairs, do=after(att_g, *first_i), branch=branch, before=half)
     else:
         g, sum_three = attend(0, pairs, do=att_g, branch=branch)
-        in_grad = input_grad(g, fsg, wa)
+        in_grad, _ = input_grad(g, fsg, wa)
 
     if direct:
-        *sent_a, kept_a = weight_grad(
-            "attend", (1, 2, 3, 0), (0, 1, 2, 3), me, left_a, g, (sum_one, sum_two, sum_three, ib_sum)
+        here = lambda: ()
+        over_u = [after(v, g) for v in over_u]
+        second_u = second_pair(pair_u, *over_u, 96)
+        onward_u = [swap(second_u[0], "dp", dp, 2), swap(second_u[1], "dp", dp, 1)]
+
+        left_a = after(left_a, *second_u)
+        sent_a, kept_a = weight_grad(
+            "attend", (0, 1, 2, 3), (0, 1, 2, 3), me, left_a, g, (sum_one, sum_two, sum_three, ib_sum)
         )
-        over_x = after(over_x, kept_a)
-        (second_x,) = combine(
-            ((4,), 48, [(v, lambda b: (2, b, upper)) for v in (kept_i, got_i)] + [(over_x, lambda b: (1, b))])
-        )
-        (second_y,) = combine(
-            ((4,), 48, [(v, lambda b: (1, b, lower)) for v in (kept_i, got_i)] + [(over_y, lambda b: (1, b))])
-        )
-        onward_x, onward_y = swap(second_x, "dp", dp, 2), swap(second_y, "dp", dp, 1)
-        over_u = after(over_u, second_x, second_y)
-        second_u = second_sum(kept_u, got_u, over_u)
-        onward_u = swap(second_u, "fsdp", fsdp, 4)
-        sent_a[3] = after(sent_a[3], second_x)
-        got_a = [swap(v, "fsdp", fsdp, 1) for v in sent_a]
-        got_a[0] = after(got_a[0], second_u)
-        ready_a = [combine(((4,), 104, [(kept_a, lambda b, n=n: (n, b)), (got_a[n], lambda b: (0, b))]))[0] for n in range(4)]
-        over_a = [swap(ready_a[m - 1], "dp", dp, m) for m in (1, 2, 3)]
-        in_grad = input_grad(g, after(fsg, *ready_a), wa)
-
-        tile, front, here = (lambda b: (b,)), (lambda b: (0, b)), (lambda: ())
-
-        def plane_at(first):
-            def terms(rows, over, onward):
-                held = [(v, lambda b: (0, first + b, rows)) for v in (kept_i, got_i)]
-                return held + [(over, lambda b: (0, first + b)), (onward, lambda b: (first + b,))]
-
-            return (2,), 96, terms(upper, over_x, onward_x), terms(lower, over_y, onward_y)
-
-        onward_x = after(onward_x, in_grad)
-        keep_i, send_i = combine(plane_at(0), plane_at(2))
+        in_grad, token = input_grad(g, after(fsg, kept_a), wa)
+
+        over_i = [after(v, token) for v in over_i]
+        second_i = second_pair(pair_i, *over_i, 96)
+        onward_i = [swap(second_i[0], "dp", dp, 2), swap(second_i[1], "dp", dp, 1)]
+
+        got_a = swap(after(sent_a, *second_i), "fsdp", fsdp, 1)
+
+        onward_u = [after(v, *second_i) for v in onward_u]
+        keep_u, send_u = last_pair(pair_u, over_u, onward_u, LONG)
+        near_u = swap(send_u, "fsdp", fsdp, 2)
+
+        pair_a = (kept_a, after(got_a, keep_u))
+        first_a = first_pair(pair_a, 104)
+        over_a = [swap(first_a[0], "dp", dp, 1), swap(first_a[1], "dp", dp, 2)]
+
+        onward_i = [after(v, *first_a) for v in onward_i]
+        keep_i, send_i = last_pair(pair_i, over_i, onward_i, LONG)
         near_i = swap(send_i, "fsdp", fsdp, 2)
 
-        onward_u = after(onward_u, keep_i)
-        (line_u,) = combine(((4,), 96, [(kept_u, front), (got_u, front), (over_u, front), (onward_u, tile)]))
-        beside_u = swap(line_u, "dp", dp, 1)
-
-        near_i = after(near_i, line_u)
-        (next_i,) = combine(((), 96, [(keep_i, lambda: (1,)), (near_i, lambda: (1,))]))
+        near_u = after(near_u, keep_i)
+        (next_u,) = combine(((), [(96, [(keep_u, lambda: (1,)), (near_u, lambda: (1,))])]))
+        last_u = swap(next_u, "fsdp", fsdp, 4)
+
+        over_a = [after(v, next_u) for v in over_a]
+        second_a = second_pair(pair_a, *over_a, 104)
+        onward_a = [swap(second_a[0], "dp", dp, 2), swap(second_a[1], "dp", dp, 1)]
+
+        near_i = after(near_i, *second_a)
+        (next_i,) = combine(((), [(96, [(keep_i, lambda: (1,)), (near_i, lambda: (1,))])]), cost=LONG)
         last_i = swap(next_i, "fsdp", fsdp, 4)
 
-        over_a[0] = after(over_a[0], next_i)
-        whole_a = combine(
-            *[((), 104, [(ready_a[3], lambda j=j: (j,))] + [(v, lambda j=j: (j,)) for v in over_a]) for j in range(4)]
-        )
+        last_u = after(last_u, next_i)
+        terms_u = [(keep_u, lambda: (0,)), (near_u, lambda: (0,)), (last_u, here)]
+        (own_u,) = combine(((), [(96, terms_u)]))
+
+        last_i = after(last_i, own_u)
+        terms_i = [(keep_i, lambda: (0,)), (near_i, lambda: (0,)), (last_i, here)]
+        (own_i,) = combine(((), [(96, terms_i)]))
+
+        onward_a = [after(v, own_i) for v in onward_a]
+        whole_a = combine(*[((), last_terms(pair_a, over_a, onward_a, 104, lambda j=j: j)) for j in range(4)])
         far_a = [swap(whole_a[j], "fsdp", fsdp, 2 * j) for j in (1, 2, 3)]
 
-        beside_u = after(beside_u, whole_a[0])
-        (pair_u,) = combine(((4,), 96, [(line_u, tile), (beside_u, lambda b: (b ^ 1,))]))
-        across_u = swap(pair_u, "dp", dp, 2)
-
-        last_i = after(last_i, pair_u)
-        (own_i,) = combine(((), 96, [(keep_i, lambda: (0,)), (near_i, lambda: (0,)), (last_i, here)]))
-
-        far_a[0] = after(far_a[0], own_i)
-        own, small_rows = finish((whole_a[0], *far_a), own_i)
-        every = spread(own, dp)
-        all_a = [v[:96] for v in every]
-        all_i = [v[96:] for v in every]
-
-        across_u = after(across_u, *every)
-        (all_u,) = combine(((4,), 96, [(pair_u, tile), (across_u, lambda b: (b ^ 2,))]))
-        small_own = small_rows
+        (own_m,) = combine(((), [(96, [(after(own_i, whole_a[0]), here)]), (96, [(own_u, here)])]))
+        every = spread(own_m, dp)
+
+        far_a[0] = after(far_a[0], own_m)
+        own_a, small_own = finish((whole_a[0], *far_a))
+        all_a = spread(own_a, dp)
         small_grads = [small_own[n, :part] for n in range(8)] + [small_own[0, 128 : 128 + blocks * part]]
+        all_i, all_u = [v[:96] for v in every], [v[96:] for v in every]
         q_g, k_g, v_g, o_g = (w.astype(F32) for w in in_order(all_a, i))
         i_g = jnp.concatenate(in_order(all_i, i), axis=1).astype(F32)
-        u_g = jnp.concatenate(in_order([all_u[n] for n in range(4)], i), axis=0).astype(F32)
+        u_g = jnp.concatenate(in_order(all_u, i), axis=0).astype(F32)
     else:
         vec_sum = jnp.concatenate([sum_three[:2], sum_two[2:5], sum_one[5:8]])
         vec_sum = vec_sum.reshape(8, fsdp, part).transpose(1, 0, 2).reshape(fsdp, 8 * part)

time: 248 us -> 223 us (0.90)
  waiting for transfers between devices: 117 us -> 77.3 us
  starting transfers between devices: 45.6 us -> 59.9 us
    ppermute x45 -> x48, waiting for transfers between devices: 117 us -> 77.3 us  [swap(): return lax.ppermute(value, axis, [(n, n ^ mask) for n in range(size)])]
    ppermute x45 -> x48, starting transfers between devices: 45.6 us -> 59.9 us  [swap(): return lax.ppermute(value, axis, [(n, n ^ mask) for n in range(size)])]
    pallas_call x25 -> x30, Pallas kernels: 10.1 us -> 11.2 us  [the longest x4 4.63 us: fill(): pl.pallas_call(functools.partial(fill_body, group, early), out_shape=loca...]
  transfers between devices with their start and end apart: 45 -> 48, of which waited for: 27 -> 25; matrix products, arithmetic and copies ran while one was open for 2% -> 2% of each run, Pallas kernels for 19% -> 22%
where the time goes in v4:
time: 223 us; the launch traced here: 222 us
  Pallas kernels  77.8 us (35%)
  waiting for transfers between devices  77.3 us (35%)
  starting transfers between devices  59.9 us (27%)
  other arithmetic  3.58 us (2%)
    ppermute x48, waiting for transfers between devices, swap(): return lax.ppermute(value, axis, [(n, n ^ mask) for n in range(size)])  77.3 us
    ppermute x48, starting transfers between devices, swap(): return lax.ppermute(value, axis, [(n, n ^ mask) for n in range(size)])  59.9 us
    pallas_call x1, Pallas kernels, middle_forward(): pl.pallas_call(middle_forward_body, out_shape=(shape(seq, width), local(s...  13.5 us
    pallas_call x3, Pallas kernels, weight_grad(): pl.pallas_call(functools.partial(weight_grad_body, kind, order, z_order),...  13.4 us
    pallas_call x2, Pallas kernels, attend_backward(): pl.pallas_call(functools.partial(attend_backward_body, first, last), out_...  12.7 us
    pallas_call x1, Pallas kernels, attend_forward(): pl.pallas_call(functools.partial(attend_forward_body, group, width // sha...  12.2 us
    pallas_call x1, Pallas kernels, middle_backward(): pl.pallas_call(middle_backward_body, out_shape=(local(blocks, seq, width)...  10.3 us
    pallas_call x4, Pallas kernels, fill(): pl.pallas_call(functools.partial(fill_body, group, early), out_shape=loca...  4.63 us
  transfers between devices with their start and end apart: 48, of which 25 were waited for; matrix products, arithmetic and copies ran while one was open for 2% of the time, Pallas kernels for 22%

profile of v4, /device:TPU:0, one launch (start us, length us, event | category | flops | bytes accessed | tf_op | source)
XLA Modules:
  0.0 222.2 jit_solution(9893879621073543251)
XLA Ops:
  2.5 3.1 %collective-permute-start.1 = (bf16[104,768]{1,0:T(8,128)(2,1)S(1)}, bf16[104,768]{1,0:T(8,128)(2,1)S(1)}, u32[]{:S(2)}, u32[]{:S(2)}) collective-permute-start(bf16[104,768]{1,0:T(8,128)(2,1)S(1)} %get-tuple-element.66.refs_7_.refs_12_), channel_id=1, source_target_pairs={{0,2},{1,3},{2,0},{3,1},{4,6},{5,7},{6,4},{7,5},{8,10},{9,11},{10,... | collective-permute-start | bytes 479240 | tf_op jit(solution)/shard_map/ppermute | solution.py:657
  8.1 3.9 %collective-permute-done.1.refs_0_ = bf16[104,768]{1,0:T(8,128)(2,1)S(1)} collective-permute-done((bf16[104,768]{1,0:T(8,128)(2,1)S(1)}, bf16[104,768]{1,0:T(8,128)(2,1)S(1)}, u32[]{:S(2)}, u32[]{:S(2)}) %collective-permute-start.1) | collective-permute-done | bytes 159776 | tf_op jit(solution)/shard_map/ppermute | solution.py:657
  12.0 8.3 %collective-permute-done.2.refs_1_ = bf16[104,768]{1,0:T(8,128)(2,1)S(1)} collective-permute-done((bf16[104,768]{1,0:T(8,128)(2,1)S(1)}, bf16[104,768]{1,0:T(8,128)(2,1)S(1)}, u32[]{:S(2)}, u32[]{:S(2)}) %collective-permute-start.2) | collective-permute-done | bytes 159776 | tf_op jit(solution)/shard_map/ppermute | solution.py:657
  36.7 3.2 %collective-permute-done.7.refs_2_.refs_8_ = bf16[3,48,768]{2,1,0:T(8,128)(2,1)S(1)} collective-permute-done((bf16[3,48,768]{2,1,0:T(8,128)(2,1)S(1)}, bf16[3,48,768]{2,1,0:T(8,128)(2,1)S(1)}, u32[]{:S(2)}, u32[]{:S(2)}) %collective-permute-start.7) | collective-permute-done | bytes 221216 | tf_op jit(solution)/shard_map/ppermute | solution.py:657
  39.9 9.6 %collective-permute-done.8.refs_1_ = bf16[192,768]{1,0:T(8,128)(2,1)S(1)} collective-permute-done((bf16[192,768]{1,0:T(8,128)(2,1)S(1)}, bf16[192,768]{1,0:T(8,128)(2,1)S(1)}, u32[]{:S(2)}, u32[]{:S(2)}) %collective-permute-start.8) | collective-permute-done | bytes 294944 | tf_op jit(solution)/shard_map/ppermute | solution.py:657
  55.6 12.2 %attend_forward.1 = (bf16[512,768]{1,0:T(8,128)(2,1)S(1)}, bf16[512,768]{1,0:T(8,128)(2,1)S(1)}, bf16[512,768]{1,0:T(8,128)(2,1)S(1)}, bf16[512,768]{1,0:T(8,128...) custom-call(s32[4]{0:T(128)S(1)} %pad_add_fusion.me_ref, ...), custom_call_target="tpu_custom_call" | custom-call | tf_op jit(solution)/shard_map/attend_forward/pallas_call | solution.py:252
  67.8 5.2 %collective-permute-done.13.refs_0_ = bf16[3,192,768]{2,1,0:T(8,128)(2,1)S(1)} collective-permute-done((bf16[3,192,768]{2,1,0:T(8,128)(2,1)S(1)}, bf16[3,192,768]{2,1,0:T(8,128)(2,1)S(1)}, u32[]{:S(2)}, u32[]{:S(2)}) %collective-permute-start.13) | collective-permute-done | bytes 884768 | tf_op jit(solution)/shard_map/ppermute | solution.py:657
  76.9 10.5 %collective-permute-done.14.refs_0_ = bf16[3,96,768]{2,1,0:T(8,128)(2,1)S(1)} collective-permute-done((bf16[3,96,768]{2,1,0:T(8,128)(2,1)S(1)}, bf16[3,96,768]{2,1,0:T(8,128)(2,1)S(1)}, u32[]{:S(2)}, u32[]{:S(2)}) %collective-permute-start.14) | collective-permute-done | bytes 442400 | tf_op jit(solution)/shard_map/ppermute | solution.py:657
  93.1 13.5 %middle_forward.1 = (bf16[512,768]{1,0:T(8,128)(2,1)}, f32[512,768]{1,0:T(8,128)S(1)}, bf16[512,768]{1,0:T(8,128)(2,1)S(1)}, bf16[3072,512]{1,0:T(8,128)(2,1)S(1...) custom-call(s32[1]{0:T(128)S(6)} %copy.107.len_ref, ...), custom_call_target="tpu_custom_call" | custom-call | tf_op jit(solution)/shard_map/middle_forward/pallas_call | solution.py:430
  106.7 4.4 %weight_grad_outer.1 = (bf16[4,4,96,768]{3,2,1,0:T(8,128)(2,1)S(1)}, bf16[4,4,96,768]{3,2,1,0:T(8,128)(2,1)S(1)}) custom-call(s32[4]{0:T(128)S(1)} %pad_add_fusion.me_ref, bf16[3072,512]{1,0:T(8,128)(2,1)S(1)} %get-tuple-element.76.left_ref, bf16[512,768]{1,0:T(8,128)(2,1)S(1)} %get-tuple-element.75.g_ref.refs_0_), custom_call_target="tpu_custom_call" | custom-call | tf_op jit(solution)/shard_map/weight_grad_outer/pallas_call | solution.py:583
  111.4 10.3 %middle_backward.1 = (bf16[4,512,768]{2,1,0:T(8,128)(2,1)S(1)}, f32[512,768]{1,0:T(8,128)S(1)}, bf16[512,768]{1,0:T(8,128)(2,1)S(1)}, bf16[512,768]{1,0:T(8,128)...) custom-call(bf16[512,768]{1,0:T(8,128)(2,1)S(1)} %after.37.low_ref, f32[512,768]{1,0:T(8,128)S(1)} %get-tuple-element.78.ssg_ref, ...), custom_call_target="tpu_custom_call" | custom-call | tf_op jit(solution)/shard_map/middle_backward/pallas_call | solution.py:490
  122.1 4.5 %weight_grad_inner.1 = (bf16[4,4,96,768]{3,2,1,0:T(8,128)(2,1)S(1)}, bf16[4,4,96,768]{3,2,1,0:T(8,128)(2,1)S(1)}) custom-call(s32[4]{0:T(128)S(1)} %pad_add_fusion.me_ref, bf16[768,512]{1,0:T(8,128)(2,1)S(1)} %get-tuple-element.83.left_ref, bf16[4,512,768]{2,1,0:T(8,128)(2,1)S(1)} %after.38.g_ref), custom_call_target="tpu_custom_call" | custom-call | tf_op jit(solution)/shard_map/weight_grad_inner/pallas_call | solution.py:583
  129.8 6.4 %attend_backward.2 = (bf16[4,512,768]{2,1,0:T(8,128)(2,1)S(1)}, f32[8,768]{1,0:T(8,128)S(1)}) custom-call(s32[1]{0:T(128)S(6)} %copy.107.len_ref, bf16[512,768]{1,0:T(8,128)(2,1)S(1)} %get-tuple-element.72.q_ref, bf16[512,768]{1,0:T(8,128)(2,1)S(1)} %get-tuple-element.73.k_ref, bf16[512,768]{1,0:T(8,128)(2,1)S(1)} %get-tuple-element.74.v_ref, ...), custom_call_target="tpu_custom_call" | custom-call | tf_op jit(solution)/shard_map/attend_backward/pallas_call | solution.py:312
  137.9 6.3 %attend_backward.3 = (bf16[4,512,768]{2,1,0:T(8,128)(2,1)S(1)}, f32[8,768]{1,0:T(8,128)S(1)}) custom-call(s32[1]{0:T(128)S(6)} %copy.107.len_ref, bf16[512,768]{1,0:T(8,128)(2,1)S(1)} %get-tuple-element.72.q_ref, bf16[512,768]{1,0:T(8,128)(2,1)S(1)} %get-tuple-element.73.k_ref, ...), custom_call_target="tpu_custom_call", output_to_operand_aliasing={{0}: (7, {}), {1}: (8, {})} | custom-call | tf_op jit(solution)/shard_map/attend_backward/pallas_call | solution.py:312
  147.5 4.5 %weight_grad_attend.1 = (bf16[4,4,104,768]{3,2,1,0:T(8,128)(2,1)S(1)}, bf16[4,4,104,768]{3,2,1,0:T(8,128)(2,1)S(1)}) custom-call(s32[4]{0:T(128)S(1)} %pad_add_fusion.me_ref, bf16[2,768,512]{2,1,0:T(8,128)(2,1)S(1)} %after.44.left_ref, bf16[4,512,768]{2,1,0:T(8,128)(2,1)S(1)} %get-tuple-element.92.refs_1_.g_ref, f32[8,768]{1,0:T(8,128)S(1)} %get-tuple-element.95.refs_0_, ...), custom_call_target="tpu_custom_call" | custom-call | tf_op jit(solution)/shard_map/weight_grad_attend/pallas_call | solution.py:583
  152.1 3.4 %input_grad.1 = (f32[512,768]{1,0:T(8,128)}, f32[8,128]{1,0:T(8,128)S(1)}) custom-call(bf16[4,512,768]{2,1,0:T(8,128)(2,1)S(1)} %get-tuple-element.92.refs_1_.g_ref, f32[512,768]{1,0:T(8,128)S(1)} %after.45.fsg_ref, bf16[4,768,768]{2,1,0:T(8,128)(2,1)S(1)} %get-tuple-element.70.wa.w_ref), custom_call_target="tpu_custom_call" | custom-call | tf_op jit(solution)/shard_map/input_grad/pallas_call | solution.py:526
  159.3 4.2 %collective-permute-done.27.refs_0_ = bf16[4,48,768]{2,1,0:T(8,128)(2,1)S(1)} collective-permute-done((bf16[4,48,768]{2,1,0:T(8,128)(2,1)S(1)}, bf16[4,48,768]{2,1,0:T(8,128)(2,1)S(1)}, u32[]{:S(2)}, u32[]{:S(2)}) %collective-permute-start.27) | collective-permute-done | bytes 294944 | tf_op jit(solution)/shard_map/ppermute | solution.py:657
  163.8 3.8 %collective-permute-start.30 = (bf16[2,96,768]{2,1,0:T(8,128)(2,1)S(1)}, bf16[2,96,768]{2,1,0:T(8,128)(2,1)S(1)}, u32[]{:S(2)}, u32[]{:S(2)}) collective-permute-start(bf16[2,96,768]{2,1,0:T(8,128)(2,1)S(1)} %get-tuple-element.104), channel_id=1, source_target_pairs={{0,2},{1,3},{2,0},{3,1},{4,6},{5,7},{6,4},{7,5},{8,10},{9,11},{10,... | collective-permute-start | bytes 884744 | tf_op jit(solution)/shard_map/ppermute | solution.py:657
  170.3 3.0 %collective-permute-start.34 = (bf16[2,96,768]{2,1,0:T(8,128)(2,1)S(1)}, bf16[2,96,768]{2,1,0:T(8,128)(2,1)S(1)}, u32[]{:S(2)}, u32[]{:S(2)}) collective-permute-start(bf16[2,96,768]{2,1,0:T(8,128)(2,1)S(1)} %get-tuple-element.106), channel_id=1, source_target_pairs={{0,2},{1,3},{2,0},{3,1},{4,6},{5,7},{6,4},{7,5},{8,10},{9,11},{10,... | collective-permute-start | bytes 884744 | tf_op jit(solution)/shard_map/ppermute | solution.py:657
  173.4 2.7 %collective-permute-start.37 = (bf16[96,768]{1,0:T(8,128)(2,1)S(1)}, bf16[96,768]{1,0:T(8,128)(2,1)S(1)}, u32[]{:S(2)}, u32[]{:S(2)}) collective-permute-start(bf16[96,768]{1,0:T(8,128)(2,1)S(1)} %combine.40.refs_1_), channel_id=1, source_target_pairs={{0,4},{1,5},{2,6},{3,7},{4,0},{5,1},{6,2},{7,3},{8,12},{9,13},{10,... | collective-permute-start | bytes 442376 | tf_op jit(solution)/shard_map/ppermute | solution.py:657
  176.1 5.2 %collective-permute-done.29.refs_0_ = bf16[2,4,48,768]{3,2,1,0:T(8,128)(2,1)S(1)} collective-permute-done((bf16[2,4,48,768]{3,2,1,0:T(8,128)(2,1)S(1)}, bf16[2,4,48,768]{3,2,1,0:T(8,128)(2,1)S(1)}, u32[]{:S(2)}, u32[]{:S(2)}) %collective-permute-start.29) | collective-permute-done | bytes 589856 | tf_op jit(solution)/shard_map/ppermute | solution.py:657
  183.1 2.8 %collective-permute-done.35.refs_0_ = bf16[2,4,56,768]{3,2,1,0:T(8,128)(2,1)S(1)} collective-permute-done((bf16[2,4,56,768]{3,2,1,0:T(8,128)(2,1)S(1)}, bf16[2,4,56,768]{3,2,1,0:T(8,128)(2,1)S(1)}, u32[]{:S(2)}, u32[]{:S(2)}) %collective-permute-start.35) | collective-permute-done | bytes 688160 | tf_op jit(solution)/shard_map/ppermute | solution.py:657
  189.7 6.2 %collective-permute-done.36.refs_0_ = bf16[96,768]{1,0:T(8,128)(2,1)S(1)} collective-permute-done((bf16[96,768]{1,0:T(8,128)(2,1)S(1)}, bf16[96,768]{1,0:T(8,128)(2,1)S(1)}, u32[]{:S(2)}, u32[]{:S(2)}) %collective-permute-start.36) | collective-permute-done | bytes 147488 | tf_op jit(solution)/shard_map/ppermute | solution.py:657
  206.2 4.1 %collective-permute-done.40.refs_2_ = bf16[104,768]{1,0:T(8,128)(2,1)S(1)} collective-permute-done((bf16[104,768]{1,0:T(8,128)(2,1)S(1)}, bf16[104,768]{1,0:T(8,128)(2,1)S(1)}, u32[]{:S(2)}, u32[]{:S(2)}) %collective-permute-start.40) | collective-permute-done | bytes 159776 | tf_op jit(solution)/shard_map/ppermute | solution.py:657
  (163 shorter events, 79.2 us)
Async XLA Ops:
  5.6 14.8 %collective-permute-start.2 = (bf16[104,768]{1,0:T(8,128)(2,1)S(1)}, bf16[104,768]{1,0:T(8,128)(2,1)S(1)}, u32[]{:S(2)}, u32[]{:S(2)}) collective-permute-start(bf16[104,768]{1,0:T(8,128)(2,1)S(1)} %get-tuple-element.66.refs_7_.refs_12_), channel_id=1, source_target_pairs={{0,4},{1,5},{2,6},{3,7},{4,0},{5,1},{6,2},{7,3},{8,12},{9,13},{10,... | collective-permute-start | bytes 479240 | tf_op jit(solution)/shard_map/ppermute | solution.py:657
  23.5 12.5 %collective-permute-start = (bf16[192,768]{1,0:T(8,128)(2,1)S(1)}, bf16[192,768]{1,0:T(8,128)(2,1)S(1)}, u32[]{:S(2)}, u32[]{:S(2)}) collective-permute-start(bf16[192,768]{1,0:T(8,128)(2,1)S(1)} %get-tuple-element.65), channel_id=1, source_target_pairs={{0,2},{1,3},{2,0},{3,1},{4,6},{5,7},{6,4},{7,5},{8,10},{9,11},{10,... | collective-permute-start | bytes 884744 | tf_op jit(solution)/shard_map/ppermute | solution.py:657
  26.0 23.5 %collective-permute-start.8 = (bf16[192,768]{1,0:T(8,128)(2,1)S(1)}, bf16[192,768]{1,0:T(8,128)(2,1)S(1)}, u32[]{:S(2)}, u32[]{:S(2)}) collective-permute-start(bf16[192,768]{1,0:T(8,128)(2,1)S(1)} %get-tuple-element.65), channel_id=1, source_target_pairs={{0,4},{1,5},{2,6},{3,7},{4,0},{5,1},{6,2},{7,3},{8,12},{9,13},{10,... | collective-permute-start | bytes 884744 | tf_op jit(solution)/shard_map/ppermute | solution.py:657
  27.0 22.5 %collective-permute-start.9 = (bf16[192,768]{1,0:T(8,128)(2,1)S(1)}, bf16[192,768]{1,0:T(8,128)(2,1)S(1)}, u32[]{:S(2)}, u32[]{:S(2)}) collective-permute-start(bf16[192,768]{1,0:T(8,128)(2,1)S(1)} %get-tuple-element.65), channel_id=1, source_target_pairs={{0,6},{1,7},{2,4},{3,5},{4,2},{5,3},{6,0},{7,1},{8,14},{9,15},{10,... | collective-permute-start | bytes 884744 | tf_op jit(solution)/shard_map/ppermute | solution.py:657
  50.9 22.1 %collective-permute-start.13 = (bf16[3,192,768]{2,1,0:T(8,128)(2,1)S(1)}, bf16[3,192,768]{2,1,0:T(8,128)(2,1)S(1)}, u32[]{:S(2)}, u32[]{:S(2)}) collective-permute-start(bf16[3,192,768]{2,1,0:T(8,128)(2,1)S(1)} %stack_three.3.refs_1_.refs_2_), channel_id=1, source_target_pairs={{0,8},{8,0},{16,24},{24,16},{1,9},{9,1},{17,25},{25,17},{2,10},{10... | collective-permute-start | bytes 2654216 | tf_op jit(solution)/shard_map/ppermute | solution.py:657
  51.5 21.7 %collective-permute-start.16 = (bf16[3,192,768]{2,1,0:T(8,128)(2,1)S(1)}, bf16[3,192,768]{2,1,0:T(8,128)(2,1)S(1)}, u32[]{:S(2)}, u32[]{:S(2)}) collective-permute-start(bf16[3,192,768]{2,1,0:T(8,128)(2,1)S(1)} %stack_three.3.refs_1_.refs_2_), channel_id=1, source_target_pairs={{0,16},{8,24},{16,0},{24,8},{1,17},{9,25},{17,1},{25,9},{2,18},{10... | collective-permute-start | bytes 2654216 | tf_op jit(solution)/shard_map/ppermute | solution.py:657
  74.6 13.3 %collective-permute-start.17 = (bf16[26,96,768]{2,1,0:T(8,128)(2,1)S(1)}, bf16[26,96,768]{2,1,0:T(8,128)(2,1)S(1)}, u32[]{:S(2)}, u32[]{:S(2)}) collective-permute-start(bf16[26,96,768]{2,1,0:T(8,128)(2,1)S(1)} %bundle.3), channel_id=1, source_target_pairs={{0,1},{1,0},{2,3},{3,2},{4,5},{5,4},{6,7},{7,6},{8,9},{9,8},{10,11... | collective-permute-start | bytes 11501576 | tf_op jit(solution)/shard_map/ppermute | solution.py:657
  74.8 12.6 %collective-permute-start.14 = (bf16[3,96,768]{2,1,0:T(8,128)(2,1)S(1)}, bf16[3,96,768]{2,1,0:T(8,128)(2,1)S(1)}, u32[]{:S(2)}, u32[]{:S(2)}) collective-permute-start(bf16[3,96,768]{2,1,0:T(8,128)(2,1)S(1)} %combine.26), channel_id=1, source_target_pairs={{0,16},{8,24},{16,0},{24,8},{1,17},{9,25},{17,1},{25,9},{2,18},{10... | collective-permute-start | bytes 1327112 | tf_op jit(solution)/shard_map/ppermute | solution.py:657
  126.8 17.4 %collective-permute-start.22 = (bf16[2,4,48,768]{3,2,1,0:T(8,128)(2,1)S(1)}, bf16[2,4,48,768]{3,2,1,0:T(8,128)(2,1)S(1)}, u32[]{:S(2)}, u32[]{:S(2)}) collective-permute-start(bf16[2,4,48,768]{3,2,1,0:T(8,128)(2,1)S(1)} %combine.28.refs_1_), channel_id=1, source_target_pairs={{0,8},{8,0},{16,24},{24,16},{1,9},{9,1},{17,25},{25,17},{2,10},{10... | collective-permute-start | bytes 1769480 | tf_op jit(solution)/shard_map/ppermute | solution.py:657
  128.3 17.5 %collective-permute-start.23 = (bf16[2,4,48,768]{3,2,1,0:T(8,128)(2,1)S(1)}, bf16[2,4,48,768]{3,2,1,0:T(8,128)(2,1)S(1)}, u32[]{:S(2)}, u32[]{:S(2)}) collective-permute-start(bf16[2,4,48,768]{3,2,1,0:T(8,128)(2,1)S(1)} %combine.29.refs_2_), channel_id=1, source_target_pairs={{0,16},{8,24},{16,0},{24,8},{1,17},{9,25},{17,1},{25,9},{2,18},{10... | collective-permute-start | bytes 1769480 | tf_op jit(solution)/shard_map/ppermute | solution.py:657
  136.4 19.2 %collective-permute-start.24 = (bf16[2,4,48,768]{3,2,1,0:T(8,128)(2,1)S(1)}, bf16[2,4,48,768]{3,2,1,0:T(8,128)(2,1)S(1)}, u32[]{:S(2)}, u32[]{:S(2)}) collective-permute-start(bf16[2,4,48,768]{3,2,1,0:T(8,128)(2,1)S(1)} %combine.30.refs_1_), channel_id=1, source_target_pairs={{0,8},{8,0},{16,24},{24,16},{1,9},{9,1},{17,25},{25,17},{2,10},{10... | collective-permute-start | bytes 1769480 | tf_op jit(solution)/shard_map/ppermute | solution.py:657
  137.2 19.9 %collective-permute-start.25 = (bf16[2,4,48,768]{3,2,1,0:T(8,128)(2,1)S(1)}, bf16[2,4,48,768]{3,2,1,0:T(8,128)(2,1)S(1)}, u32[]{:S(2)}, u32[]{:S(2)}) collective-permute-start(bf16[2,4,48,768]{3,2,1,0:T(8,128)(2,1)S(1)} %combine.31.refs_2_), channel_id=1, source_target_pairs={{0,16},{8,24},{16,0},{24,8},{1,17},{9,25},{17,1},{25,9},{2,18},{10... | collective-permute-start | bytes 1769480 | tf_op jit(solution)/shard_map/ppermute | solution.py:657
  144.3 19.1 %collective-permute-start.27 = (bf16[4,48,768]{2,1,0:T(8,128)(2,1)S(1)}, bf16[4,48,768]{2,1,0:T(8,128)(2,1)S(1)}, u32[]{:S(2)}, u32[]{:S(2)}) collective-permute-start(bf16[4,48,768]{2,1,0:T(8,128)(2,1)S(1)} %combine.32.refs_1_), channel_id=1, source_target_pairs={{0,16},{8,24},{16,0},{24,8},{1,17},{9,25},{17,1},{25,9},{2,18},{10... | collective-permute-start | bytes 884744 | tf_op jit(solution)/shard_map/ppermute | solution.py:657
  145.9 17.5 %collective-permute-start.28 = (bf16[4,48,768]{2,1,0:T(8,128)(2,1)S(1)}, bf16[4,48,768]{2,1,0:T(8,128)(2,1)S(1)}, u32[]{:S(2)}, u32[]{:S(2)}) collective-permute-start(bf16[4,48,768]{2,1,0:T(8,128)(2,1)S(1)} %combine.33.refs_2_), channel_id=1, source_target_pairs={{0,8},{8,0},{16,24},{24,16},{1,9},{9,1},{17,25},{25,17},{2,10},{10... | collective-permute-start | bytes 884744 | tf_op jit(solution)/shard_map/ppermute | solution.py:657
  157.3 12.7 %collective-permute-start.31 = (bf16[4,48,768]{2,1,0:T(8,128)(2,1)S(1)}, bf16[4,48,768]{2,1,0:T(8,128)(2,1)S(1)}, u32[]{:S(2)}, u32[]{:S(2)}) collective-permute-start(bf16[4,48,768]{2,1,0:T(8,128)(2,1)S(1)} %combine.34.refs_1_), channel_id=1, source_target_pairs={{0,16},{8,24},{16,0},{24,8},{1,17},{9,25},{17,1},{25,9},{2,18},{10... | collective-permute-start | bytes 884744 | tf_op jit(solution)/shard_map/ppermute | solution.py:657
  168.0 13.3 %collective-permute-start.29 = (bf16[2,4,48,768]{3,2,1,0:T(8,128)(2,1)S(1)}, bf16[2,4,48,768]{3,2,1,0:T(8,128)(2,1)S(1)}, u32[]{:S(2)}, u32[]{:S(2)}) collective-permute-start(bf16[2,4,48,768]{3,2,1,0:T(8,128)(2,1)S(1)} %combine.37.refs_1_), channel_id=1, source_target_pairs={{0,8},{8,0},{16,24},{24,16},{1,9},{9,1},{17,25},{25,17},{2,10},{10... | collective-permute-start | bytes 1769480 | tf_op jit(solution)/shard_map/ppermute | solution.py:657
  168.6 17.4 %collective-permute-start.35 = (bf16[2,4,56,768]{3,2,1,0:T(8,128)(2,1)S(1)}, bf16[2,4,56,768]{3,2,1,0:T(8,128)(2,1)S(1)}, u32[]{:S(2)}, u32[]{:S(2)}) collective-permute-start(bf16[2,4,56,768]{3,2,1,0:T(8,128)(2,1)S(1)} %combine.38.refs_2_), channel_id=1, source_target_pairs={{0,16},{8,24},{16,0},{24,8},{1,17},{9,25},{17,1},{25,9},{2,18},{10... | collective-permute-start | bytes 2064392 | tf_op jit(solution)/shard_map/ppermute | solution.py:657
  170.3 18.1 %collective-permute-start.34 = (bf16[2,96,768]{2,1,0:T(8,128)(2,1)S(1)}, bf16[2,96,768]{2,1,0:T(8,128)(2,1)S(1)}, u32[]{:S(2)}, u32[]{:S(2)}) collective-permute-start(bf16[2,96,768]{2,1,0:T(8,128)(2,1)S(1)} %get-tuple-element.106), channel_id=1, source_target_pairs={{0,2},{1,3},{2,0},{3,1},{4,6},{5,7},{6,4},{7,5},{8,10},{9,11},{10,... | collective-permute-start | bytes 884744 | tf_op jit(solution)/shard_map/ppermute | solution.py:657
  173.4 16.3 %collective-permute-start.37 = (bf16[96,768]{1,0:T(8,128)(2,1)S(1)}, bf16[96,768]{1,0:T(8,128)(2,1)S(1)}, u32[]{:S(2)}, u32[]{:S(2)}) collective-permute-start(bf16[96,768]{1,0:T(8,128)(2,1)S(1)} %combine.40.refs_1_), channel_id=1, source_target_pairs={{0,4},{1,5},{2,6},{3,7},{4,0},{5,1},{6,2},{7,3},{8,12},{9,13},{10,... | collective-permute-start | bytes 442376 | tf_op jit(solution)/shard_map/ppermute | solution.py:657
  181.4 14.5 %collective-permute-start.33 = (bf16[4,48,768]{2,1,0:T(8,128)(2,1)S(1)}, bf16[4,48,768]{2,1,0:T(8,128)(2,1)S(1)}, u32[]{:S(2)}, u32[]{:S(2)}) collective-permute-start(bf16[4,48,768]{2,1,0:T(8,128)(2,1)S(1)} %combine.41.refs_1_), channel_id=1, source_target_pairs={{0,16},{8,24},{16,0},{24,8},{1,17},{9,25},{17,1},{25,9},{2,18},{10... | collective-permute-start | bytes 884744 | tf_op jit(solution)/shard_map/ppermute | solution.py:657
  197.3 12.9 %collective-permute-start.40 = (bf16[104,768]{1,0:T(8,128)(2,1)S(1)}, bf16[104,768]{1,0:T(8,128)(2,1)S(1)}, u32[]{:S(2)}, u32[]{:S(2)}) collective-permute-start(bf16[104,768]{1,0:T(8,128)(2,1)S(1)} %get-tuple-element.109), channel_id=1, source_target_pairs={{0,4},{1,5},{2,6},{3,7},{4,0},{5,1},{6,2},{7,3},{8,12},{9,13},{10,... | collective-permute-start | bytes 479240 | tf_op jit(solution)/shard_map/ppermute | solution.py:657
  200.8 13.9 %collective-permute-start.47 = (bf16[192,768]{1,0:T(8,128)(2,1)S(1)}, bf16[192,768]{1,0:T(8,128)(2,1)S(1)}, u32[]{:S(2)}, u32[]{:S(2)}) collective-permute-start(bf16[192,768]{1,0:T(8,128)(2,1)S(1)} %combine.47.refs_1_), channel_id=1, source_target_pairs={{0,24},{8,16},{16,8},{24,0},{1,25},{9,17},{17,9},{25,1},{2,26},{10... | collective-permute-start | bytes 884744 | tf_op jit(solution)/shard_map/ppermute | solution.py:657
  203.1 13.2 %collective-permute-start.46 = (bf16[192,768]{1,0:T(8,128)(2,1)S(1)}, bf16[192,768]{1,0:T(8,128)(2,1)S(1)}, u32[]{:S(2)}, u32[]{:S(2)}) collective-permute-start(bf16[192,768]{1,0:T(8,128)(2,1)S(1)} %combine.47.refs_1_), channel_id=1, source_target_pairs={{0,16},{8,24},{16,0},{24,8},{1,17},{9,25},{17,1},{25,9},{2,18},{10... | collective-permute-start | bytes 884744 | tf_op jit(solution)/shard_map/ppermute | solution.py:657
  203.6 13.4 %collective-permute-start.45 = (bf16[192,768]{1,0:T(8,128)(2,1)S(1)}, bf16[192,768]{1,0:T(8,128)(2,1)S(1)}, u32[]{:S(2)}, u32[]{:S(2)}) collective-permute-start(bf16[192,768]{1,0:T(8,128)(2,1)S(1)} %combine.47.refs_1_), channel_id=1, source_target_pairs={{0,8},{8,0},{16,24},{24,16},{1,9},{9,1},{17,25},{25,17},{2,10},{10... | collective-permute-start | bytes 884744 | tf_op jit(solution)/shard_map/ppermute | solution.py:657
  (26 other events, 201.2 us)
